TPU v7x, 32 devices: a whole 2x2x4 slice. The times are simulated.
32 devices in a mesh: fsdp: 8 (over z, x), tensor: 4 (over y, core).
Axes of the slice: x: 2, y: 2, z: 4, core: 2. Of those that a mesh axis runs over, the one named last changes fastest.
Arguments:
- inputs: bfloat16 [16384, 1024], P(('fsdp', 'tensor')), may hold values from -6 to 6
- segments: int32 [16384], P('fsdp'), may hold values from 0 to 303, as said below
- cotangent: bfloat16 [16384, 1024], P(('fsdp', 'tensor')), may hold values from -6 to 6
- attention_gain: float32 [1024], P(('fsdp', 'tensor')), may hold values from 0.5 to 1.5
- attention_shift: float32 [1024], P(('fsdp', 'tensor')), may hold values from -1.8 to 1.8
- feedforward_gain: float32 [1024], P(('fsdp', 'tensor')), may hold values from 0.5 to 1.5
- feedforward_shift: float32 [1024], P(('fsdp', 'tensor')), may hold values from -1.8 to 1.8
- project_weight: bfloat16 [1024, 3072], P('fsdp', 'tensor'), may hold values from -0.1875 to 0.1875
- project_bias: bfloat16 [3072], P(('tensor', 'fsdp')), may hold values from -3 to 3
- dense_weight: bfloat16 [1024, 1024], P(('tensor', 'fsdp')), may hold values from -0.75 to 0.75
- dense_bias: float32 [1024], P(('fsdp', 'tensor')), may hold values from -1.8 to 1.8
- expand_weight: bfloat16 [1024, 4096], P('fsdp', 'tensor'), may hold values from -0.1875 to 0.1875
- expand_bias: bfloat16 [4096], P(('tensor', 'fsdp')), may hold values from -3 to 3
- shrink_weight: bfloat16 [4096, 1024], P(('tensor', 'fsdp')), may hold values from -0.09375 to 0.09375
- shrink_bias: float32 [1024], P(('fsdp', 'tensor')), may hold values from -1.8 to 1.8
Outputs:
- output: bfloat16 [16384, 1024], P(('fsdp', 'tensor'))
- inputs_gradient: bfloat16 [16384, 1024], P(('fsdp', 'tensor'))
- attention_gain_gradient: float32 [1024], P(('fsdp', 'tensor'))
- attention_shift_gradient: float32 [1024], P(('fsdp', 'tensor'))
- feedforward_gain_gradient: float32 [1024], P(('fsdp', 'tensor'))
- feedforward_shift_gradient: float32 [1024], P(('fsdp', 'tensor'))
- project_weight_gradient: float32 [1024, 3072], P('fsdp', 'tensor')
- project_bias_gradient: float32 [3072], P(('tensor', 'fsdp'))
- dense_weight_gradient: float32 [1024, 1024], P(('tensor', 'fsdp'))
- dense_bias_gradient: float32 [1024], P(('fsdp', 'tensor'))
- expand_weight_gradient: float32 [1024, 4096], P('fsdp', 'tensor')
- expand_bias_gradient: float32 [4096], P(('tensor', 'fsdp'))
- shrink_weight_gradient: float32 [4096, 1024], P(('tensor', 'fsdp'))
- shrink_bias_gradient: float32 [1024], P(('fsdp', 'tensor'))
Inputs may be any that keep to these rules, and one draw needn't show every extreme that they name: `segments`: within each aligned run of 1024 tokens (one sequence) the nonzero segment numbers never fall and occur in no other run; 0 marks padding, which stands only at the end of a run.
All inputs are finite; a program needn't handle non-finite values.
Results may differ from a plain program's by a relative error of at most 0.012.
Values may be sent and summed in bfloat16 or wider, within the bound.
No kernel may reach another device: no remote copies, remote signals or barrier semaphores. Data moves between devices by JAX's collectives and lax.ppermute only.
A program may use at most 192 MiB of HBM per device.

v0:
```python
from functools import partial
import math

import jax
import jax.numpy as jnp
from jax import lax
from jax.sharding import PartitionSpec as P

HD = 64
ROT = 16
SEQ_LEN = 1024


EPS = 1e-05
NEGATIVE = -1e30


def layer_norm(values, gain, shift):
    centre = values - jnp.mean(values, axis=-1, keepdims=True)
    spread = jnp.mean(centre * centre, axis=-1, keepdims=True)
    return centre * lax.rsqrt(spread + EPS) * gain + shift


def rotary_tables(positions):
    half = ROT // 2
    rates = jnp.exp(
        jnp.arange(half, dtype=jnp.int32).astype(jnp.float32) * (-2.0 * math.log(10000.0) / ROT)
    )
    angles = positions.astype(jnp.float32)[:, None] * rates[None, :]
    cosine = jnp.concatenate([jnp.cos(angles), jnp.cos(angles)], axis=1)[:, None, :]
    sine = jnp.concatenate([jnp.sin(angles), jnp.sin(angles)], axis=1)[:, None, :]
    return (cosine, sine)


def rotate(vectors, cosine, sine):
    half = ROT // 2
    turned = vectors[..., :ROT]
    swapped = jnp.concatenate([-turned[..., half:], turned[..., :half]], axis=-1)
    return jnp.concatenate([turned * cosine + swapped * sine, vectors[..., ROT:]], axis=-1)


def rotate_back(grads, cosine, sine):
    half = ROT // 2
    turned = grads[..., :ROT]
    scaled = turned * sine
    backward = jnp.concatenate([scaled[..., half:], -scaled[..., :half]], axis=-1)
    return jnp.concatenate([turned * cosine + backward, grads[..., ROT:]], axis=-1)


def allowed_mask(query_labels, key_labels, query_start):
    query_index = query_start + jnp.arange(query_labels.shape[0], dtype=jnp.int32)
    key_index = jnp.arange(key_labels.shape[0], dtype=jnp.int32)
    causal = key_index[None, :] <= query_index[:, None]
    same = query_labels[:, None] == key_labels[None, :]
    alone = (query_labels[:, None] != 0) | (key_index[None, :] == query_index[:, None])
    return causal & same & alone


def block_scores(query_block, keys, labels, start):
    scale = 1.0 / math.sqrt(HD)
    scores = (
        jnp.einsum("qhd,khd->hqk", query_block, keys, preferred_element_type=jnp.float32) * scale
    )
    mask = allowed_mask(labels[start : start + query_block.shape[0]], labels, start)
    return jnp.where(mask[None], scores, NEGATIVE)


def attend_sequence(items):
    query, keys, values, labels = items
    length = keys.shape[0]
    rows_block = min(512, length)
    outputs = []
    totals = []
    for block in range(length // rows_block):
        start = block * rows_block
        scores = block_scores(query[start : start + rows_block], keys, labels, start)
        top = jnp.max(scores, axis=-1, keepdims=True)
        probs = jnp.exp(scores - top)
        total = jnp.sum(probs, axis=-1, keepdims=True)
        probs = probs / total
        mixed = jnp.einsum(
            "hqk,khd->qhd", probs.astype(jnp.bfloat16), values, preferred_element_type=jnp.float32
        )
        outputs.append(mixed.astype(jnp.bfloat16))
        totals.append((top + jnp.log(total))[..., 0])
    return (jnp.concatenate(outputs, axis=0), jnp.concatenate(totals, axis=1))


def attend_back(items):
    query, keys, values, labels, totals, grads = items
    scale = 1.0 / math.sqrt(HD)
    length = keys.shape[0]
    rows_block = min(512, length)
    key_grad = jnp.zeros(keys.shape, jnp.float32)
    value_grad = jnp.zeros(values.shape, jnp.float32)
    query_grads = []
    for block in range(length // rows_block):
        start = block * rows_block
        query_block = query[start : start + rows_block]
        grad_block = grads[start : start + rows_block]
        scores = block_scores(query_block, keys, labels, start)
        probs = jnp.exp(scores - totals[:, start : start + rows_block, None])
        probs_grad = jnp.einsum(
            "qhd,khd->hqk", grad_block, values, preferred_element_type=jnp.float32
        )
        inner = jnp.sum(probs * probs_grad, axis=-1, keepdims=True)
        scores_grad = (probs * (probs_grad - inner)).astype(jnp.bfloat16)
        query_grads.append(
            jnp.einsum("hqk,khd->qhd", scores_grad, keys, preferred_element_type=jnp.float32)
            * scale
        )
        key_grad = (
            key_grad
            + jnp.einsum(
                "hqk,qhd->khd", scores_grad, query_block, preferred_element_type=jnp.float32
            )
            * scale
        )
        value_grad = value_grad + jnp.einsum(
            "hqk,qhd->khd",
            probs.astype(jnp.bfloat16),
            grad_block,
            preferred_element_type=jnp.float32,
        )
    return (jnp.concatenate(query_grads, axis=0), key_grad, value_grad)


def contract_rows(left, right):
    return lax.dot_general(
        left, right, (((0,), (0,)), ((), ())), preferred_element_type=jnp.float32
    )


def contract_columns(left, right):
    return lax.dot_general(
        left, right, (((1,), (1,)), ((), ())), preferred_element_type=jnp.float32
    )


def local(
    inputs,
    segments,
    cotangent,
    attention_gain,
    attention_shift,
    feedforward_gain,
    feedforward_shift,
    project_weight,
    project_bias,
    dense_weight,
    dense_bias,
    expand_weight,
    expand_bias,
    shrink_weight,
    shrink_bias,
):
    rank = lax.axis_index("tensor")
    rows = inputs.shape[0]
    group = segments.shape[0]
    count = group // SEQ_LEN
    vectors = (
        lax.all_gather(attention_gain, ("fsdp", "tensor"), axis=0, tiled=True),
        lax.all_gather(attention_shift, ("fsdp", "tensor"), axis=0, tiled=True),
        lax.all_gather(feedforward_gain, ("fsdp", "tensor"), axis=0, tiled=True),
        lax.all_gather(feedforward_shift, ("fsdp", "tensor"), axis=0, tiled=True),
        lax.all_gather(dense_bias, ("fsdp", "tensor"), axis=0, tiled=True),
        lax.all_gather(shrink_bias, ("fsdp", "tensor"), axis=0, tiled=True),
    )
    gain_one, shift_one, gain_two, shift_two, dense_full, shrink_full = vectors
    gathered = (
        lax.all_gather(project_weight, "fsdp", axis=0, tiled=True),
        lax.all_gather(expand_weight, "fsdp", axis=0, tiled=True),
        lax.all_gather(dense_weight, "fsdp", axis=0, tiled=True),
        lax.all_gather(shrink_weight, "fsdp", axis=0, tiled=True),
        lax.all_gather(project_bias, "fsdp", axis=0, tiled=True),
        lax.all_gather(expand_bias, "fsdp", axis=0, tiled=True),
    )
    project_local, expand_local, dense_local, shrink_local, project_offset, expand_offset = gathered
    features = inputs.astype(jnp.float32)
    local_one = layer_norm(features, gain_one, shift_one).astype(jnp.bfloat16)
    local_two = layer_norm(features, gain_two, shift_two).astype(jnp.bfloat16)
    normed_one, normed_two = (
        lax.all_gather(local_one, "tensor", axis=0, tiled=True),
        lax.all_gather(local_two, "tensor", axis=0, tiled=True),
    )
    positions = jnp.arange(group, dtype=jnp.int32) % SEQ_LEN
    cosine, sine = rotary_tables(positions)
    heads = project_local.shape[1] // (3 * HD)
    projected = jnp.dot(
        normed_one, project_local, preferred_element_type=jnp.float32
    ) + project_offset.astype(jnp.float32)
    projected = projected.reshape(group, heads, 3, HD)
    query = rotate(projected[:, :, 0], cosine, sine).astype(jnp.bfloat16)
    keys = rotate(projected[:, :, 1], cosine, sine).astype(jnp.bfloat16)
    values = projected[:, :, 2].astype(jnp.bfloat16)

    def shaped(array):
        return array.reshape((count, SEQ_LEN) + array.shape[1:])

    labels = segments.reshape(count, SEQ_LEN)
    mixed, totals = lax.map(attend_sequence, (shaped(query), shaped(keys), shaped(values), labels))
    mixed = mixed.reshape(group, heads * HD)
    hidden = jnp.dot(
        normed_two, expand_local, preferred_element_type=jnp.float32
    ) + expand_offset.astype(jnp.float32)
    active = jax.nn.gelu(hidden, approximate=False).astype(jnp.bfloat16)
    mixed_rows = lax.slice_in_dim(mixed, 0, rows * lax.axis_size("tensor"), axis=0)
    branch = lax.psum_scatter(
        (
            jnp.dot(mixed_rows, dense_local, preferred_element_type=jnp.float32)
            + jnp.dot(active, shrink_local, preferred_element_type=jnp.float32)
        ).astype(jnp.bfloat16),
        "tensor",
        scatter_dimension=0,
        tiled=True,
    ).astype(jnp.float32)
    output = (features + branch + dense_full + shrink_full).astype(jnp.bfloat16)
    own_labels = lax.dynamic_slice_in_dim(segments, rank * rows, rows, 0)
    upstream = cotangent.astype(jnp.float32) * (own_labels != 0).astype(jnp.float32)[:, None]
    branch_grad = lax.all_gather(upstream.astype(jnp.bfloat16), "tensor", axis=0, tiled=True)
    bias_grad = jnp.sum(upstream, axis=0)
    shrink_grad = contract_rows(active, branch_grad)
    active_grad = contract_columns(branch_grad, shrink_local)
    gelu_value, gelu_pull = jax.vjp(partial(jax.nn.gelu, approximate=False), hidden)
    hidden_grad = gelu_pull(active_grad)[0].astype(jnp.bfloat16)
    expand_grad = contract_rows(normed_two, hidden_grad)
    expand_offset_grad = jnp.sum(hidden_grad.astype(jnp.float32), axis=0)
    normed_two_grad = contract_columns(hidden_grad, expand_local)
    dense_grad = contract_rows(mixed, branch_grad)
    mixed_grad = (
        contract_columns(branch_grad, dense_local).astype(jnp.bfloat16).reshape(group, heads, HD)
    )
    query_grad, key_grad, value_grad = lax.map(
        attend_back,
        (shaped(query), shaped(keys), shaped(values), labels, totals, shaped(mixed_grad)),
    )
    query_grad = rotate_back(query_grad.reshape(group, heads, HD), cosine, sine)
    key_grad = rotate_back(key_grad.reshape(group, heads, HD), cosine, sine)
    projected_grad = jnp.stack([query_grad, key_grad, value_grad.reshape(group, heads, HD)], axis=2)
    projected_grad = projected_grad.reshape(group, 3 * heads * HD).astype(jnp.bfloat16)
    project_grad = contract_rows(normed_one, projected_grad)
    project_offset_grad = jnp.sum(projected_grad.astype(jnp.float32), axis=0)
    normed_one_grad = contract_columns(projected_grad, project_local)
    weight_sums = (
        lax.psum_scatter(project_grad, "fsdp", scatter_dimension=0, tiled=True),
        lax.psum_scatter(expand_grad, "fsdp", scatter_dimension=0, tiled=True),
        lax.psum_scatter(dense_grad, "fsdp", scatter_dimension=0, tiled=True),
        lax.psum_scatter(shrink_grad, "fsdp", scatter_dimension=0, tiled=True),
        lax.psum_scatter(project_offset_grad, "fsdp", scatter_dimension=0, tiled=True),
        lax.psum_scatter(expand_offset_grad, "fsdp", scatter_dimension=0, tiled=True),
    )
    project_sum, expand_sum, dense_sum, shrink_sum, project_offset_sum, expand_offset_sum = (
        weight_sums
    )
    one_rows, two_rows = (
        lax.psum_scatter(
            normed_one_grad.astype(jnp.bfloat16), "tensor", scatter_dimension=0, tiled=True
        ).astype(jnp.float32),
        lax.psum_scatter(
            normed_two_grad.astype(jnp.bfloat16), "tensor", scatter_dimension=0, tiled=True
        ).astype(jnp.float32),
    )
    norm_value, first_pull = jax.vjp(layer_norm, features, gain_one, shift_one)
    first_inputs, first_gain, first_shift = first_pull(one_rows)
    norm_other, second_pull = jax.vjp(layer_norm, features, gain_two, shift_two)
    second_inputs, second_gain, second_shift = second_pull(two_rows)
    inputs_gradient = (upstream + first_inputs + second_inputs).astype(jnp.bfloat16)
    vector_sums = (
        lax.psum_scatter(first_gain, ("fsdp", "tensor"), scatter_dimension=0, tiled=True),
        lax.psum_scatter(first_shift, ("fsdp", "tensor"), scatter_dimension=0, tiled=True),
        lax.psum_scatter(second_gain, ("fsdp", "tensor"), scatter_dimension=0, tiled=True),
        lax.psum_scatter(second_shift, ("fsdp", "tensor"), scatter_dimension=0, tiled=True),
        lax.psum_scatter(bias_grad, ("fsdp", "tensor"), scatter_dimension=0, tiled=True),
    )
    gain_one_sum, shift_one_sum, gain_two_sum, shift_two_sum, bias_sum = vector_sums
    return (
        output,
        inputs_gradient,
        gain_one_sum,
        shift_one_sum,
        gain_two_sum,
        shift_two_sum,
        project_sum,
        project_offset_sum,
        dense_sum,
        bias_sum,
        expand_sum,
        expand_offset_sum,
        shrink_sum,
        bias_sum,
    )


def solution(mesh):
    in_specs = (
        P(("fsdp", "tensor"), None),
        P("fsdp"),
        P(("fsdp", "tensor"), None),
        P(("fsdp", "tensor")),
        P(("fsdp", "tensor")),
        P(("fsdp", "tensor")),
        P(("fsdp", "tensor")),
        P("fsdp", "tensor"),
        P(("tensor", "fsdp")),
        P(("tensor", "fsdp"), None),
        P(("fsdp", "tensor")),
        P("fsdp", "tensor"),
        P(("tensor", "fsdp")),
        P(("tensor", "fsdp"), None),
        P(("fsdp", "tensor")),
    )
    out_specs = (
        P(("fsdp", "tensor"), None),
        P(("fsdp", "tensor"), None),
        P(("fsdp", "tensor")),
        P(("fsdp", "tensor")),
        P(("fsdp", "tensor")),
        P(("fsdp", "tensor")),
        P("fsdp", "tensor"),
        P(("tensor", "fsdp")),
        P(("tensor", "fsdp"), None),
        P(("fsdp", "tensor")),
        P("fsdp", "tensor"),
        P(("tensor", "fsdp")),
        P(("tensor", "fsdp"), None),
        P(("fsdp", "tensor")),
    )
    return jax.shard_map(local, mesh=mesh, in_specs=in_specs, out_specs=out_specs, check_vma=False)
```

profile of v0, /device:TPU:0, one launch (start us, length us, event | category | flops | bytes accessed | tf_op | source)
XLA Modules:
  0.0 900.5 jit_solution(8306996030455223238)
XLA Ops:
  11.4 42.7 %all-reduce.15 = (f32[1024]{0:T(1024)S(1)}, f32[1024]{0:T(1024)S(1)}, f32[1024]{0:T(1024)S(1)}, f32[1024]{0:T(1024)S(1)}) all-reduce(f32[1024]{0:T(1024)S(1)} %dynamic-update-slice.4, f32[1024]{0:T(1024)S(1)} %dynamic-update-slice.3, f32[1024]{0:T(1024)S(1)} %dynamic-update-slice.1, ...), channel_id=1, replica_groups=mesh['fsdp'=8,'tensor'=4] {'fsdp','tensor'}, use_global_device_ids=true, to_apply=%add.4 | all-reduce | flops 4096 | bytes 32768
  66.4 21.0 %all-reduce.2 = bf16[768]{0:T(1024)(128)(2,1)S(1)} all-reduce(bf16[768]{0:T(1024)(128)(2,1)S(1)} %dynamic-update-slice.2), channel_id=1, replica_groups=mesh['fsdp'=8,'tensor'=4] {'fsdp'}, use_global_device_ids=true, to_apply=%add.2 | all-reduce | flops 768 | bytes 3072
  87.3 33.6 %all_gather.50 = bf16[256,1024]{1,0:T(8,128)(2,1)} all-gather(bf16[32,1024]{1,0:T(8,128)(2,1)S(1)} %copy-done.28), channel_id=1, replica_groups=mesh['fsdp'=8,'tensor'=4] {'fsdp'}, dimensions={0}, use_global_device_ids=true | all-gather | bytes 589824 | tf_op jit(solution)/shard_map/all_gather | solution.py:173
  142.6 37.2 %while.26 = (s32[]{:T(128)}, bf16[2,1024,4,64]{1,3,2,0:T(8,128)(2,1)}, f32[2,4,1024]{2,1,0:T(4,128)S(1)}, bf16[2,1024,4,64]{1,3,2,0:T(8,128)(2,1)}, s32[2,1024]{...) while((s32[]{:T(128)}, ...), condition=%wide.region_7.8_spmd, body=%wide.region_2.7_spmd.sunk | while | flops 1131677184 | bytes 58922628 | solution.py:201
  192.9 193.4 %while.27 = (s32[]{:T(128)}, f32[2,1024,4,64]{1,0,3,2:T(2,128)}, f32[2,1024,4,64]{1,0,3,2:T(2,128)}, bf16[2,1024,4,64]{1,0,3,2:T(2,128)(2,1)}, bf16[2,1024,4,64]...) while((s32[]{:T(128)}, f32[2,1024,4,64]{1,0,3,2:T(2,128)}, ...), condition=%wide.region_12.13_spmd, body=%wide.region_9.12_spmd.sunk | while | flops 2755130880 | bytes 284876160 | solution.py:233
  215.8 18.7 %dynamic_update_slice.28 = f32[2,1024,4,64]{1,0,3,2:T(2,128)} dynamic-update-slice(f32[2,1024,4,64]{1,0,3,2:T(2,128)} %get-tuple-element.462, f32[1,1024,4,64]{1,0,3,2:T(1,128)S(1)} %copy.97, s32[]{:T(128)} %get-tuple-element.460, s32[]{:T(128)} %constant.44.clone.1..sunk.1, s32[]{:T(128)} %constant.44.clone.1..sunk.1, s32[]{:T(128)} %constant.44.clone.1..sunk.1) | dynamic-update-slice | bytes 2097156 | tf_op jit(solution)/shard_map/while/body/jit(dynamic_update_index_in_dim)/dynamic_update_slice | solution.py:233
  240.8 18.7 %dynamic_update_slice.27 = f32[2,1024,4,64]{1,0,3,2:T(2,128)} dynamic-update-slice(f32[2,1024,4,64]{1,0,3,2:T(2,128)} %get-tuple-element.461, f32[1,1024,4,64]{1,0,3,2:T(1,128)S(1)} %copy.96, s32[]{:T(128)} %get-tuple-element.460, s32[]{:T(128)} %constant.44.clone.1..sunk.1, s32[]{:T(128)} %constant.44.clone.1..sunk.1, s32[]{:T(128)} %constant.44.clone.1..sunk.1) | dynamic-update-slice | bytes 2097156 | tf_op jit(solution)/shard_map/while/body/jit(dynamic_update_index_in_dim)/dynamic_update_slice | solution.py:233
  272.1 17.4 %dynamic_update_slice.29 = bf16[2,1024,4,64]{1,0,3,2:T(2,128)(2,1)} dynamic-update-slice(bf16[2,1024,4,64]{1,0,3,2:T(2,128)(2,1)} %get-tuple-element.463, bf16[1,1024,4,64]{1,0,3,2:T(2,128)(2,1)S(1)} %copy.98, s32[]{:T(128)} %get-tuple-element.460, s32[]{:T(128)} %constant.44.clone.1..sunk.1, s32[]{:T(128)} %constant.44.clone.1..sunk.1, s32[]{:T(128)} %constant.44.clone.1..sunk.1) | dynamic-update-slice | bytes 1048580 | tf_op jit(solution)/shard_map/while/body/jit(dynamic_update_index_in_dim)/dynamic_update_slice | solution.py:233
  312.3 18.7 %dynamic_update_slice.28 = f32[2,1024,4,64]{1,0,3,2:T(2,128)} dynamic-update-slice(f32[2,1024,4,64]{1,0,3,2:T(2,128)} %get-tuple-element.462, f32[1,1024,4,64]{1,0,3,2:T(1,128)S(1)} %copy.97, s32[]{:T(128)} %get-tuple-element.460, s32[]{:T(128)} %constant.44.clone.1..sunk.1, s32[]{:T(128)} %constant.44.clone.1..sunk.1, s32[]{:T(128)} %constant.44.clone.1..sunk.1) | dynamic-update-slice | bytes 2097156 | tf_op jit(solution)/shard_map/while/body/jit(dynamic_update_index_in_dim)/dynamic_update_slice | solution.py:233
  337.3 18.7 %dynamic_update_slice.27 = f32[2,1024,4,64]{1,0,3,2:T(2,128)} dynamic-update-slice(f32[2,1024,4,64]{1,0,3,2:T(2,128)} %get-tuple-element.461, f32[1,1024,4,64]{1,0,3,2:T(1,128)S(1)} %copy.96, s32[]{:T(128)} %get-tuple-element.460, s32[]{:T(128)} %constant.44.clone.1..sunk.1, s32[]{:T(128)} %constant.44.clone.1..sunk.1, s32[]{:T(128)} %constant.44.clone.1..sunk.1) | dynamic-update-slice | bytes 2097156 | tf_op jit(solution)/shard_map/while/body/jit(dynamic_update_index_in_dim)/dynamic_update_slice | solution.py:233
  368.4 17.4 %dynamic_update_slice.29 = bf16[2,1024,4,64]{1,0,3,2:T(2,128)(2,1)} dynamic-update-slice(bf16[2,1024,4,64]{1,0,3,2:T(2,128)(2,1)} %get-tuple-element.463, bf16[1,1024,4,64]{1,0,3,2:T(2,128)(2,1)S(1)} %copy.98, s32[]{:T(128)} %get-tuple-element.460, s32[]{:T(128)} %constant.44.clone.1..sunk.1, s32[]{:T(128)} %constant.44.clone.1..sunk.1, s32[]{:T(128)} %constant.44.clone.1..sunk.1) | dynamic-update-slice | bytes 1048580 | tf_op jit(solution)/shard_map/while/body/jit(dynamic_update_index_in_dim)/dynamic_update_slice | solution.py:233
  410.6 16.1 %all-gather = bf16[8,1,128]{2,1,0:T(2,128)(2,1)S(1)} all-gather(bf16[1,1,128]{2,1,0:T(2,128)(2,1)S(1)} %bitcast.260), channel_id=1, replica_groups=mesh['fsdp'=8,'tensor'=4] {'fsdp'}, dimensions={0}, use_global_device_ids=true | all-gather | bytes 2304 | tf_op jit(solution)/shard_map/all_gather | solution.py:176
  426.8 10.7 %fusion.139 = f32[2048,1024]{1,0:T(8,128)} fusion(bf16[2048,1024]{1,0:T(8,128)(2,1)} %all-gather.12.cloned.1.call-done, bf16[1024,1024]{1,0:T(8,128)(2,1)} %all-gather.14.cloned.1.call-done), kind=kOutput, calls=%fused_computation.245 | convolution fusion | flops 4294967296 | bytes 14680064 | tf_op jit(solution)/shard_map/dot_general | solution.py:203
  437.5 28.0 %convert_reduce_fusion = (f32[1024]{0:T(1024)S(1)}, bf16[2048,1024]{1,0:T(8,128)(2,1)S(1)}, f32[2048,1024]{1,0:T(8,128)}) fusion(f32[2048,1024]{1,0:T(8,128)} %fusion.139, f32[1024]{0:T(1024)S(1)} %bitcast.258, bf16[2048,1024]{1,0:T(8,128)(2,1)} %all-gather.18.cloned.1.call-done, bf16[1024,1024]{1,0:T(8,128)(2,1)} %all-gather.16.cloned.1.call-done), kind=kOutput, calls=%fused_computation.132 | convolution fusion | flops 4452252672 | bytes 27271168 | tf_op jit(solution)/shard_map/dot_general | solution.py:135
  476.7 12.3 %multiply_convert_fusion.2 = bf16[2048,1024]{1,0:T(8,128)(2,1)} fusion(f32[2048,1024]{1,0:T(8,128)} %get-tuple-element.214, f32[2048,1024]{1,0:T(8,128)} %fusion.139, f32[1024]{0:T(1024)S(1)} %bitcast.259), kind=kLoop, calls=%fused_computation.135 | loop fusion | flops 8388608 | bytes 20975616 | tf_op jit(solution)/shard_map/convert_element_type | solution.py:206
  503.3 8.4 fusion.141
  512.0 10.0 %fusion.144 = f32[1024,1024]{1,0:T(8,128)} fusion(bf16[2048,1024]{1,0:T(8,128)(2,1)} %multiply_convert_fusion.2, bf16[2048,1024]{1,0:T(8,128)(2,1)} %all-gather.18.cloned.1.call-done), kind=kOutput, calls=%fused_computation.250 | convolution fusion | flops 4294967296 | bytes 12582912 | tf_op jit(solution)/shard_map/dot_general | solution.py:129
  522.1 10.5 %fusion.143 = f32[1024,1024]{1,0:T(8,128)} fusion(bf16[2048,1024]{1,0:T(8,128)(2,1)} %all-gather.12.cloned.1.call-done, bf16[2048,1024]{1,0:T(8,128)(2,1)} %copy-done.46), kind=kOutput, calls=%fused_computation.249 | convolution fusion | flops 4294967296 | bytes 12582912 | tf_op jit(solution)/shard_map/dot_general | solution.py:129
  534.8 20.0 %all-reduce.16 = (f32[768]{0:T(1024)S(1)}, f32[1024]{0:T(1024)S(1)}) all-reduce(f32[768]{0:T(1024)S(1)} %reduce_sum.174, f32[1024]{0:T(1024)S(1)} %get-tuple-element.212), channel_id=10, replica_groups=mesh['fsdp'=8,'tensor'=4] {'fsdp'}, use_global_device_ids=true, to_apply=%region_29.30.clone | all-reduce | flops 1792 | bytes 14336
  564.6 37.5 %all-reduce.14 = (f32[1024]{0:T(1024)S(1)}, f32[1024]{0:T(1024)S(1)}, f32[1024]{0:T(1024)S(1)}, f32[1024]{0:T(1024)S(1)}, f32[1024]{0:T(1024)S(1)}, /*index=5*/f32[1024]{0:T(1024)S(1)}, f32[1024]{0:T(1024)S(1)}) all-reduce(f32[1024]{0:T(1024)S(1)} %dynamic-update-slice.6, ...), channel_id=1, replica_groups=mesh['fsdp'=8,'tensor'=4] {'fsdp','tensor'}, use_global_device_ids=true, to_apply=%add.6 | all-reduce | flops 7168 | bytes 57344
  607.2 24.7 %reduce-scatter.16.cloned.1.call-done = f32[32,1024]{1,0:T(8,128)} async-done(((f32[256,1024]{1,0:T(8,128)}), f32[32,1024]{1,0:T(8,128)}) %reduce-scatter.16.cloned.1.call-update) | async-done | bytes 131088 | tf_op jit(solution)/shard_map/reduce_scatter | solution.py:247
  631.9 77.4 %reduce-scatter.14.cloned.1.call-done = f32[128,768]{1,0:T(8,128)} async-done(((f32[1024,768]{1,0:T(8,128)}), f32[128,768]{1,0:T(8,128)}) %reduce-scatter.14.cloned.1.call-update) | async-done | bytes 393232 | tf_op jit(solution)/shard_map/reduce_scatter | solution.py:245
  709.3 91.2 %reduce-scatter.20.cloned.1.call-done = f32[128,1024]{1,0:T(8,128)} async-done(((f32[1024,1024]{1,0:T(8,128)}), f32[128,1024]{1,0:T(8,128)}) %reduce-scatter.20.cloned.1.call-update) | async-done | bytes 524304 | tf_op jit(solution)/shard_map/reduce_scatter | solution.py:248
  800.5 92.5 %reduce-scatter.18.cloned.1.call-done = f32[128,1024]{1,0:T(8,128)} async-done(((f32[1024,1024]{1,0:T(8,128)}), f32[128,1024]{1,0:T(8,128)}) %reduce-scatter.18.cloned.1.call-update) | async-done | bytes 524304 | tf_op jit(solution)/shard_map/reduce_scatter | solution.py:246
  (315 shorter events, 235.7 us)
Async XLA Ops:
  7.2 53.9 %copy-start.36 = (s32[2048]{0:T(1024)S(1)}, s32[2048]{0:T(1024)}, u32[]{:S(2)}) copy-start(s32[2048]{0:T(1024)} %param.20) | copy-start | bytes 24580
  7.2 54.6 %copy-start.11 = (bf16[512,1024]{1,0:T(8,128)(2,1)S(1)}, bf16[512,1024]{1,0:T(8,128)(2,1)}, u32[]{:S(2)}) copy-start(bf16[512,1024]{1,0:T(8,128)(2,1)} %param.21) | copy-start | bytes 3145732
  7.2 114.1 %all-gather.10.cloned.1.call-start = ((), (), s32[]{:S(2)}) async-start(), calls=%async_computation.8 | async-start | bytes 1769472 | tf_op jit(solution)/shard_map/all_gather | solution.py:171
  7.9 113.4 %all-gather.8.cloned.1.call-start = ((), (), s32[]{:S(2)}) async-start(), calls=%async_computation.7 | async-start | bytes 5242880 | tf_op jit(solution)/shard_map/all_gather | solution.py:183
  57.8 29.6 %copy-start.28 = (bf16[32,1024]{1,0:T(8,128)(2,1)S(1)}, bf16[32,1024]{1,0:T(8,128)(2,1)}, u32[]{:S(2)}) copy-start(bf16[32,1024]{1,0:T(8,128)(2,1)} %param.28) | copy-start | bytes 196612
  61.0 118.8 %all-gather.18.cloned.1.call-start = ((), (), s32[]{:S(2)}) async-start(), calls=%async_computation.13 | async-start | bytes 5242880 | tf_op jit(solution)/shard_map/all_gather | solution.py:220
  63.0 363.8 %all-gather.14.cloned.1.call-start = ((), (), s32[]{:S(2)}) async-start(), calls=%async_computation.10 | async-start | bytes 2359296 | tf_op jit(solution)/shard_map/all_gather | solution.py:172
  63.6 363.2 %all-gather.12.cloned.1.call-start = ((), (), s32[]{:S(2)}) async-start(), calls=%async_computation.9 | async-start | bytes 5242880 | tf_op jit(solution)/shard_map/all_gather | solution.py:184
  64.2 373.3 %all-gather.16.cloned.1.call-start = ((), (), s32[]{:S(2)}) async-start(), calls=%async_computation.11 | async-start | bytes 2359296 | tf_op jit(solution)/shard_map/all_gather | solution.py:174
  64.7 491.2 %reduce-scatter.10.cloned.1.call-start = ((), (), s32[]{:S(2)}) async-start(), calls=%async_computation.14 | async-start | bytes 5242880 | tf_op jit(solution)/shard_map/reduce_scatter | solution.py:256
  142.6 37.2 %copy-start.16 = (bf16[256,1024]{1,0:T(8,128)(2,1)S(1)}, bf16[256,1024]{1,0:T(8,128)(2,1)}, u32[]{:S(2)}) copy-start(bf16[256,1024]{1,0:T(8,128)(2,1)} %all_gather.50) | copy-start | bytes 1572868
  265.3 24.2 %copy-start.6 = (bf16[2,1024,4,64]{1,3,2,0:T(8,128)(2,1)S(1)}, bf16[2,1024,4,64]{1,3,2,0:T(8,128)(2,1)}, u32[]{:S(2)}) copy-start(bf16[2,1024,4,64]{1,3,2,0:T(8,128)(2,1)} %copy-done.5) | copy-start | bytes 3145732 | tf_op jit(solution)/shard_map/while
  410.0 145.9 %reduce-scatter.12.cloned.1.call-start = ((), (), s32[]{:S(2)}) async-start(), calls=%async_computation.15 | async-start | bytes 5242880 | tf_op jit(solution)/shard_map/reduce_scatter | solution.py:259
  437.5 30.0 %copy-start.40 = (bf16[1024,1024]{1,0:T(8,128)(2,1)S(1)}, bf16[1024,1024]{1,0:T(8,128)(2,1)}, u32[]{:S(2)}) copy-start(bf16[1024,1024]{1,0:T(8,128)(2,1)} %all-gather.14.cloned.1.call-done) | copy-start | bytes 6291460
  473.8 130.7 %reduce-scatter.8.cloned.1.call-start = ((), (), s32[]{:S(2)}) async-start(), calls=%async_computation.12 | async-start | bytes 5242880 | tf_op jit(solution)/shard_map/reduce_scatter | solution.py:208
  498.7 133.2 %reduce-scatter.16.cloned.1.call-start = ((), (), s32[]{:S(2)}) async-start(), calls=%async_computation.17 | async-start | bytes 1179648 | tf_op jit(solution)/shard_map/reduce_scatter | solution.py:247
  503.3 206.1 %reduce-scatter.14.cloned.1.call-start = ((), (), s32[]{:S(2)}) async-start(), calls=%async_computation.16 | async-start | bytes 3538944 | tf_op jit(solution)/shard_map/reduce_scatter | solution.py:245
  511.7 288.8 %reduce-scatter.20.cloned.1.call-start = ((), (), s32[]{:S(2)}) async-start(), calls=%async_computation.19 | async-start | bytes 4718592 | tf_op jit(solution)/shard_map/reduce_scatter | solution.py:248
  522.1 370.9 %reduce-scatter.18.cloned.1.call-start = ((), (), s32[]{:S(2)}) async-start(), calls=%async_computation.18 | async-start | bytes 4718592 | tf_op jit(solution)/shard_map/reduce_scatter | solution.py:246
  532.7 25.9 %copy-start.35 = (f32[512]{0:T(512)S(1)}, f32[512]{0:T(512)}, u32[]{:S(2)}) copy-start(f32[512]{0:T(512)} %copy-done.34) | copy-start | bytes 6148
  532.7 25.9 %copy-start.30 = (f32[512]{0:T(512)S(1)}, f32[512]{0:T(512)}, u32[]{:S(2)}) copy-start(f32[512]{0:T(512)} %copy-done.29) | copy-start | bytes 6148
  532.7 29.3 %copy-start.12 = (bf16[512,1024]{1,0:T(8,128)(2,1)S(1)}, bf16[512,1024]{1,0:T(8,128)(2,1)}, u32[]{:S(2)}) copy-start(bf16[512,1024]{1,0:T(8,128)(2,1)} %param.21) | copy-start | bytes 3145732
  532.7 29.3 %copy-start.33 = (f32[512]{0:T(512)S(1)}, f32[512]{0:T(512)}, u32[]{:S(2)}) copy-start(f32[512]{0:T(512)} %copy-done.32) | copy-start | bytes 6148
  602.2 291.3 %copy-start.45 = (f32[32]{0:T(128)}, f32[32]{0:T(128)S(1)}, u32[]{:S(2)}) copy-start(f32[32]{0:T(128)S(1)} %dynamic-slice.7) | copy-start | bytes 388
  (44 other events, 313.4 us)
Sparse Core Ops, SparseCore 0:
  10.2 47.2 all-gather.9
  61.1 34.3 all-gather.7
  97.0 34.4 all-gather.17
  133.6 49.2 all-gather.13
  184.9 32.9 all-gather.11
  219.9 49.2 all-gather.15
  410.1 41.0 reduce-scatter.9
  474.0 43.1 reduce-scatter.11
  519.7 44.4 reduce-scatter.7
  568.4 63.4 reduce-scatter.15
  636.1 73.1 reduce-scatter.13
  713.4 87.0 reduce-scatter.19
  805.1 87.8 reduce-scatter.17
where the time goes:
time: 914 us; the launch traced here: 901 us
  waiting for transfers between devices  288 us (32%)
  matrix products  186 us (20%)
  blocking collectives  171 us (19%)
  local copies, waits for them, and re-layouts  168 us (18%)
  other arithmetic  68.2 us (7%)
  between operations  17.2 us (2%)
    unnamed x4, blocking collectives  121 us
    dynamic_update_slice x12, local copies, waits for them, and re-layouts, local(): lax.map(attend_back, (shaped(query), shaped(keys), shaped(values), labels...  115 us
    reduce_scatter x1, waiting for transfers between devices, local(): lax.psum_scatter(expand_grad, 'fsdp', scatter_dimension=0, tiled=True)  92.5 us
    reduce_scatter x1, waiting for transfers between devices, local(): lax.psum_scatter(shrink_grad, 'fsdp', scatter_dimension=0, tiled=True)  91.2 us
    reduce_scatter x1, waiting for transfers between devices, local(): lax.psum_scatter(project_grad, 'fsdp', scatter_dimension=0, tiled=True)  77.4 us
    dot_general x4, matrix products, contract_columns(): lax.dot_general(left, right, (((1,), (1,)), ((), ())), preferred_element_...  44.1 us
    all_gather x1, blocking collectives, local(): lax.all_gather(dense_weight, 'fsdp', axis=0, tiled=True)  33.6 us
    dot_general x4, matrix products, contract_rows(): lax.dot_general(left, right, (((0,), (0,)), ((), ())), preferred_element_...  33.4 us
  transfers between devices with their start and end apart: 13, of which 4 were waited for; matrix products, arithmetic and copies ran while one was open for 46% of the time, Pallas kernels for 0%

commit v1 on v0

v1 whole, which is shorter than its diff:
```python
import math

import jax
import jax.numpy as jnp
from jax import lax
from jax.experimental import pallas as pl
from jax.experimental.pallas import tpu as pltpu
from jax.sharding import PartitionSpec as P

HD = 64
ROT = 16
SEQ_LEN = 1024
EPS = 1e-05
NEGATIVE = -1e30
QB = 256
VMEM_BYTES = 60 * 1024 * 1024
def nt(a,b): return lax.dot_general(a,b,(((1,),(1,)),((),())),preferred_element_type=jnp.float32)
def nn(a,b): return lax.dot_general(a,b,(((1,),(0,)),((),())),preferred_element_type=jnp.float32)

def attention_kernel(x_ref,c_ref,w_ref,b_ref,d_ref,lrow_ref,lcol_ref,cos_ref,up_ref,dn_ref,
                     mixed_ref,pg_ref, q_s,k_s,v_s,g_s,kt_s,vt_s,gt_s,pt_s,dst_s,ot_s,dqt_s,dk_s,dv_s):
    S=x_ref.shape[0]; width=d_ref.shape[0]; pairs=width//128; nb=S//QB
    scale=1.0/math.sqrt(HD)
    cos=cos_ref[...]; up=up_ref[...]; dn=dn_ref[...]
    def rot(u):
        return u*cos + pltpu.roll(u,8,axis=1)*up + pltpu.roll(u,120,axis=1)*dn
    def rot_back(w):
        return w*cos + pltpu.roll(w*up,120,axis=1) + pltpu.roll(w*dn,8,axis=1)
    xv=x_ref[...]
    gv=nt(c_ref[...],d_ref[...])
    for p in range(pairs):
        lo=p*128
        g=gv[:,lo:lo+128]
        g_s[:,lo:lo+128]=g.astype(jnp.bfloat16)
        q=nn(xv,w_ref[:,lo:lo+128])+b_ref[:,lo:lo+128]
        q_s[:,lo:lo+128]=(rot(q).astype(jnp.bfloat16).astype(jnp.float32)*scale).astype(jnp.bfloat16)
        k=nn(xv,w_ref[:,width+lo:width+lo+128])+b_ref[:,width+lo:width+lo+128]
        k_s[:,lo:lo+128]=rot(k).astype(jnp.bfloat16)
        v=nn(xv,w_ref[:,2*width+lo:2*width+lo+128])+b_ref[:,2*width+lo:2*width+lo+128]
        v_s[:,lo:lo+128]=v.astype(jnp.bfloat16)
    lane=lax.broadcasted_iota(jnp.int32,(1,128),1)
    krow=lax.broadcasted_iota(jnp.int32,(QB,QB),0); qcol=lax.broadcasted_iota(jnp.int32,(QB,QB),1)
    tri=krow<=qcol
    for p in range(pairs):
        lo=p*128
        sl=slice(lo,lo+128)
        kt_s[...]=k_s[:,sl].T
        vt_s[...]=v_s[:,sl].T
        gt_s[...]=g_s[:,sl].astype(jnp.float32).T
        for a in range(2):
            half=(lane>=64*a)&(lane<64*a+64)
            hs=slice(64*a,64*a+64)
            for i in range(nb):
                L=(i+1)*QB
                rows=slice(i*QB,L)
                zero=jnp.zeros((),jnp.bfloat16)
                qm=jnp.where(half,q_s[rows,sl],zero)
                gm=jnp.where(half,g_s[rows,sl],zero)
                s=nt(k_s[0:L,sl],qm)
                same=lcol_ref[0:L,:]==lrow_ref[:,rows]
                pieces=[]
                if i: pieces.append(jnp.where(same[:L-QB],s[:L-QB],NEGATIVE))
                pieces.append(jnp.where(same[L-QB:]&tri,s[L-QB:],NEGATIVE))
                s=jnp.concatenate(pieces,axis=0) if i else pieces[0]
                m=jnp.max(s,axis=0,keepdims=True)
                e=jnp.exp(s-m)
                l=jnp.sum(e,axis=0,keepdims=True)
                pr=e*(1.0/l)
                pb=pr.astype(jnp.bfloat16)
                pt_s[0:L,rows]=pb
                ot=nn(vt_s[hs,0:L],pb)
                ot_s[hs,rows]=ot
                dp=nt(v_s[0:L,sl],gm)
                D=jnp.sum(gt_s[hs,rows]*ot,axis=0,keepdims=True)
                ds=(pr*(dp-D)).astype(jnp.bfloat16)
                dst_s[0:L,rows]=ds
                dqt_s[hs,rows]=nn(kt_s[hs,0:L],ds)*scale
            for j in range(nb):
                rows=slice(j*QB,S); out=slice(j*QB,(j+1)*QB)
                qm=jnp.where(half,q_s[rows,sl],zero)
                gm=jnp.where(half,g_s[rows,sl],zero)
                dk=nn(dst_s[out,rows],qm); dv=nn(pt_s[out,rows],gm)
                if a==0:
                    dk_s[out,:]=dk; dv_s[out,:]=dv
                else:
                    dk_s[out,:]+=dk; dv_s[out,:]+=dv
        mixed_ref[:,sl]=ot_s[...].T.astype(jnp.bfloat16)
        pg_ref[:,lo:lo+128]=rot_back(dqt_s[...].T).astype(jnp.bfloat16)
        pg_ref[:,width+lo:width+lo+128]=rot_back(dk_s[...]).astype(jnp.bfloat16)
        pg_ref[:,2*width+lo:2*width+lo+128]=dv_s[...].astype(jnp.bfloat16)

def rotary_rows():
    half=ROT//2
    pos=jnp.arange(SEQ_LEN,dtype=jnp.int32).astype(jnp.float32)
    rates=jnp.exp(jnp.arange(half,dtype=jnp.int32).astype(jnp.float32)*(-2.0*math.log(10000.0)/ROT))
    ang=pos[:,None]*rates[None,:]
    c,s=jnp.cos(ang),jnp.sin(ang)
    one=jnp.ones((SEQ_LEN,HD-ROT),jnp.float32); z8=jnp.zeros((SEQ_LEN,half),jnp.float32); zr=jnp.zeros((SEQ_LEN,HD-ROT),jnp.float32)
    cos=jnp.concatenate([c,c,one]*2,axis=1)
    up=jnp.concatenate([z8,s,zr]*2,axis=1)
    dn=jnp.concatenate([-s,z8,zr]*2,axis=1)
    return cos,up,dn

def attention(xhat,ct,w,b,dense,labels):
    n,S=labels.shape; width=dense.shape[0]; D=xhat.shape[1]
    idx=jnp.arange(S,dtype=jnp.int32)[None,:]
    marks=jnp.where(labels!=0,labels,-1-idx)
    lrow=marks[:,None,:]; lcol=marks[:,:,None]
    cos,up,dn=rotary_rows()
    full=lambda shape: pl.BlockSpec(shape,lambda s:tuple(0 for _ in shape))
    bf=jnp.bfloat16; f32=jnp.float32
    return pl.pallas_call(
        attention_kernel,
        grid=(n,),
        in_specs=[pl.BlockSpec((S,D),lambda s:(s,0)),pl.BlockSpec((S,D),lambda s:(s,0)),
                  full(w.shape),full(b.shape),full(dense.shape),
                  pl.BlockSpec((None,1,S),lambda s:(s,0,0)),pl.BlockSpec((None,S,1),lambda s:(s,0,0)),
                  full(cos.shape),full(cos.shape),full(cos.shape)],
        out_specs=[pl.BlockSpec((S,width),lambda s:(s,0)),pl.BlockSpec((S,3*width),lambda s:(s,0))],
        out_shape=[jax.ShapeDtypeStruct((n*S,width),bf),jax.ShapeDtypeStruct((n*S,3*width),bf)],
        scratch_shapes=[pltpu.VMEM((S,width),bf)]*4+[pltpu.VMEM((128,S),bf)]*2+[pltpu.VMEM((128,S),f32)]
            +[pltpu.VMEM((S,S),bf)]*2+[pltpu.VMEM((128,S),f32)]*2+[pltpu.VMEM((S,128),f32)]*2,
        compiler_params=pltpu.CompilerParams(vmem_limit_bytes=VMEM_BYTES),
        name="attention",
    )(xhat,ct,w,b,dense,lrow,lcol,cos,up,dn)


def exchange(value, axis, size, offset):
    return lax.ppermute(value, axis, [(i, i ^ offset) for i in range(size)])


def sum_over(value, axis, size):
    offset = 1
    while offset < size:
        value = value + exchange(value, axis, size, offset)
        offset *= 2
    return value


def slots(value, index, size):
    row = lax.broadcasted_iota(jnp.int32, (size, 1), 0)
    return jnp.where(row == index, value[None, :], 0.0)


def gather_blocks(block, size):
    far = [block] + [exchange(block, "fsdp", size, 2 * m) for m in range(1, size // 2)]
    blocks = []
    for piece in far:
        blocks += [piece, exchange(piece, "fsdp", size, 1)]
    return blocks


def join_kernel(place_ref, *refs):
    out_ref = refs[-1]
    for k in range(len(refs) - 1):
        rows = refs[k].shape[0]
        start = pl.multiple_of(lax.bitwise_xor(place_ref[0], k) * rows, rows)
        out_ref[pl.ds(start, rows), :] = refs[k][...]


def join_scaled_kernel(place_ref, *refs):
    gain_ref, shift_ref, out_ref, bias_ref = refs[-4:]
    total = None
    for k in range(len(refs) - 4):
        rows = refs[k].shape[0]
        start = pl.multiple_of(lax.bitwise_xor(place_ref[0], k) * rows, rows)
        weight = refs[k][...].astype(jnp.float32)
        part = jnp.sum(weight * shift_ref[pl.ds(start, rows), :], axis=0, keepdims=True)
        total = part if total is None else total + part
        out_ref[pl.ds(start, rows), :] = (weight * gain_ref[pl.ds(start, rows), :]).astype(
            jnp.bfloat16
        )
    bias_ref[...] = total


def join(place, blocks):
    rows, columns = blocks[0].shape
    whole = pl.BlockSpec(memory_space=pltpu.VMEM)
    return pl.pallas_call(
        join_kernel,
        in_specs=[pl.BlockSpec(memory_space=pltpu.SMEM)] + [whole] * len(blocks),
        out_specs=whole,
        out_shape=jax.ShapeDtypeStruct((rows * len(blocks), columns), jnp.bfloat16),
        compiler_params=pltpu.CompilerParams(vmem_limit_bytes=VMEM_BYTES),
        name="join",
    )(place, *blocks)


def join_scaled(place, blocks, gain, shift):
    rows, columns = blocks[0].shape
    whole = pl.BlockSpec(memory_space=pltpu.VMEM)
    return pl.pallas_call(
        join_scaled_kernel,
        in_specs=[pl.BlockSpec(memory_space=pltpu.SMEM)] + [whole] * (len(blocks) + 2),
        out_specs=[whole, whole],
        out_shape=[
            jax.ShapeDtypeStruct((rows * len(blocks), columns), jnp.bfloat16),
            jax.ShapeDtypeStruct((1, columns), jnp.float32),
        ],
        compiler_params=pltpu.CompilerParams(vmem_limit_bytes=VMEM_BYTES),
        name="join_scaled",
    )(place, *blocks, gain[:, None], shift[:, None])


def grads_kernel(place_ref, left_ref, right_ref, near_ref, own_ref):
    product = lax.dot_general(
        left_ref[...],
        right_ref[...],
        (((0,), (0,)), ((), ())),
        preferred_element_type=jnp.float32,
    )
    rows = product.shape[0] // 2
    low, high = product[:rows], product[rows:]
    swap = (place_ref[0] & 1) == 1
    own_ref[...] = jnp.where(swap, high, low).astype(jnp.bfloat16)
    near_ref[...] = jnp.where(swap, low, high).astype(jnp.bfloat16)


def paired_grads(place, left, right, size):
    tokens, rows = left.shape
    columns = right.shape[1]
    pairs = size // 2
    block = rows // size
    return pl.pallas_call(
        grads_kernel,
        grid_spec=pltpu.PrefetchScalarGridSpec(
            num_scalar_prefetch=1,
            grid=(pairs,),
            in_specs=[
                pl.BlockSpec(
                    (tokens, 2 * block),
                    lambda m, place: (
                        0,
                        lax.bitwise_xor(lax.shift_right_logical(place[0], 1), m),
                    ),
                ),
                pl.BlockSpec((tokens, columns), lambda m, place: (0, 0)),
            ],
            out_specs=[pl.BlockSpec((None, block, columns), lambda m, place: (m, 0, 0))] * 2,
        ),
        out_shape=[jax.ShapeDtypeStruct((pairs, block, columns), jnp.bfloat16)] * 2,
        compiler_params=pltpu.CompilerParams(vmem_limit_bytes=VMEM_BYTES),
        name="grads",
    )(place, left, right)


def contract_rows(left, right):
    return lax.dot_general(
        left, right, (((0,), (0,)), ((), ())), preferred_element_type=jnp.float32
    )


def scatter_pairs(near, own, size):
    arrived = exchange(near, "fsdp", size, 1)
    total = own[0].astype(jnp.float32) + arrived[0].astype(jnp.float32)
    for m in range(1, size // 2):
        part = (own[m].astype(jnp.float32) + arrived[m].astype(jnp.float32)).astype(jnp.bfloat16)
        total = total + exchange(part, "fsdp", size, 2 * m).astype(jnp.float32)
    return total


def scattered_grads(place, left, right, size):
    rows = left.shape[1]
    block = rows // size
    if size == 8 and block % 128 == 0:
        near, own = paired_grads(place, left, right, size)
        return scatter_pairs(near, own, size)
    product = contract_rows(left, right)
    if size != 8:
        return lax.psum_scatter(product, "fsdp", scatter_dimension=0, tiled=True)
    parts = product.astype(jnp.bfloat16).reshape(size, block, right.shape[1])
    index = place[0]

    def take(k):
        return lax.dynamic_index_in_dim(parts, lax.bitwise_xor(index, k), 0, keepdims=False)

    near = jnp.stack([take(2 * m + 1) for m in range(size // 2)])
    own = [take(2 * m) for m in range(size // 2)]
    return scatter_pairs(near, own, size)


def gather_rows(place, block, size):
    if size == 8:
        return join(place, gather_blocks(block, size))
    return lax.all_gather(block, "fsdp", axis=0, tiled=True)


def gather_scaled(place, block, gain, shift, size):
    if size == 8:
        return join_scaled(place, gather_blocks(block, size), gain, shift)
    weight = lax.all_gather(block, "fsdp", axis=0, tiled=True).astype(jnp.float32)
    return (weight * gain[:, None]).astype(jnp.bfloat16), jnp.sum(
        weight * shift[:, None], axis=0, keepdims=True
    )


def sequence_rows(value, core):
    other = exchange(value, "tensor", 4, 2)
    pieces = []
    for part in (value, other):
        partner = exchange(part, "tensor", 4, 1)
        pieces.append(jnp.where(core == 0, part, partner))
        pieces.append(jnp.where(core == 0, partner, part))
    return jnp.concatenate(pieces, axis=0)


def owner_rows(value, core, rows):
    def half(start, which):
        return lax.dynamic_slice_in_dim(value, start + which * rows, rows, 0)

    far = exchange(half(2 * rows, 1 - core), "tensor", 4, 1)
    near = exchange(half(0, 1 - core), "tensor", 4, 1)
    far = (half(2 * rows, core).astype(jnp.float32) + far.astype(jnp.float32)).astype(jnp.bfloat16)
    far = exchange(far, "tensor", 4, 2)
    return (
        half(0, core).astype(jnp.float32) + near.astype(jnp.float32) + far.astype(jnp.float32)
    )


def normalise(features):
    centre = features - jnp.mean(features, axis=-1, keepdims=True)
    rate = lax.rsqrt(jnp.mean(centre * centre, axis=-1, keepdims=True) + EPS)
    return centre * rate, rate


def by_part(array):
    shape = array.shape
    array = array.reshape(shape[:-1] + (shape[-1] // (3 * HD), 3, HD))
    return jnp.swapaxes(array, -3, -2).reshape(shape)


def by_head(array):
    shape = array.shape
    array = array.reshape(shape[:-1] + (3, shape[-1] // (3 * HD), HD))
    return jnp.swapaxes(array, -3, -2).reshape(shape)


def local(
    inputs,
    segments,
    cotangent,
    attention_gain,
    attention_shift,
    feedforward_gain,
    feedforward_shift,
    project_weight,
    project_bias,
    dense_weight,
    dense_bias,
    expand_weight,
    expand_bias,
    shrink_weight,
    shrink_bias,
):
    f32, bf16 = jnp.float32, jnp.bfloat16
    size = lax.axis_size("fsdp")
    across = lax.axis_size("tensor")
    rows, width = inputs.shape
    assert across == 4 and 2 * rows == SEQ_LEN and segments.shape[0] == 2 * SEQ_LEN
    index = lax.axis_index("fsdp")
    rank = lax.axis_index("tensor")
    core = rank % 2
    chip = rank // 2
    place = index.astype(jnp.int32)[None]
    block = width // size

    features = inputs.astype(f32)
    normed_own, rate = normalise(features)
    own_labels = lax.dynamic_slice_in_dim(segments, rank * rows, rows, 0)
    upstream = cotangent.astype(f32) * (own_labels != 0).astype(f32)[:, None]

    small = jnp.concatenate(
        [
            attention_gain,
            attention_shift,
            feedforward_gain,
            feedforward_shift,
            dense_bias + shrink_bias,
        ]
    )
    piece = small.shape[0] // 5
    small = sum_over(slots(small, rank, across), "tensor", across)
    own_vectors = jnp.swapaxes(small.reshape(across, 5, piece), 0, 1).reshape(5, block)
    counts = (5 * block, project_bias.shape[0], expand_bias.shape[0])
    packed = jnp.concatenate(
        [own_vectors.reshape(-1), project_bias.astype(f32), expand_bias.astype(f32)]
    )
    packed = sum_over(slots(packed, index, size), "fsdp", size)
    vectors = jnp.swapaxes(packed[:, : counts[0]].reshape(size, 5, block), 0, 1).reshape(5, width)
    project_offset = by_part(packed[:, counts[0] : counts[0] + counts[1]].reshape(-1))
    expand_offset = packed[:, counts[0] + counts[1] :].reshape(-1)
    gain_one, shift_one, gain_two, shift_two, out_bias = vectors

    normed = sequence_rows(normed_own.astype(bf16), core)
    expand_local, expand_extra = gather_scaled(place, expand_weight, gain_two, shift_two, size)
    branch_grad = sequence_rows(upstream.astype(bf16), core)
    shrink_local = gather_rows(place, shrink_weight, size)
    project_local, project_extra = gather_scaled(
        place, by_part(project_weight), gain_one, shift_one, size
    )
    dense_local = gather_rows(place, dense_weight, size)

    hidden = jnp.dot(normed, expand_local, preferred_element_type=f32) + (
        expand_offset[None, :] + expand_extra
    )
    phi = 0.5 * (1.0 + lax.erf(hidden * (1.0 / math.sqrt(2.0))))
    active = (hidden * phi).astype(bf16)
    slope = phi + hidden * (jnp.exp(-0.5 * hidden * hidden) * (1.0 / math.sqrt(2.0 * math.pi)))
    shrink_sum = scattered_grads(place, active, branch_grad, size)
    hidden_grad = (nt(branch_grad, shrink_local) * slope).astype(bf16)
    expand_sum = scattered_grads(place, normed, hidden_grad, size)
    expand_offset_grad = jnp.sum(hidden_grad.astype(f32), axis=0)
    bias_grad = jnp.sum(branch_grad.astype(f32), axis=0)

    labels = segments.reshape(2, SEQ_LEN)
    labels = jnp.where(chip == 0, labels, labels[::-1])
    mixed, projected_grad = attention(
        normed,
        branch_grad,
        project_local,
        project_offset[None, :] + project_extra,
        dense_local,
        labels,
    )
    dense_sum = scattered_grads(place, mixed, branch_grad, size)
    project_sum = scattered_grads(place, normed, projected_grad, size)
    project_offset_grad = jnp.sum(projected_grad.astype(f32), axis=0)

    branch = (nn(mixed, dense_local) + nn(active, shrink_local)).astype(bf16)
    branch = owner_rows(branch, core, rows)
    output = (features + branch + out_bias[None, :]).astype(bf16)

    normed_grad = (nt(projected_grad, project_local) + nt(hidden_grad, expand_local)).astype(bf16)
    normed_grad = owner_rows(normed_grad, core, rows)
    inner = jnp.mean(normed_grad * normed_own, axis=-1, keepdims=True)
    centre = jnp.mean(normed_grad, axis=-1, keepdims=True)
    inputs_gradient = (upstream + rate * (normed_grad - centre - normed_own * inner)).astype(bf16)

    totals = sum_over(
        jnp.concatenate([project_offset_grad, expand_offset_grad, bias_grad])[None, :],
        "fsdp",
        size,
    )[0]
    wide = project_offset_grad.shape[0]
    hidden_units = expand_offset_grad.shape[0]
    project_totals = totals[:wide]
    expand_totals = totals[wide : wide + hidden_units]
    bias_totals = totals[wide + hidden_units :]

    def mine(vector, count, start):
        return lax.dynamic_slice_in_dim(vector, start * count, count, 0)

    own_project = by_part(project_weight).astype(f32)
    own_expand = expand_weight.astype(f32)
    partial = jnp.stack(
        [
            jnp.sum(own_project * project_sum, axis=1),
            jnp.sum(own_project * project_totals[None, :], axis=1),
            jnp.sum(own_expand * expand_sum, axis=1),
            jnp.sum(own_expand * expand_totals[None, :], axis=1),
        ]
    )
    partial = sum_over(partial, "tensor", across)
    partial = lax.dynamic_slice_in_dim(partial, rank * piece, piece, 1)
    project_gradient = own_vectors[0][:, None] * project_sum + (
        own_vectors[1][:, None] * project_totals[None, :]
    )
    expand_gradient = own_vectors[2][:, None] * expand_sum + (
        own_vectors[3][:, None] * expand_totals[None, :]
    )
    bias_sum = mine(bias_totals, piece, index * across + rank)
    return (
        output,
        inputs_gradient,
        partial[0],
        partial[1],
        partial[2],
        partial[3],
        by_head(project_gradient),
        mine(by_head(project_totals), project_bias.shape[0], index),
        dense_sum,
        bias_sum,
        expand_gradient,
        mine(expand_totals, expand_bias.shape[0], index),
        shrink_sum,
        bias_sum,
    )


def solution(mesh):
    in_specs = (
        P(("fsdp", "tensor"), None),
        P("fsdp"),
        P(("fsdp", "tensor"), None),
        P(("fsdp", "tensor")),
        P(("fsdp", "tensor")),
        P(("fsdp", "tensor")),
        P(("fsdp", "tensor")),
        P("fsdp", "tensor"),
        P(("tensor", "fsdp")),
        P(("tensor", "fsdp"), None),
        P(("fsdp", "tensor")),
        P("fsdp", "tensor"),
        P(("tensor", "fsdp")),
        P(("tensor", "fsdp"), None),
        P(("fsdp", "tensor")),
    )
    out_specs = (
        P(("fsdp", "tensor"), None),
        P(("fsdp", "tensor"), None),
        P(("fsdp", "tensor")),
        P(("fsdp", "tensor")),
        P(("fsdp", "tensor")),
        P(("fsdp", "tensor")),
        P("fsdp", "tensor"),
        P(("tensor", "fsdp")),
        P(("tensor", "fsdp"), None),
        P(("fsdp", "tensor")),
        P("fsdp", "tensor"),
        P(("tensor", "fsdp")),
        P(("tensor", "fsdp"), None),
        P(("fsdp", "tensor")),
    )
    return jax.shard_map(local, mesh=mesh, in_specs=in_specs, out_specs=out_specs, check_vma=False)
```

time: 914 us -> 450 us (0.49)
  blocking collectives: 171 us -> 0 us
  matrix products: 186 us -> 48.7 us
  local copies, waits for them, and re-layouts: 168 us -> 31.3 us
  waiting for transfers between devices: 288 us -> 162 us
  Pallas kernels: 0 us -> 83.8 us
  starting transfers between devices: 0.99 us -> 64.6 us
  other arithmetic: 68.2 us -> 52.7 us
  between operations: 17.2 us -> 1.91 us
    reduce_scatter x7 -> x0, waiting for transfers between devices: 286 us -> none  [the longest x1 92.5 us: local(): lax.psum_scatter(expand_grad, 'fsdp', scatter_dimension=0, tiled=True)]
    ppermute x0 -> x66, waiting for transfers between devices: none -> 162 us  [exchange(): return lax.ppermute(value, axis, [(i, i ^ offset) for i in range(size)])]
    unnamed x4 -> x0, blocking collectives: 121 us -> none
    dynamic_update_slice x12 -> x0, local copies, waits for them, and re-layouts: 115 us -> none  [local(): lax.map(attend_back, (shaped(query), shaped(keys), shaped(values), labels...]
    dot_general x36 -> x6, matrix products: 152 us -> 47.4 us  [the longest x3 20.4 us: nt(): lax.dot_general(a, b, (((1,), (1,)), ((), ())), preferred_element_type=jn...]
    pallas_call x0 -> x8, Pallas kernels: none -> 83.8 us  [the longest x1 46.4 us: attention(): pl.pallas_call(attention_kernel, grid=(n,), in_specs=[pl.BlockSpec((S, D)...]
    ppermute x0 -> x66, starting transfers between devices: none -> 64.6 us  [exchange(): return lax.ppermute(value, axis, [(i, i ^ offset) for i in range(size)])]
    all_gather x2 -> x0, blocking collectives: 49.7 us -> none  [the longest x1 33.6 us: local(): lax.all_gather(dense_weight, 'fsdp', axis=0, tiled=True)]
  transfers between devices with their start and end apart: 13 -> 66, of which waited for: 4 -> 28; matrix products, arithmetic and copies ran while one was open for 46% -> 17% of each run, Pallas kernels for 0% -> 3%
where the time goes in v1:
time: 450 us; the launch traced here: 445 us
  waiting for transfers between devices  162 us (36%)
  Pallas kernels  83.8 us (19%)
  starting transfers between devices  64.6 us (14%)
  other arithmetic  52.7 us (12%)
  matrix products  48.7 us (11%)
  local copies, waits for them, and re-layouts  31.3 us (7%)
    ppermute x66, waiting for transfers between devices, exchange(): return lax.ppermute(value, axis, [(i, i ^ offset) for i in range(size)])  162 us
    ppermute x66, starting transfers between devices, exchange(): return lax.ppermute(value, axis, [(i, i ^ offset) for i in range(size)])  64.6 us
    pallas_call x1, Pallas kernels, attention(): pl.pallas_call(attention_kernel, grid=(n,), in_specs=[pl.BlockSpec((S, D)...  46.4 us
    pallas_call x3, Pallas kernels, paired_grads(): pl.pallas_call(grads_kernel, grid_spec=pltpu.PrefetchScalarGridSpec(num_s...  24.9 us
    dot_general x3, matrix products, nt(): lax.dot_general(a, b, (((1,), (1,)), ((), ())), preferred_element_type=jn...  20.4 us
    dot_general x2, matrix products, nn(): lax.dot_general(a, b, (((1,), (0,)), ((), ())), preferred_element_type=jn...  15.6 us
    dot_general x1, matrix products, local(): jnp.dot(normed, expand_local, preferred_element_type=f32)  11.3 us
  transfers between devices with their start and end apart: 66, of which 28 were waited for; matrix products, arithmetic and copies ran while one was open for 17% of the time, Pallas kernels for 3%

profile of v1, /device:TPU:0, one launch (start us, length us, event | category | flops | bytes accessed | tf_op | source)
XLA Modules:
  0.0 444.8 jit_solution(12808104482891050019)
XLA Ops:
  30.6 7.6 %collective-permute-done.17 = f32[8,864]{1,0:T(8,128)S(1)} collective-permute-done((f32[8,864]{1,0:T(8,128)S(1)}, f32[8,864]{1,0:T(8,128)S(1)}, u32[]{:S(2)}, u32[]{:S(2)}) %collective-permute-start.17) | collective-permute-done | bytes 27680 | tf_op jit(solution)/shard_map/ppermute | solution.py:129
  46.8 15.0 %collective-permute-done.9.refs_4_ = bf16[128,768]{1,0:T(8,128)(2,1)} collective-permute-done((bf16[128,768]{1,0:T(8,128)(2,1)S(1)}, bf16[128,768]{1,0:T(8,128)(2,1)}, u32[]{:S(2)}, u32[]{:S(2)}) %collective-permute-start.9) | collective-permute-done | bytes 196640 | tf_op jit(solution)/shard_map/ppermute | solution.py:129
  61.9 3.8 collective-permute-start.30
  75.3 9.7 %collective-permute-done.28.refs_4_ = bf16[128,1024]{1,0:T(8,128)(2,1)S(1)} collective-permute-done((bf16[128,1024]{1,0:T(8,128)(2,1)}, bf16[128,1024]{1,0:T(8,128)(2,1)S(1)}, u32[]{:S(2)}, u32[]{:S(2)}) %collective-permute-start.28) | collective-permute-done | bytes 262176 | tf_op jit(solution)/shard_map/ppermute | solution.py:129
  104.5 4.0 collective-permute-done.34.refs_3_
  108.6 3.9 collective-permute-done.31.refs_7_
  141.5 4.0 join_scaled.3
  162.9 46.4 %attention.1 = (bf16[2048,256]{1,0:T(8,128)(2,1)}, bf16[2048,768]{1,0:T(8,128)(2,1)}) custom-call(bf16[2048,1024]{1,0:T(8,128)(2,1)} %pad_maximum_fusion.x_ref.left_ref, bf16[2048,1024]{1,0:T(8,128)(2,1)} %get-tuple-element.89.c_ref.right_ref, bf16[1024,768]{1,0:T(8,128)(2,1)} %get-tuple-element.26.w_ref, f32[1,768]{1,0:T(1,128)} %add.309.b_ref, ...), custom_call_target="tpu_custom_call" | custom-call | tf_op jit(solution)/shard_map/attention/pallas_call | solution.py:112
  211.7 7.6 %grads.3 = (bf16[4,128,768]{2,1,0:T(8,128)(2,1)}, bf16[4,128,768]{2,1,0:T(8,128)(2,1)}) custom-call(s32[1]{0:T(128)} %bitcast.place_ref, bf16[2048,1024]{1,0:T(8,128)(2,1)} %pad_maximum_fusion.x_ref.left_ref, bf16[2048,768]{1,0:T(8,128)(2,1)} %get-tuple-element.31.right_ref), custom_call_target="tpu_custom_call" | custom-call | tf_op jit(solution)/shard_map/grads/pallas_call | solution.py:224
  219.3 11.3 %multiply_convert_fusion = (bf16[2048,1024]{1,0:T(8,128)(2,1)}, f32[2048,1024]{1,0:T(8,128)}) fusion(f32[1024]{0:T(1024)S(1)} %bitcast.145, bf16[1024,1024]{1,0:T(8,128)(2,1)} %get-tuple-element.29, bf16[512,1024]{1,0:T(8,128)(2,1)} %copy-done.12, bf16[512,1024]{1,0:T(8,128)(2,1)} %copy-done.11, bf16[512,1024]{1,0:T(8,128)(2,1)} %copy-done.10, ...), kind=kOutput, calls=%fused_computation.11 | convolution fusion | flops 4324327424 | bytes 18878464 | tf_op jit(solution)/shard_map/dot_general | solution.py:403
  230.6 8.7 %grads.5 = (bf16[4,128,1024]{2,1,0:T(8,128)(2,1)}, bf16[4,128,1024]{2,1,0:T(8,128)(2,1)}) custom-call(s32[1]{0:T(128)} %bitcast.place_ref, bf16[2048,1024]{1,0:T(8,128)(2,1)} %get-tuple-element.141.left_ref, bf16[2048,1024]{1,0:T(8,128)(2,1)} %get-tuple-element.89.c_ref.right_ref), custom_call_target="tpu_custom_call" | custom-call | tf_op jit(solution)/shard_map/grads/pallas_call | solution.py:224
  239.3 10.9 %fusion.52 = f32[2048,1024]{1,0:T(8,128)} fusion(bf16[2048,1024]{1,0:T(8,128)(2,1)} %get-tuple-element.141.left_ref, bf16[1024,1024]{1,0:T(8,128)(2,1)} %join.3), kind=kOutput, calls=%fused_computation.142 | convolution fusion | flops 4294967296 | bytes 14680064 | tf_op jit(solution)/shard_map/dot_general | solution.py:18
  250.2 9.1 %convert_reduce_fusion.1 = (f32[1024]{0:T(1024)S(1)}, bf16[2048,1024]{1,0:T(8,128)(2,1)}) fusion(f32[2048,1024]{1,0:T(8,128)S(1)} %copy-done.64, f32[1024]{0:T(1024)S(1)} %bitcast.146, bf16[2048,1024]{1,0:T(8,128)(2,1)S(1)} %copy-done, bf16[1024,1024]{1,0:T(8,128)(2,1)S(1)} %copy-done.13), kind=kOutput, calls=%fused_computation.8 | convolution fusion | flops 4322229248 | bytes 18882560 | tf_op jit(solution)/shard_map/dot_general | solution.py:17
  259.3 8.7 %grads.4 = (bf16[4,128,1024]{2,1,0:T(8,128)(2,1)}, bf16[4,128,1024]{2,1,0:T(8,128)(2,1)}) custom-call(s32[1]{0:T(128)} %bitcast.place_ref, bf16[2048,1024]{1,0:T(8,128)(2,1)} %pad_maximum_fusion.x_ref.left_ref, bf16[2048,1024]{1,0:T(8,128)(2,1)} %get-tuple-element.140.right_ref), custom_call_target="tpu_custom_call" | custom-call | tf_op jit(solution)/shard_map/grads/pallas_call | solution.py:224
  268.0 7.4 %fusion.53 = f32[2048,1024]{1,0:T(8,128)S(1)} fusion(bf16[2048,1024]{1,0:T(8,128)(2,1)} %get-tuple-element.140.right_ref, bf16[1024,1024]{1,0:T(8,128)(2,1)} %get-tuple-element.29), kind=kOutput, calls=%fused_computation.143 | convolution fusion | flops 4294967296 | bytes 14680064 | tf_op jit(solution)/shard_map/dot_general | solution.py:17
  281.7 4.8 %add_convert_fusion.1 = bf16[2048,1024]{1,0:T(8,128)(2,1)S(1)} fusion(f32[2048,1024]{1,0:T(8,128)} %fusion.52, bf16[2048,256]{1,0:T(8,128)(2,1)S(1)} %copy-done.19, bf16[256,1024]{1,0:T(8,128)(2,1)S(1)} %copy-done.9), kind=kOutput, calls=%fused_computation.10 | convolution fusion | flops 1077936128 | bytes 14155776 | tf_op jit(solution)/shard_map/dot_general | solution.py:18
  289.9 14.1 %collective-permute-done.49 = f32[1,2816]{1,0:T(1,128)S(1)} collective-permute-done((f32[1,2816]{1,0:T(1,128)S(1)}, f32[1,2816]{1,0:T(1,128)S(1)}, u32[]{:S(2)}, u32[]{:S(2)}) %collective-permute-start.49) | collective-permute-done | bytes 11296 | tf_op jit(solution)/shard_map/ppermute | solution.py:129
  304.8 3.9 add_convert_fusion
  326.3 9.0 %collective-permute-done.60 = bf16[32,1024]{1,0:T(8,128)(2,1)S(1)} collective-permute-done((bf16[32,1024]{1,0:T(8,128)(2,1)}, bf16[32,1024]{1,0:T(8,128)(2,1)S(1)}, u32[]{:S(2)}, u32[]{:S(2)}) %collective-permute-start.60) | collective-permute-done | bytes 65568 | tf_op jit(solution)/shard_map/ppermute | solution.py:129
  338.7 4.1 collective-permute-done.48
  342.8 4.1 collective-permute-done.47
  360.5 5.4 %collective-permute-done.55 = bf16[128,1024]{1,0:T(8,128)(2,1)S(1)} collective-permute-done((bf16[128,1024]{1,0:T(8,128)(2,1)S(1)}, bf16[128,1024]{1,0:T(8,128)(2,1)S(1)}, u32[]{:S(2)}, u32[]{:S(2)}) %collective-permute-start.55) | collective-permute-done | bytes 262176 | tf_op jit(solution)/shard_map/ppermute | solution.py:129
  368.0 17.0 %collective-permute-done.54 = bf16[128,1024]{1,0:T(8,128)(2,1)S(1)} collective-permute-done((bf16[128,1024]{1,0:T(8,128)(2,1)S(1)}, bf16[128,1024]{1,0:T(8,128)(2,1)S(1)}, u32[]{:S(2)}, u32[]{:S(2)}) %collective-permute-start.54) | collective-permute-done | bytes 262176 | tf_op jit(solution)/shard_map/ppermute | solution.py:129
  401.6 37.0 %collective-permute-done.57 = f32[4,128]{1,0:T(4,128)S(1)} collective-permute-done((f32[4,128]{1,0:T(4,128)S(1)}, f32[4,128]{1,0:T(4,128)S(1)}, u32[]{:S(2)}, u32[]{:S(2)}) %collective-permute-start.57) | collective-permute-done | bytes 2080 | tf_op jit(solution)/shard_map/ppermute | solution.py:129
  (360 shorter events, 185.2 us)
Async XLA Ops:
  2.8 22.5 %collective-permute-start.21 = (bf16[32,1024]{1,0:T(8,128)(2,1)}, bf16[32,1024]{1,0:T(8,128)(2,1)}, u32[]{:S(2)}, u32[]{:S(2)}) collective-permute-start(bf16[32,1024]{1,0:T(8,128)(2,1)} %refs_0_.3), channel_id=1, source_target_pairs={{0,16},{4,20},{8,24},{12,28},{16,0},{20,4},{24,8},{28,12},{1,17},{... | collective-permute-start | bytes 196616 | tf_op jit(solution)/shard_map/ppermute | solution.py:129
  21.6 24.5 %collective-permute-start.11 = (bf16[128,768]{1,0:T(8,128)(2,1)S(1)}, bf16[128,768]{1,0:T(8,128)(2,1)S(1)}, u32[]{:S(2)}, u32[]{:S(2)}) collective-permute-start(bf16[128,768]{1,0:T(8,128)(2,1)S(1)} %copy.85.refs_0_), channel_id=1, source_target_pairs={{0,24},{4,28},{8,16},{12,20},{16,8},{20,12},{24,0},{28,4},{1,25},{... | collective-permute-start | bytes 589832 | tf_op jit(solution)/shard_map/ppermute | solution.py:129
  27.7 38.0 %collective-permute-start.35 = (bf16[128,1024]{1,0:T(8,128)(2,1)}, bf16[128,1024]{1,0:T(8,128)(2,1)S(1)}, u32[]{:S(2)}, u32[]{:S(2)}) collective-permute-start(bf16[128,1024]{1,0:T(8,128)(2,1)} %refs_0_.5), channel_id=1, source_target_pairs={{0,16},{4,20},{8,24},{12,28},{16,0},{20,4},{24,8},{28,12},{1,17},{... | collective-permute-start | bytes 786440 | tf_op jit(solution)/shard_map/ppermute | solution.py:129
  30.6 35.1 %collective-permute-start.33 = (bf16[128,1024]{1,0:T(8,128)(2,1)}, bf16[128,1024]{1,0:T(8,128)(2,1)S(1)}, u32[]{:S(2)}, u32[]{:S(2)}) collective-permute-start(bf16[128,1024]{1,0:T(8,128)(2,1)} %refs_0_.5), channel_id=1, source_target_pairs={{0,8},{4,12},{8,0},{12,4},{16,24},{20,28},{24,16},{28,20},{1,9},{5... | collective-permute-start | bytes 786440 | tf_op jit(solution)/shard_map/ppermute | solution.py:129
  70.4 59.3 %collective-permute-start.4 = (bf16[512,1024]{1,0:T(8,128)(2,1)}, bf16[512,1024]{1,0:T(8,128)(2,1)}, u32[]{:S(2)}, u32[]{:S(2)}) collective-permute-start(bf16[512,1024]{1,0:T(8,128)(2,1)} %fusion.19), channel_id=1, source_target_pairs={{0,2},{1,3},{2,0},{3,1},{4,6},{5,7},{6,4},{7,5},{8,10},{9,11},{10,... | collective-permute-start | bytes 3145736 | tf_op jit(solution)/shard_map/ppermute | solution.py:129
  102.9 47.0 %collective-permute-start.1 = (bf16[512,1024]{1,0:T(8,128)(2,1)}, bf16[512,1024]{1,0:T(8,128)(2,1)}, u32[]{:S(2)}, u32[]{:S(2)}) collective-permute-start(bf16[512,1024]{1,0:T(8,128)(2,1)} %fusion.10), channel_id=1, source_target_pairs={{0,2},{1,3},{2,0},{3,1},{4,6},{5,7},{6,4},{7,5},{8,10},{9,11},{10,... | collective-permute-start | bytes 3145736 | tf_op jit(solution)/shard_map/ppermute | solution.py:129
  108.5 41.9 %collective-permute-start = (bf16[512,1024]{1,0:T(8,128)(2,1)}, bf16[512,1024]{1,0:T(8,128)(2,1)}, u32[]{:S(2)}, u32[]{:S(2)}) collective-permute-start(bf16[512,1024]{1,0:T(8,128)(2,1)} %fusion.10), channel_id=1, source_target_pairs={{0,1},{1,0},{2,3},{3,2},{4,5},{5,4},{6,7},{7,6},{8,9},{9,8},{10,11... | collective-permute-start | bytes 3145736 | tf_op jit(solution)/shard_map/ppermute | solution.py:129
  112.5 39.7 %collective-permute-start.3 = (bf16[512,1024]{1,0:T(8,128)(2,1)}, bf16[512,1024]{1,0:T(8,128)(2,1)}, u32[]{:S(2)}, u32[]{:S(2)}) collective-permute-start(bf16[512,1024]{1,0:T(8,128)(2,1)} %fusion.19), channel_id=1, source_target_pairs={{0,1},{1,0},{2,3},{3,2},{4,5},{5,4},{6,7},{7,6},{8,9},{9,8},{10,11... | collective-permute-start | bytes 3145736 | tf_op jit(solution)/shard_map/ppermute | solution.py:129
  129.8 24.5 %collective-permute-start.5 = (bf16[512,1024]{1,0:T(8,128)(2,1)}, bf16[512,1024]{1,0:T(8,128)(2,1)}, u32[]{:S(2)}, u32[]{:S(2)}) collective-permute-start(bf16[512,1024]{1,0:T(8,128)(2,1)} %collective-permute-done.4), channel_id=1, source_target_pairs={{0,1},{1,0},{2,3},{3,2},{4,5},{5,4},{6,7},{7,6},{8,9},{9,8},{10,11... | collective-permute-start | bytes 3145736 | tf_op jit(solution)/shard_map/ppermute | solution.py:129
  277.5 37.3 %collective-permute-start.58 = (bf16[4,32,1024]{2,1,0:T(8,128)(2,1)}, bf16[4,32,1024]{2,1,0:T(8,128)(2,1)}, u32[]{:S(2)}, u32[]{:S(2)}) collective-permute-start(bf16[4,32,1024]{2,1,0:T(8,128)(2,1)} %pad_maximum_fusion.2), channel_id=1, source_target_pairs={{0,4},{4,0},{8,12},{12,8},{16,20},{20,16},{24,28},{28,24},{1,5},{5... | collective-permute-start | bytes 786440 | tf_op jit(solution)/shard_map/ppermute | solution.py:129
  277.8 41.6 %collective-permute-start.45 = (bf16[4,128,768]{2,1,0:T(8,128)(2,1)}, bf16[4,128,768]{2,1,0:T(8,128)(2,1)}, u32[]{:S(2)}, u32[]{:S(2)}) collective-permute-start(bf16[4,128,768]{2,1,0:T(8,128)(2,1)} %get-tuple-element.33), channel_id=1, source_target_pairs={{0,4},{4,0},{8,12},{12,8},{16,20},{20,16},{24,28},{28,24},{1,5},{5... | collective-permute-start | bytes 2359304 | tf_op jit(solution)/shard_map/ppermute | solution.py:129
  279.6 24.4 %collective-permute-start.49 = (f32[1,2816]{1,0:T(1,128)S(1)}, f32[1,2816]{1,0:T(1,128)S(1)}, u32[]{:S(2)}, u32[]{:S(2)}) collective-permute-start(f32[1,2816]{1,0:T(1,128)S(1)} %broadcast_in_dim.96), channel_id=1, source_target_pairs={{0,4},{4,0},{8,12},{12,8},{16,20},{20,16},{24,28},{28,24},{1,5},{5... | collective-permute-start | bytes 33800 | tf_op jit(solution)/shard_map/ppermute | solution.py:129
  279.9 69.5 %collective-permute-start.52 = (bf16[4,128,1024]{2,1,0:T(8,128)(2,1)}, bf16[4,128,1024]{2,1,0:T(8,128)(2,1)}, u32[]{:S(2)}, u32[]{:S(2)}) collective-permute-start(bf16[4,128,1024]{2,1,0:T(8,128)(2,1)} %get-tuple-element.35), channel_id=1, source_target_pairs={{0,4},{4,0},{8,12},{12,8},{16,20},{20,16},{24,28},{28,24},{1,5},{5... | collective-permute-start | bytes 3145736 | tf_op jit(solution)/shard_map/ppermute | solution.py:129
  289.9 63.2 %collective-permute-start.40 = (bf16[512,1024]{1,0:T(8,128)(2,1)}, bf16[512,1024]{1,0:T(8,128)(2,1)}, u32[]{:S(2)}, u32[]{:S(2)}) collective-permute-start(bf16[512,1024]{1,0:T(8,128)(2,1)} %get-tuple-element.93), channel_id=1, source_target_pairs={{0,1},{1,0},{2,3},{3,2},{4,5},{5,4},{6,7},{7,6},{8,9},{9,8},{10,11... | collective-permute-start | bytes 3145736 | tf_op jit(solution)/shard_map/ppermute | solution.py:129
  323.0 33.7 %collective-permute-start.62 = (bf16[4,128,1024]{2,1,0:T(8,128)(2,1)}, bf16[4,128,1024]{2,1,0:T(8,128)(2,1)}, u32[]{:S(2)}, u32[]{:S(2)}) collective-permute-start(bf16[4,128,1024]{2,1,0:T(8,128)(2,1)} %get-tuple-element.37), channel_id=1, source_target_pairs={{0,4},{4,0},{8,12},{12,8},{16,20},{20,16},{24,28},{28,24},{1,5},{5... | collective-permute-start | bytes 3145736 | tf_op jit(solution)/shard_map/ppermute | solution.py:129
  342.8 44.4 %collective-permute-start.43 = (bf16[512,1024]{1,0:T(8,128)(2,1)}, bf16[512,1024]{1,0:T(8,128)(2,1)}, u32[]{:S(2)}, u32[]{:S(2)}) collective-permute-start(bf16[512,1024]{1,0:T(8,128)(2,1)} %get-tuple-element.91), channel_id=1, source_target_pairs={{0,1},{1,0},{2,3},{3,2},{4,5},{5,4},{6,7},{7,6},{8,9},{9,8},{10,11... | collective-permute-start | bytes 3145736 | tf_op jit(solution)/shard_map/ppermute | solution.py:129
  353.2 31.8 %collective-permute-start.54 = (bf16[128,1024]{1,0:T(8,128)(2,1)S(1)}, bf16[128,1024]{1,0:T(8,128)(2,1)S(1)}, u32[]{:S(2)}, u32[]{:S(2)}) collective-permute-start(bf16[128,1024]{1,0:T(8,128)(2,1)S(1)} %get-tuple-element.102), channel_id=1, source_target_pairs={{0,16},{4,20},{8,24},{12,28},{16,0},{20,4},{24,8},{28,12},{1,17},{... | collective-permute-start | bytes 786440 | tf_op jit(solution)/shard_map/ppermute | solution.py:129
  356.8 82.5 %collective-permute-start.42 = (bf16[512,1024]{1,0:T(8,128)(2,1)S(1)}, bf16[512,1024]{1,0:T(8,128)(2,1)S(1)}, u32[]{:S(2)}, u32[]{:S(2)}) collective-permute-start(bf16[512,1024]{1,0:T(8,128)(2,1)S(1)} %copy-done.18), channel_id=1, source_target_pairs={{0,1},{1,0},{2,3},{3,2},{4,5},{5,4},{6,7},{7,6},{8,9},{9,8},{10,11... | collective-permute-start | bytes 3145736 | tf_op jit(solution)/shard_map/ppermute | solution.py:129
  359.4 32.9 %collective-permute-start.63 = (bf16[128,1024]{1,0:T(8,128)(2,1)S(1)}, bf16[128,1024]{1,0:T(8,128)(2,1)S(1)}, u32[]{:S(2)}, u32[]{:S(2)}) collective-permute-start(bf16[128,1024]{1,0:T(8,128)(2,1)S(1)} %get-tuple-element.97), channel_id=1, source_target_pairs={{0,8},{4,12},{8,0},{12,4},{16,24},{20,28},{24,16},{28,20},{1,9},{5... | collective-permute-start | bytes 786440 | tf_op jit(solution)/shard_map/ppermute | solution.py:129
  366.0 26.7 %collective-permute-start.65 = (bf16[128,1024]{1,0:T(8,128)(2,1)S(1)}, bf16[128,1024]{1,0:T(8,128)(2,1)S(1)}, u32[]{:S(2)}, u32[]{:S(2)}) collective-permute-start(bf16[128,1024]{1,0:T(8,128)(2,1)S(1)} %get-tuple-element.98), channel_id=1, source_target_pairs={{0,24},{4,28},{8,16},{12,20},{16,8},{20,12},{24,0},{28,4},{1,25},{... | collective-permute-start | bytes 786440 | tf_op jit(solution)/shard_map/ppermute | solution.py:129
  389.0 50.3 %collective-permute-start.44 = (bf16[512,1024]{1,0:T(8,128)(2,1)S(1)}, bf16[512,1024]{1,0:T(8,128)(2,1)S(1)}, u32[]{:S(2)}, u32[]{:S(2)}) collective-permute-start(bf16[512,1024]{1,0:T(8,128)(2,1)S(1)} %add_convert_fusion.2), channel_id=1, source_target_pairs={{0,2},{1,3},{2,0},{3,1},{4,6},{5,7},{6,4},{7,5},{8,10},{9,11},{10,... | collective-permute-start | bytes 3145736 | tf_op jit(solution)/shard_map/ppermute | solution.py:129
  392.3 47.8 %collective-permute-start.39 = (bf16[512,1024]{1,0:T(8,128)(2,1)S(1)}, bf16[512,1024]{1,0:T(8,128)(2,1)S(1)}, u32[]{:S(2)}, u32[]{:S(2)}) collective-permute-start(bf16[512,1024]{1,0:T(8,128)(2,1)S(1)} %copy-done.17), channel_id=1, source_target_pairs={{0,1},{1,0},{2,3},{3,2},{4,5},{5,4},{6,7},{7,6},{8,9},{9,8},{10,11... | collective-permute-start | bytes 3145736 | tf_op jit(solution)/shard_map/ppermute | solution.py:129
  392.6 47.5 %collective-permute-start.41 = (bf16[512,1024]{1,0:T(8,128)(2,1)S(1)}, bf16[512,1024]{1,0:T(8,128)(2,1)S(1)}, u32[]{:S(2)}, u32[]{:S(2)}) collective-permute-start(bf16[512,1024]{1,0:T(8,128)(2,1)S(1)} %add_convert_fusion.3), channel_id=1, source_target_pairs={{0,2},{1,3},{2,0},{3,1},{4,6},{5,7},{6,4},{7,5},{8,10},{9,11},{10,... | collective-permute-start | bytes 3145736 | tf_op jit(solution)/shard_map/ppermute | solution.py:129
  396.4 42.2 %collective-permute-start.57 = (f32[4,128]{1,0:T(4,128)S(1)}, f32[4,128]{1,0:T(4,128)S(1)}, u32[]{:S(2)}, u32[]{:S(2)}) collective-permute-start(f32[4,128]{1,0:T(4,128)S(1)} %fusion.49), channel_id=1, source_target_pairs={{0,2},{1,3},{2,0},{3,1},{4,6},{5,7},{6,4},{7,5},{8,10},{9,11},{10,... | collective-permute-start | bytes 6152 | tf_op jit(solution)/shard_map/ppermute | solution.py:129
  (107 other events, 1792.7 us)

commit v2 on v0

v2 whole, which is shorter than its diff:
```python
import functools
import math

import jax
import jax.numpy as jnp
from jax import lax
from jax.experimental import pallas as pl
from jax.experimental.pallas import tpu as pltpu
from jax.sharding import PartitionSpec as P

HD = 64
ROT = 16
SEQ_LEN = 1024
EPS = 1e-05
NEGATIVE = -1e30
QB = 256
CHUNK = 128
PARAMS = pltpu.CompilerParams(vmem_limit_bytes=60 * 1024 * 1024)
BF16 = jnp.bfloat16
F32 = jnp.float32
COST = 1.0
VMEM = pl.BlockSpec(memory_space=pltpu.VMEM)
SMEM = pl.BlockSpec(memory_space=pltpu.SMEM)
ANY = pl.BlockSpec(memory_space=pl.ANY)


def shape_of(dims, kind=BF16):
    return jax.ShapeDtypeStruct(dims, kind)


def cost(flops, moved):
    return pl.CostEstimate(
        flops=int(flops * COST), bytes_accessed=int(moved * COST), transcendentals=0
    )


def nn(left, right):
    return lax.dot_general(left, right, (((1,), (0,)), ((), ())), preferred_element_type=F32)


def nt(left, right):
    return lax.dot_general(left, right, (((1,), (1,)), ((), ())), preferred_element_type=F32)


def tn(left, right):
    return lax.dot_general(left, right, (((0,), (0,)), ((), ())), preferred_element_type=F32)


def copies(pairs, sems, first=0):
    made = [pltpu.make_async_copy(s, d, sems.at[first + i]) for i, (s, d) in enumerate(pairs)]
    for copy in made:
        copy.start()
    return made


def pack_kernel(project_ref, dense_ref, shrink_ref, turns_ref, out_ref, cos_ref, up_ref, dn_ref):
    heads = project_ref.shape[1] // (3 * HD)
    rows = dense_ref.shape[0]
    width = heads * HD
    out_ref[0] = shrink_ref[...]
    for part in range(3):
        pieces = [
            project_ref[:, (3 * head + part) * HD : (3 * head + part + 1) * HD]
            for head in range(heads)
        ]
        out_ref[1, :, part * width : (part + 1) * width] = jnp.concatenate(pieces, axis=1)
    for j in range(4):
        columns = slice(j * width, (j + 1) * width)
        out_ref[1, j * rows : (j + 1) * rows, 3 * width :] = dense_ref[:, columns]
    half = ROT // 2
    length = turns_ref.shape[0]
    cosine, sine = turns_ref[:, :half], turns_ref[:, half:]
    rest = jnp.zeros((length, HD - ROT), F32)
    none = jnp.zeros((length, half), F32)
    cos_ref[...] = jnp.concatenate([cosine, cosine, rest + 1.0] * 2, axis=1)
    up_ref[...] = jnp.concatenate([none, sine, rest] * 2, axis=1)
    dn_ref[...] = jnp.concatenate([-sine, none, rest] * 2, axis=1)


def pack(project, dense, shrink, turns):
    table = shape_of((turns.shape[0], 2 * HD), F32)
    return pl.pallas_call(
        pack_kernel,
        in_specs=[VMEM] * 4,
        out_specs=[VMEM] * 4,
        out_shape=[shape_of((2,) + shrink.shape)] + [table] * 3,
        compiler_params=PARAMS,
        cost_estimate=cost(0, 3 << 20),
        name="pack",
    )(project, dense, shrink, turns)


def column(row):
    return jnp.broadcast_to(row, (8, row.shape[1])).T[:, :1]


def shift_times(shift, weight):
    high = shift.astype(BF16)
    rest = shift - high.astype(F32)
    middle = rest.astype(BF16)
    low = (rest - middle.astype(F32)).astype(BF16)
    parts = nn(jnp.concatenate([high, middle, low], axis=0), weight)
    return jnp.sum(parts, axis=0, keepdims=True)


def scaled_rows(place, k, weight, gain_ref, shift_ref):
    rows = weight.shape[0]
    start = pl.multiple_of(lax.bitwise_xor(place, k) * rows, rows)
    part = shift_times(shift_ref[:, pl.ds(start, rows)], weight)
    gain = column(gain_ref[:, pl.ds(start, rows)])
    return start, (weight.astype(F32) * gain).astype(BF16), part


def block_list(refs):
    own, near, far, far_near, pair, pair_near = refs
    return [own, near, pair.at[0], pair_near.at[0], far, far_near, pair.at[1], pair_near.at[1]]


def join_rest_kernel(place_ref, *refs):
    gain_ref, shift_ref, offset_ref, shrink_ref, project_ref, dense_ref, bias_ref = refs[6:]
    total = offset_ref[...]
    wide = project_ref.shape[1]
    for k, ref in enumerate(block_list(refs[:6])):
        block = ref[1]
        start, scaled, part = scaled_rows(
            place_ref[0], k, block[:, :wide], gain_ref, shift_ref
        )
        shrink_ref[pl.ds(start, block.shape[0]), :] = ref[0]
        project_ref[pl.ds(start, block.shape[0]), :] = scaled
        total = total + part
        rows = block.shape[0] // 4
        across = block.shape[1] // 4
        base = pl.multiple_of(lax.bitwise_xor(place_ref[0], k) * rows, rows)
        for j in range(4):
            dense_ref[pl.ds(base, rows), j * across : (j + 1) * across] = block[
                j * rows : (j + 1) * rows, wide:
            ]
    bias_ref[...] = total


def join_rest(place, blocks, gain, shift, offset):
    _, rows, columns = blocks[0].shape
    total = 8 * rows
    wide = offset.shape[1]
    return pl.pallas_call(
        join_rest_kernel,
        in_specs=[SMEM] + [VMEM] * 9,
        out_specs=[VMEM] * 4,
        out_shape=[
            shape_of((total, columns)),
            shape_of((total, wide)),
            shape_of((total // 4, columns)),
            shape_of((1, wide), F32),
        ],
        compiler_params=PARAMS,
        cost_estimate=cost(1e9, 10 << 20),
        name="join_rest",
    )(place, *blocks, gain, shift, offset)


def join_expand_kernel(place_ref, *refs):
    gain_ref, shift_ref, offset_ref, out_ref, bias_ref = refs[6:]
    total = offset_ref[...]
    for k, ref in enumerate(block_list(refs[:6])):
        start, scaled, part = scaled_rows(place_ref[0], k, ref[...], gain_ref, shift_ref)
        out_ref[pl.ds(start, scaled.shape[0]), :] = scaled
        total = total + part
    bias_ref[...] = total


def join_expand(place, blocks, gain, shift, offset):
    rows, columns = blocks[0].shape
    return pl.pallas_call(
        join_expand_kernel,
        in_specs=[SMEM] + [VMEM] * 9,
        out_specs=[VMEM] * 2,
        out_shape=[shape_of((8 * rows, columns)), shape_of((1, columns), F32)],
        compiler_params=PARAMS,
        cost_estimate=cost(1e9, 6 << 20),
        name="join_expand",
    )(place, *blocks, gain, shift, offset)


def normalise(features):
    centre = features - jnp.mean(features, axis=-1, keepdims=True)
    rate = lax.rsqrt(jnp.mean(centre * centre, axis=-1, keepdims=True) + EPS)
    return centre * rate, rate


def prepare_kernel(inputs_ref, cotangent_ref, keep_ref, both_ref, sum_ref):
    both_ref[0] = normalise(inputs_ref[...].astype(F32))[0].astype(BF16)
    upstream = cotangent_ref[...].astype(F32) * keep_ref[...]
    both_ref[1] = upstream.astype(BF16)
    sum_ref[...] = jnp.sum(upstream, axis=0, keepdims=True)


def prepare(inputs, cotangent, keep):
    return pl.pallas_call(
        prepare_kernel,
        in_specs=[VMEM] * 3,
        out_specs=[VMEM] * 2,
        out_shape=[shape_of((2,) + inputs.shape), shape_of((1, inputs.shape[1]), F32)],
        compiler_params=PARAMS,
        cost_estimate=cost(0, 6 << 20),
        name="prepare",
    )(inputs, cotangent, keep)


def attention_kernel(
    core_ref,
    first_ref,
    second_ref,
    w_ref,
    b_ref,
    d_ref,
    lrow_ref,
    cos_ref,
    up_ref,
    dn_ref,
    mixed_ref,
    pg_ref,
    sum_ref,
    q_s,
    k_s,
    v_s,
    g_s,
    kt_s,
    vt_s,
    gt_s,
    pt_s,
    dst_s,
    ot_s,
    dqt_s,
    dk_s,
    dv_s,
    out_s,
    scores_s,
    qm_s,
    gm_s,
    lcol_s,
):
    half_rows = first_ref.shape[1]
    length = 2 * half_rows
    width = d_ref.shape[0]
    blocks = length // QB
    scale = 1.0 / math.sqrt(HD)

    def starts(piece):
        return pl.multiple_of(lax.bitwise_xor(core_ref[0], piece) * half_rows, half_rows)

    for piece, ref in enumerate((first_ref, second_ref)):
        rows = pl.ds(starts(piece), half_rows)
        cos, up, dn = cos_ref[rows, :], up_ref[rows, :], dn_ref[rows, :]

        def rotate(u):
            return u * cos + pltpu.roll(u, 8, axis=1) * up + pltpu.roll(u, 120, axis=1) * dn

        tokens = ref[0]
        g_s[rows, :] = nt(ref[1], d_ref[...]).astype(BF16)
        q = nn(tokens, w_ref[:, :width]) + b_ref[:, :width]
        k = nn(tokens, w_ref[:, width : 2 * width]) + b_ref[:, width : 2 * width]
        for lo in range(0, width, 128):
            sl = slice(lo, lo + 128)
            turned = rotate(q[:, sl]).astype(BF16).astype(F32)
            q_s[rows, sl] = (turned * scale).astype(BF16)
            k_s[rows, sl] = rotate(k[:, sl]).astype(BF16)
        v_s[rows, :] = (nn(tokens, w_ref[:, 2 * width :]) + b_ref[:, 2 * width :]).astype(BF16)

    cos, up, dn = cos_ref[...], up_ref[...], dn_ref[...]

    def rotate_back(w):
        return w * cos + pltpu.roll(w * up, 120, axis=1) + pltpu.roll(w * dn, 8, axis=1)

    lane = lax.broadcasted_iota(jnp.int32, (1, 128), 1)
    zero = jnp.zeros((), BF16)
    lcol_s[...] = column(lrow_ref[...])

    def folded_rows(value, fold):
        return fold(value.reshape(value.shape[0] // 8, 8, value.shape[1]), axis=0)

    def pair(p, carry):
        lo = pl.multiple_of(p * 128, 128)
        sl = pl.ds(lo, 128)
        kt_s[...] = k_s[:, sl].T
        vt_s[...] = v_s[:, sl].T
        gt_s[...] = g_s[:, sl].astype(F32).T
        for a in range(2):
            half = (lane >= HD * a) & (lane < HD * (a + 1))
            qm_s[a] = jnp.where(half, q_s[:, sl], zero)
            gm_s[a] = jnp.where(half, g_s[:, sl], zero)
        for i in range(blocks):
            for a in range(2):
                hs = slice(HD * a, HD * (a + 1))
                end = (i + 1) * QB
                rows = slice(i * QB, end)
                qm = qm_s[a, rows, :]
                gm = gm_s[a, rows, :]
                chunks = [slice(c, c + CHUNK) for c in range(0, end, CHUNK)]
                top = None
                for cs in chunks:
                    s = nt(k_s[cs, sl], qm)
                    same = lcol_s[cs, :] == lrow_ref[:, rows]
                    if cs.start >= i * QB:
                        key = lax.broadcasted_iota(jnp.int32, (CHUNK, QB), 0)
                        query = lax.broadcasted_iota(jnp.int32, (CHUNK, QB), 1)
                        same = same & (key + (cs.start - i * QB) <= query)
                    s = jnp.where(same, s, NEGATIVE)
                    scores_s[a, cs, :] = s
                    part = folded_rows(s, jnp.max)
                    top = part if top is None else jnp.maximum(top, part)
                top = jnp.max(top, axis=0, keepdims=True)
                total = None
                for cs in chunks:
                    e = jnp.exp(scores_s[a, cs, :] - top)
                    scores_s[a, cs, :] = e
                    part = folded_rows(e, jnp.sum)
                    total = part if total is None else total + part
                rate = 1.0 / jnp.sum(total, axis=0, keepdims=True)
                for cs in chunks:
                    pt_s[a, cs, rows] = (scores_s[a, cs, :] * rate).astype(BF16)
                out = nn(vt_s[hs, 0:end], pt_s[a, 0:end, rows])
                ot_s[hs, rows] = out
                inner = jnp.sum(gt_s[hs, rows] * out, axis=0, keepdims=True)
                for cs in chunks:
                    dp = nt(v_s[cs, sl], gm) - inner
                    dst_s[a, cs, rows] = (scores_s[a, cs, :] * rate * dp).astype(BF16)
                dqt_s[hs, rows] = nn(kt_s[hs, 0:end], dst_s[a, 0:end, rows]) * scale
        for j in range(blocks):
            rows = slice(j * QB, length)
            out = slice(j * QB, (j + 1) * QB)
            dk_s[out, :] = nn(dst_s[0, out, rows], qm_s[0, rows, :]) + nn(
                dst_s[1, out, rows], qm_s[1, rows, :]
            )
            dv_s[out, :] = nn(pt_s[0, out, rows], gm_s[0, rows, :]) + nn(
                pt_s[1, out, rows], gm_s[1, rows, :]
            )

        def put(at, values):
            cols = pl.ds(pl.multiple_of(at + lo, 128), 128)
            values = values.astype(BF16)
            sum_ref[:, cols] = jnp.sum(values.astype(F32), axis=0, keepdims=True)
            out_s[...] = values
            for piece in range(2):
                pg_ref[piece, :, cols] = out_s[pl.ds(starts(piece), half_rows), :]

        put(0, rotate_back(dqt_s[...].T))
        put(width, rotate_back(dk_s[...]))
        put(2 * width, dv_s[...])
        out_s[...] = ot_s[...].T.astype(BF16)
        for piece in range(2):
            mixed_ref[piece, :, sl] = out_s[pl.ds(starts(piece), half_rows), :]
        return carry

    lax.fori_loop(0, width // 128, pair, 0)


def attention(core, parts, w, b, dense, marks, tables):
    half_rows = parts[0].shape[1]
    length = 2 * half_rows
    width = dense.shape[0]
    return pl.pallas_call(
        attention_kernel,
        in_specs=[SMEM] + [VMEM] * 9,
        out_specs=[VMEM] * 3,
        out_shape=[
            shape_of((2, half_rows, width)),
            shape_of((2, half_rows, 3 * width)),
            shape_of((1, 3 * width), F32),
        ],
        scratch_shapes=[pltpu.VMEM((length, width), BF16)] * 4
        + [pltpu.VMEM((128, length), BF16)] * 2
        + [pltpu.VMEM((128, length), F32)]
        + [pltpu.VMEM((2, length, length), BF16)] * 2
        + [pltpu.VMEM((128, length), F32)] * 2
        + [pltpu.VMEM((length, 128), F32)] * 2
        + [pltpu.VMEM((length, 128), BF16)]
        + [pltpu.VMEM((2, length, QB), F32)]
        + [pltpu.VMEM((2, length, 128), BF16)] * 2
        + [pltpu.VMEM((length, 1), jnp.int32)],
        compiler_params=PARAMS,
        cost_estimate=cost(2.3e10, 8 << 20),
        name="attention",
    )(core, *parts, w, b, dense, marks[None, :], *tables)


def rotary_turns():
    half = ROT // 2
    places = jnp.arange(SEQ_LEN, dtype=jnp.int32).astype(F32)
    rates = jnp.exp(
        jnp.arange(half, dtype=jnp.int32).astype(F32) * (-2.0 * math.log(10000.0) / ROT)
    )
    angles = places[:, None] * rates[None, :]
    return jnp.concatenate([jnp.cos(angles), jnp.sin(angles)], axis=1)


def turn(slot):
    return 2 * (slot % 2) + slot // 2


def put_pair(place_ref, m, product, near_s, own_s, columns=slice(None)):
    rows = product.shape[0] // 2
    low, high = product[:rows], product[rows:]
    swap = (place_ref[0] & 1) == 1
    own_s[m, :, columns] = jnp.where(swap, high, low).astype(BF16)
    near_s[m, :, columns] = jnp.where(swap, low, high).astype(BF16)


def pair_rows(place_ref, m, width):
    other = lax.bitwise_xor(lax.shift_right_logical(place_ref[0], 1), turn(m))
    return pl.ds(pl.multiple_of(other * width, width), width)


def loaded(parts, held, sems, first, which=None):
    if which is not None:
        parts = [ref.at[which] for ref in parts]
    rows = parts[0].shape[0]
    return copies(
        [(ref, held.at[pl.ds(p * rows, rows), :]) for p, ref in enumerate(parts)], sems, first
    )


def hidden_kernel(
    a_ref,
    b_ref,
    c_ref,
    d_ref,
    w_ref,
    bias_ref,
    act_ref,
    slope_ref,
    tokens_s,
    w_s,
    act_s,
    slope_s,
    in_sems,
    out_sems,
):
    rows = a_ref.shape[1]
    loads = copies([(w_ref, w_s)], in_sems)
    loads += loaded((a_ref, b_ref, c_ref, d_ref), tokens_s, in_sems, 1, 0)
    loads[0].wait()
    stores = []
    for p in range(4):
        loads[1 + p].wait()
        at = pl.ds(p * rows, rows)
        hidden = nn(tokens_s[at, :], w_s[...]) + bias_ref[...]
        phi = 0.5 * (1.0 + lax.erf(hidden * (1.0 / math.sqrt(2.0))))
        act_s[at, :] = (hidden * phi).astype(BF16)
        bell = jnp.exp(-0.5 * hidden * hidden) * (1.0 / math.sqrt(2.0 * math.pi))
        slope_s[at, :] = (phi + hidden * bell).astype(BF16)
        stores += copies(
            [(act_s.at[at, :], act_ref.at[at, :]), (slope_s.at[at, :], slope_ref.at[at, :])],
            out_sems,
            2 * p,
        )
    for copy in stores:
        copy.wait()


def hidden_layer(parts, w, bias):
    _, rows, width = parts[0].shape
    units = w.shape[1]
    return pl.pallas_call(
        hidden_kernel,
        in_specs=[ANY] * 5 + [VMEM],
        out_specs=[ANY] * 2,
        out_shape=[shape_of((4 * rows, units))] * 2,
        scratch_shapes=[pltpu.VMEM((4 * rows, width), BF16), pltpu.VMEM(w.shape, BF16)]
        + [pltpu.VMEM((4 * rows, units), BF16)] * 2
        + [pltpu.SemaphoreType.DMA((5,)), pltpu.SemaphoreType.DMA((8,))],
        compiler_params=PARAMS,
        cost_estimate=cost(6e9, 14 << 20),
        name="hidden",
    )(*parts, w, bias)


def shrink_grads_kernel(
    place_ref, act_ref, a_ref, b_ref, c_ref, d_ref, near_ref, own_ref, grads_s, in_sems
):
    m = pl.program_id(0)

    @pl.when(m == 0)
    def _():
        for copy in loaded((a_ref, b_ref, c_ref, d_ref), grads_s, in_sems, 0, 1):
            copy.wait()

    product = tn(act_ref[...], grads_s[...])
    rows = product.shape[0] // 2
    low, high = product[:rows], product[rows:]
    swap = (place_ref[0] & 1) == 1
    own_ref[...] = jnp.where(swap, high, low).astype(BF16)
    near_ref[...] = jnp.where(swap, low, high).astype(BF16)


def shrink_grads(place, active, parts, pairs):
    _, rows, width = parts[0].shape
    units = active.shape[1]
    block = units // (2 * pairs)
    return pl.pallas_call(
        shrink_grads_kernel,
        grid_spec=pltpu.PrefetchScalarGridSpec(
            num_scalar_prefetch=1,
            grid=(pairs,),
            in_specs=[
                pl.BlockSpec(
                    (4 * rows, 2 * block),
                    lambda m, place: (
                        0,
                        lax.bitwise_xor(lax.shift_right_logical(place[0], 1), turn(m)),
                    ),
                )
            ]
            + [ANY] * 4,
            out_specs=[pl.BlockSpec((None, block, width), lambda m, place: (m, 0, 0))] * 2,
            scratch_shapes=[
                pltpu.VMEM((4 * rows, width), BF16),
                pltpu.SemaphoreType.DMA((4,)),
            ],
        ),
        out_shape=[shape_of((pairs, block, width))] * 2,
        compiler_params=PARAMS,
        cost_estimate=cost(6e9, 10 << 20),
        name="shrink_grads",
    )(place, active, *parts)


def unhidden_kernel(
    place_ref,
    a_ref,
    b_ref,
    c_ref,
    d_ref,
    w_ref,
    slope_ref,
    grad_ref,
    near_ref,
    own_ref,
    sum_ref,
    grads_s,
    tokens_s,
    w_s,
    slope_s,
    near_s,
    own_s,
    in_sems,
    out_sems,
):
    rows = a_ref.shape[1]
    parts = (a_ref, b_ref, c_ref, d_ref)
    loads = copies([(w_ref, w_s)], in_sems)
    loads += loaded(parts, grads_s, in_sems, 1, 1)
    loads += copies(
        [
            (slope_ref.at[pl.ds(p * rows, rows), :], slope_s.at[pl.ds(p * rows, rows), :])
            for p in range(4)
        ],
        in_sems,
        5,
    )
    loads += loaded(parts, tokens_s, in_sems, 9, 0)
    loads[0].wait()
    stores = []
    for p in range(4):
        loads[1 + p].wait()
        loads[5 + p].wait()
        at = pl.ds(p * rows, rows)
        grad = (nt(grads_s[at, :], w_s[...]) * slope_s[at, :].astype(F32)).astype(BF16)
        slope_s[at, :] = grad
        part = jnp.sum(grad.astype(F32), axis=0, keepdims=True)
        if p == 0:
            sum_ref[...] = part
        else:
            sum_ref[...] += part
        stores += copies([(slope_s.at[at, :], grad_ref.at[at, :])], out_sems, p)
    for copy in loads[9:]:
        copy.wait()
    count, block, _ = near_ref.shape
    for m in range(count):
        product = tn(tokens_s[:, pair_rows(place_ref, m, 2 * block)], slope_s[...])
        put_pair(place_ref, m, product, near_s, own_s)
        stores += copies(
            [(near_s.at[m], near_ref.at[m]), (own_s.at[m], own_ref.at[m])], out_sems, 4 + 2 * m
        )
    for copy in stores:
        copy.wait()


def unhidden_layer(place, parts, w, slope, pairs):
    _, rows, width = parts[0].shape
    units = w.shape[0]
    blocks = (pairs, width // (2 * pairs), units)
    return pl.pallas_call(
        unhidden_kernel,
        in_specs=[SMEM] + [ANY] * 6,
        out_specs=[ANY] * 3 + [VMEM],
        out_shape=[shape_of((4 * rows, units))]
        + [shape_of(blocks)] * 2
        + [shape_of((1, units), F32)],
        scratch_shapes=[pltpu.VMEM((4 * rows, width), BF16)] * 2
        + [pltpu.VMEM(w.shape, BF16)]
        + [pltpu.VMEM((4 * rows, units), BF16)]
        + [pltpu.VMEM(blocks, BF16)] * 2
        + [pltpu.SemaphoreType.DMA((13,)), pltpu.SemaphoreType.DMA((4 + 2 * pairs,))],
        compiler_params=PARAMS,
        cost_estimate=cost(1.2e10, 22 << 20),
        name="unhidden",
    )(place, *parts, w, slope)


def attention_grads_kernel(
    place_ref,
    a_ref,
    b_ref,
    c_ref,
    d_ref,
    mixed_one_ref,
    pg_one_ref,
    mixed_two_ref,
    pg_two_ref,
    near_ref,
    late_ref,
    own_ref,
    grads_s,
    tokens_s,
    mixed_s,
    pg_s,
    dense_s,
    near_s,
    own_s,
    in_sems,
    out_sems,
):
    parts = (a_ref, b_ref, c_ref, d_ref)
    mixed = [ref.at[p] for ref in (mixed_one_ref, mixed_two_ref) for p in range(2)]
    pg = [ref.at[p] for ref in (pg_one_ref, pg_two_ref) for p in range(2)]
    loads = loaded(parts, grads_s, in_sems, 0, 1)
    loads += loaded(mixed, mixed_s, in_sems, 4)
    loads += loaded(parts, tokens_s, in_sems, 8, 0)
    loads += loaded(pg, pg_s, in_sems, 12)
    for copy in loads[:8]:
        copy.wait()
    count, block, columns = own_ref.shape
    wide = pg_s.shape[1]
    few = block // 4
    dense_s[...] = tn(mixed_s[...], grads_s[...])
    for copy in loads[8:]:
        copy.wait()
    across = columns // 4
    swap = (place_ref[0] & 1) == 1
    stores = []
    for m in (2, 3, 0, 1):
        product = tn(tokens_s[:, pair_rows(place_ref, m, 2 * block)], pg_s[...])
        put_pair(place_ref, m, product, near_s, own_s, slice(0, wide))
        product = dense_s[pair_rows(place_ref, m, 2 * few), :]
        low, high = product[:few], product[few:]
        own = jnp.where(swap, high, low).astype(BF16)
        near = jnp.where(swap, low, high).astype(BF16)
        for j in range(4):
            cols = slice(j * across, (j + 1) * across)
            own_s[m, j * few : (j + 1) * few, wide:] = own[:, cols]
            near_s[m, j * few : (j + 1) * few, wide:] = near[:, cols]
        near_at = near_ref if m >= count // 2 else late_ref
        stores += copies(
            [(near_s.at[m], near_at.at[m % 2]), (own_s.at[m], own_ref.at[m])], out_sems, 2 * m
        )
    for copy in stores:
        copy.wait()


def attention_grads(place, parts, one, two, pairs):
    _, rows, width = parts[0].shape
    heads = one[0].shape[-1]
    wide = one[1].shape[-1]
    blocks = (pairs, width // (2 * pairs), wide + heads)
    return pl.pallas_call(
        attention_grads_kernel,
        in_specs=[SMEM] + [ANY] * 8,
        out_specs=[ANY] * 3,
        out_shape=[shape_of((pairs // 2,) + blocks[1:])] * 2 + [shape_of(blocks)],
        scratch_shapes=[pltpu.VMEM((4 * rows, width), BF16)] * 2
        + [pltpu.VMEM((4 * rows, heads), BF16), pltpu.VMEM((4 * rows, wide), BF16)]
        + [pltpu.VMEM((heads, width), F32)]
        + [pltpu.VMEM(blocks, BF16)] * 2
        + [pltpu.SemaphoreType.DMA((16,)), pltpu.SemaphoreType.DMA((2 * pairs,))],
        compiler_params=PARAMS,
        cost_estimate=cost(7e9, 16 << 20),
        name="attention_grads",
    )(place, *parts, *one, *two)


def results_kernel(
    mixed_ref,
    pg_ref,
    act_ref,
    grad_ref,
    dense_ref,
    shrink_ref,
    project_ref,
    expand_ref,
    mine_ref,
    theirs_ref,
    mixed_s,
    pg_s,
    act_s,
    grad_s,
    dense_s,
    shrink_s,
    project_s,
    expand_s,
    out_s,
    in_sems,
    out_sems,
    *,
    first,
):
    rows = mixed_ref.shape[1]
    theirs = pl.ds((first + 1) * rows, rows)
    mine = pl.ds(first * rows, rows)
    loads = copies(
        [
            (shrink_ref, shrink_s),
            (act_ref.at[theirs, :], act_s.at[1]),
            (mixed_ref, mixed_s),
            (dense_ref, dense_s),
            (expand_ref, expand_s),
            (grad_ref.at[theirs, :], grad_s.at[1]),
            (pg_ref, pg_s),
            (project_ref, project_s),
            (act_ref.at[mine, :], act_s.at[0]),
            (grad_ref.at[mine, :], grad_s.at[0]),
        ],
        in_sems,
    )
    stores = []
    for at, (piece, gradient, waits) in enumerate(
        ((1, 0, loads[:4]), (1, 1, loads[4:8]), (0, 0, loads[8:9]), (0, 1, loads[9:]))
    ):
        for copy in waits:
            copy.wait()
        if gradient:
            total = nt(grad_s[piece], expand_s[...]) + nt(pg_s[piece], project_s[...])
        else:
            total = nn(act_s[piece], shrink_s[...]) + nn(mixed_s[piece], dense_s[...])
        out_s[at] = total.astype(BF16)
        out_ref = theirs_ref if piece else mine_ref
        stores += copies([(out_s.at[at], out_ref.at[gradient])], out_sems, at)
    for copy in stores:
        copy.wait()


def results(mixed, pg, act, grad, dense, shrink, project, expand, first):
    _, rows, heads = mixed.shape
    wide = pg.shape[-1]
    units = act.shape[-1]
    width = dense.shape[1]
    return pl.pallas_call(
        functools.partial(results_kernel, first=first),
        in_specs=[ANY] * 8,
        out_specs=[ANY] * 2,
        out_shape=[shape_of((2, rows, width))] * 2,
        scratch_shapes=[pltpu.VMEM(mixed.shape, BF16), pltpu.VMEM(pg.shape, BF16)]
        + [pltpu.VMEM((2, rows, units), BF16)] * 2
        + [pltpu.VMEM(w.shape, BF16) for w in (dense, shrink, project, expand)]
        + [pltpu.VMEM((4, rows, width), BF16)]
        + [pltpu.SemaphoreType.DMA((10,)), pltpu.SemaphoreType.DMA((4,))],
        compiler_params=PARAMS,
        cost_estimate=cost(8e9, 16 << 20),
        name="results",
    )(mixed, pg, act, grad, dense, shrink, project, expand)


def exchange(value, axis, size, offset):
    return lax.ppermute(value, axis, [(i, i ^ offset) for i in range(size)])


def sum_over(value, axis, size, offset=1):
    while offset < size:
        value = value + exchange(value, axis, size, offset)
        offset *= 2
    return value


def slots(value, index, size):
    row = lax.broadcasted_iota(jnp.int32, (size, 1), 0)
    return jnp.where(row == index, value[None, :], 0.0)


def after(values, *first):
    return lax.optimization_barrier(tuple(values) + first)[: len(values)]


def hop(value, size, offset):
    return exchange(value, "fsdp", size, offset)


class Gather:
    def __init__(self, block, size, near=True):
        self.own, self.size = block, size
        self.far = hop(block, size, 4)
        self.near = hop(block, size, 1) if near else None
        self.far_near = None

    def second(self, *first):
        own, far = after((self.own, self.far), *first) if first else (self.own, self.far)
        self.pair = hop(jnp.stack([own, far]), self.size, 2)
        if self.far_near is None:
            self.far_near = hop(far, self.size, 1)

    def second_near(self):
        self.far_near = hop(self.far, self.size, 1)

    def third(self, *first):
        (pair,) = after((self.pair,), *first) if first else (self.pair,)
        self.pair_near = hop(pair, self.size, 1)

    def blocks(self, *first):
        every = (self.own, self.near, self.far, self.far_near, self.pair, self.pair_near)
        return after(every, *first) if first else every


class Scatter:
    def __init__(self, near, own, size, late=None):
        self.own, self.size = own, size
        if late is None:
            near = hop(near, size, 1)
            self.near, self.late = near[2:], near[:2]
            self.arrived = near
        else:
            self.near, self.late = hop(near, size, 1), hop(late, size, 1)
            self.arrived = self.near

    def second(self, *first):
        near, own = after((self.near, self.own[2:]), self.late, *first)
        self.pair = hop((own.astype(F32) + near.astype(F32)).astype(BF16), self.size, 2)
        return self.arrived

    def third(self, *first):
        pair, near = after((self.pair, self.late), *first) if first else (self.pair, self.late)
        total = self.own[1].astype(F32) + near[1].astype(F32) + pair[1].astype(F32)
        self.far = hop(total.astype(BF16), self.size, 4)
        return pair

    def terms(self):
        return self.own, self.late, self.pair, self.far

    def total(self):
        return sum(term.astype(F32) for term in (self.own[0], self.late[0], self.pair[0], self.far))


def row_of(value):
    return jnp.broadcast_to(value, (value.shape[0], 128)).T[:1, :]


def block_total(own_ref, late_ref, pair_ref, far_ref, columns):
    total = own_ref[:, columns].astype(F32) + late_ref[:, columns].astype(F32)
    return total + pair_ref[:, columns].astype(F32) + far_ref[:, columns].astype(F32)


def finish_project_kernel(
    own_ref, late_ref, pair_ref, far_ref, w_ref, sum_ref, vector_ref, grad_ref, dense_ref, part_ref
):
    wide = w_ref.shape[1]
    heads = wide // (3 * HD)
    gain, shift = column(vector_ref[0:1, :]), column(vector_ref[1:2, :])
    first = second = 0.0
    for head in range(heads):
        for part in range(3):
            at = (part * heads + head) * HD
            to = (head * 3 + part) * HD
            total = block_total(own_ref, late_ref, pair_ref, far_ref, slice(at, at + HD))
            weight = w_ref[:, to : to + HD].astype(F32)
            sums = sum_ref[:, at : at + HD]
            grad_ref[:, to : to + HD] = gain * total + shift * sums
            first = first + jnp.sum(weight * total, axis=1, keepdims=True)
            second = second + jnp.sum(weight * sums, axis=1, keepdims=True)
    part_ref[0:1, :] = row_of(first)
    part_ref[1:2, :] = row_of(second)
    rows, width = dense_ref.shape
    across = width // 4
    total = block_total(own_ref, late_ref, pair_ref, far_ref, slice(wide, wide + across))
    for j in range(4):
        dense_ref[:, j * across : (j + 1) * across] = total[j * rows : (j + 1) * rows, :]


def finish_project(terms, weight, sums, vectors, rows):
    width = weight.shape[0] * 8
    lead = pl.BlockSpec((None, weight.shape[0], width), lambda i: (0, 0, 0))
    whole = [
        pl.BlockSpec(shape, lambda i: (0, 0))
        for shape in (terms[3].shape, weight.shape, sums.shape, vectors.shape)
    ]
    outs = (weight.shape, (rows, width), (2, weight.shape[0]))
    return pl.pallas_call(
        finish_project_kernel,
        grid=(1,),
        in_specs=[lead] * 3 + whole,
        out_specs=[pl.BlockSpec(shape, lambda i: (0, 0)) for shape in outs],
        out_shape=[shape_of(shape, F32) for shape in outs],
        compiler_params=PARAMS,
        cost_estimate=cost(0, 4 << 20),
        name="finish_project",
    )(*terms, weight, sums, vectors)


def finish_expand_kernel(
    own_ref, late_ref, pair_ref, far_ref, w_ref, sum_ref, vector_ref, grad_ref, part_ref
):
    gain, shift = column(vector_ref[2:3, :]), column(vector_ref[3:4, :])
    total = block_total(own_ref, late_ref, pair_ref, far_ref, slice(None))
    weight = w_ref[...].astype(F32)
    grad_ref[...] = gain * total + shift * sum_ref[...]
    part_ref[0:1, :] = row_of(jnp.sum(weight * total, axis=1, keepdims=True))
    part_ref[1:2, :] = row_of(jnp.sum(weight * sum_ref[...], axis=1, keepdims=True))


def finish_expand(terms, weight, sums, vectors):
    lead = pl.BlockSpec((None,) + weight.shape, lambda i: (0, 0, 0))
    whole = [
        pl.BlockSpec(shape, lambda i: (0, 0))
        for shape in (terms[3].shape, weight.shape, sums.shape, vectors.shape)
    ]
    outs = (weight.shape, (2, weight.shape[0]))
    return pl.pallas_call(
        finish_expand_kernel,
        grid=(1,),
        in_specs=[lead] * 3 + whole,
        out_specs=[pl.BlockSpec(shape, lambda i: (0, 0)) for shape in outs],
        out_shape=[shape_of(shape, F32) for shape in outs],
        compiler_params=PARAMS,
        cost_estimate=cost(0, 4 << 20),
        name="finish_expand",
    )(*terms, weight, sums, vectors)


def finish_tokens_kernel(
    mine_ref, near_ref, far_ref, inputs_ref, cotangent_ref, keep_ref, bias_ref, out_ref, grad_ref
):
    def total(which):
        return (
            mine_ref[which].astype(F32) + near_ref[which].astype(F32) + far_ref[which].astype(F32)
        )

    features = inputs_ref[...].astype(F32)
    out_ref[...] = (features + total(0) + bias_ref[...]).astype(BF16)
    normed, rate = normalise(features)
    grad = total(1)
    inner = jnp.mean(grad * normed, axis=-1, keepdims=True)
    centre = jnp.mean(grad, axis=-1, keepdims=True)
    upstream = cotangent_ref[...].astype(F32) * keep_ref[...]
    grad_ref[...] = (upstream + rate * (grad - centre - normed * inner)).astype(BF16)


def finish_tokens(mine, near, far, inputs, cotangent, keep, bias):
    rows, width = inputs.shape
    step = rows // 4
    both = pl.BlockSpec((2, step, width), lambda i: (0, i, 0))
    block = pl.BlockSpec((step, width), lambda i: (i, 0))
    return pl.pallas_call(
        finish_tokens_kernel,
        grid=(4,),
        in_specs=[both] * 3
        + [block] * 2
        + [pl.BlockSpec((step, 1), lambda i: (i, 0)), pl.BlockSpec((1, width), lambda i: (0, 0))],
        out_specs=[block] * 2,
        out_shape=[shape_of((rows, width))] * 2,
        compiler_params=PARAMS,
        cost_estimate=cost(0, 12 << 20),
        name="finish_tokens",
    )(mine, near, far, inputs, cotangent, keep, bias)


def by_part(array):
    shape = array.shape
    array = array.reshape(shape[:-1] + (shape[-1] // (3 * HD), 3, HD))
    return jnp.swapaxes(array, -3, -2).reshape(shape)


def by_head(array):
    shape = array.shape
    array = array.reshape(shape[:-1] + (3, shape[-1] // (3 * HD), HD))
    return jnp.swapaxes(array, -3, -2).reshape(shape)


def gathered(weight):
    return lax.all_gather(weight, "fsdp", axis=0, tiled=True)


def folded(weight, gain, shift, offset):
    weight = gathered(weight).astype(F32)
    bias = offset[None, :] + jnp.sum(weight * shift[:, None], axis=0, keepdims=True)
    return (weight * gain[:, None]).astype(BF16), bias


def whole_rows(own, near):
    whole = jnp.stack([own, near], axis=1).astype(F32)[jnp.array([0, 2, 1, 3])]
    return whole.reshape(-1, whole.shape[-1])


def scattered(value):
    return lax.psum_scatter(value, "fsdp", scatter_dimension=0, tiled=True)


def local(
    inputs,
    segments,
    cotangent,
    attention_gain,
    attention_shift,
    feedforward_gain,
    feedforward_shift,
    project_weight,
    project_bias,
    dense_weight,
    dense_bias,
    expand_weight,
    expand_bias,
    shrink_weight,
    shrink_bias,
):
    size = lax.axis_size("fsdp")
    across = lax.axis_size("tensor")
    rows, width = inputs.shape
    assert across == 4 and 2 * rows == SEQ_LEN and segments.shape[0] == 2 * SEQ_LEN
    index = lax.axis_index("fsdp")
    rank = lax.axis_index("tensor")
    core = (rank % 2).astype(jnp.int32)[None]
    chip = rank // 2
    block = width // size
    pairs = 4
    direct = size == 2 * pairs
    place = (index if direct else index * 0).astype(jnp.int32)[None]

    own_labels = lax.dynamic_slice_in_dim(segments, rank * rows, rows, 0)
    keep = (own_labels != 0).astype(F32)[:, None]
    early = inputs
    if direct:
        first = Gather(expand_weight, size)
    packed_weights, *tables = pack(project_weight, dense_weight, shrink_weight, rotary_turns())
    if direct:
        (early,) = after((early,), packed_weights)
    own, bias_grad = prepare(early, cotangent, keep)

    small = jnp.concatenate(
        [
            attention_gain,
            attention_shift,
            feedforward_gain,
            feedforward_shift,
            dense_bias + shrink_bias,
        ]
    )
    piece = small.shape[0] // 5
    small = slots(small, rank, across)
    small_far = small + exchange(small, "tensor", across, 2)
    small = small_far + exchange(small_far, "tensor", across, 1)
    own_vectors = jnp.swapaxes(small.reshape(across, 5, piece), 0, 1).reshape(5, block)
    counts = (5 * block, project_bias.shape[0], expand_bias.shape[0])
    packed = jnp.concatenate(
        [own_vectors.reshape(-1), project_bias.astype(F32), expand_bias.astype(F32)]
    )
    packed = slots(packed, index, size)
    packed_near = packed + exchange(packed, "fsdp", size, 1)
    if direct:
        (packed_near,) = after((packed_near,), first.far, first.near, own)
    if direct:
        packed_far = packed_near + exchange(packed_near, "fsdp", size, 4)
        packed = packed_far + exchange(packed_far, "fsdp", size, 2)
    else:
        packed = sum_over(packed_near, "fsdp", size, 2)
    vectors = jnp.swapaxes(packed[:, : counts[0]].reshape(size, 5, block), 0, 1).reshape(5, width)
    project_offset = by_part(packed[:, counts[0] : counts[0] + counts[1]].reshape(-1))
    expand_offset = packed[:, counts[0] + counts[1] :].reshape(-1)

    (own,) = after((own,), small_far)

    def chip_pair(value):
        return exchange(value, "tensor", across, 1)

    def other_chip(value):
        return exchange(value, "tensor", across, 2)

    labels = segments.reshape(2, SEQ_LEN)
    labels = jnp.where(chip == 0, labels, labels[::-1])
    places = jnp.arange(SEQ_LEN, dtype=jnp.int32)[None, :]
    marks = jnp.where(labels != 0, labels, -1 - places)
    across_chip = other_chip(own)
    own_near, _ = after((own, small), packed_far) if direct else (own, small)
    partner = chip_pair(own_near)
    if direct:
        first.second_near()
        (own_block,) = after((packed_weights,), packed_near)
        rest_near = hop(own_block, size, 1)
        first.second(packed, rest_near)
        (packed_weights,) = after((packed_weights,), packed)
        rest = Gather(packed_weights, size, False)
        first.third(first.far_near)
        rest.near = rest_near
        rest.second(first.pair, first.far_near)
        expand, expand_row = join_expand(
            place,
            first.blocks(rest.far),
            vectors[2][None, :],
            vectors[3][None, :],
            expand_offset[None, :],
        )
        across_chip, expand = after((across_chip, expand), rest.far_near, rest.pair, partner)
        rest.third(expand)
    else:
        expand, expand_row = folded(expand_weight, vectors[2], vectors[3], expand_offset)
        project, project_row = folded(
            by_part(project_weight), vectors[0], vectors[1], project_offset
        )
        dense = gathered(dense_weight)
        shrink = gathered(shrink_weight)
    parts = (own, partner, across_chip, chip_pair(across_chip))

    active, slope = hidden_layer(parts, expand, expand_row)
    shrink_near, shrink_own = shrink_grads(place, active, parts, pairs)
    if direct:
        shrink_sums = Scatter(shrink_near, shrink_own, size)
        shrink, project, dense, project_row = join_rest(
            place,
            rest.blocks(shrink_own),
            vectors[0][None, :],
            vectors[1][None, :],
            project_offset[None, :],
        )
    hidden_grad, expand_near, expand_own, expand_offset_grad = unhidden_layer(
        place, parts, shrink, slope, pairs
    )
    if direct:
        expand_sums = Scatter(expand_near, expand_own, size)
        ready = shrink_sums.second(expand_own)
        (project,) = after((project,), ready)
    else:
        (project,) = after((project,), expand_own)

    def attend(sequence):
        at = slice(2 * sequence, 2 * sequence + 2)
        return attention(core, parts[at], project, project_row, dense, marks[sequence], tables)

    two = attend(1)
    weights = (dense, shrink, project, expand)
    act = active
    if direct:
        ready = shrink_sums.third(two[2])
        more = expand_sums.second(two[2])
        (act,) = after((active,), ready, more)
    far_mine, far_theirs = results(two[0], two[1], act, hidden_grad, *weights, first=2)
    far = chip_pair(far_theirs)
    far_sum = (far_mine.astype(F32) + far.astype(F32)).astype(BF16)
    far = other_chip(far_sum)
    if direct:
        ready = expand_sums.third(far_mine)
        (project,) = after((project,), ready, shrink_sums.far)
    else:
        (project,) = after((project,), far_mine)
    one = attend(0)
    if direct:
        (pair_grads,) = after((one[1],), expand_sums.far, far_sum)
        one = (one[0], pair_grads, one[2])
    both_near, both_late, both_own = attention_grads(place, parts, one[:2], two[:2], pairs)
    project_offset_grad = one[2] + two[2]
    wide = project_offset_grad.shape[1]
    units = expand_offset_grad.shape[1]
    few = dense_weight.shape[0]
    totals = jnp.concatenate([project_offset_grad, expand_offset_grad, bias_grad], axis=1)
    (totals,) = after((totals,), both_own)
    totals = totals_near = totals + exchange(totals, "fsdp", size, 1)
    if direct:
        totals = totals_pair = totals + exchange(totals, "fsdp", size, 2)
        totals = totals + exchange(totals, "fsdp", size, 4)
    else:
        totals = sum_over(totals, "fsdp", size, 2)
    project_totals = totals[:, :wide]
    expand_totals = totals[:, wide : wide + units]
    bias_totals = totals[0, wide + units :]

    act = active
    if direct:
        both_sums = Scatter(both_near, both_own, size, both_late)
        (act,) = after((active,), both_own)
    near_mine, near_theirs = results(one[0], one[1], act, hidden_grad, *weights, first=0)
    def mine(vector, count, start):
        return lax.dynamic_slice_in_dim(vector, start * count, count, 0)

    own_rows = own_vectors[:4]
    if direct:
        both_sums.second(near_mine, totals_pair)
        shrink_sum = shrink_sums.total()
        expand_gradient, expand_parts = finish_expand(
            expand_sums.terms(), expand_weight, expand_totals, own_rows
        )
        ready = both_sums.third(expand_gradient, shrink_sum)
        far, near_mine, near_theirs = after((far, near_mine, near_theirs), ready)
        near = chip_pair(near_theirs)
        output, inputs_gradient = finish_tokens(
            near_mine, near, far, inputs, cotangent, keep, vectors[4][None, :]
        )
        (project_totals,) = after((project_totals,), output)
        project_gradient, dense_sum, project_parts = finish_project(
            both_sums.terms(), project_weight, project_totals, own_rows, few
        )
        partial = [project_parts, expand_parts]
    else:
        near = chip_pair(near_theirs)
        output, inputs_gradient = finish_tokens(
            near_mine, near, far, inputs, cotangent, keep, vectors[4][None, :]
        )
        shrink_sum = scattered(whole_rows(shrink_own, shrink_near))
        expand_sum = scattered(whole_rows(expand_own, expand_near))
        both = whole_rows(both_own, jnp.concatenate([both_late, both_near]))
        project_sum = scattered(both[:, :wide])
        dense_sum = both[:, wide:].reshape(2 * pairs, 4, -1, width // 4)
        dense_sum = scattered(jnp.swapaxes(dense_sum, 1, 2).reshape(-1, width))
        columns = own_rows[:, :, None]
        project_gradient = by_head(columns[0] * project_sum + columns[1] * project_totals)
        expand_gradient = columns[2] * expand_sum + columns[3] * expand_totals
        own_project = by_part(project_weight).astype(F32)
        own_expand = expand_weight.astype(F32)
        partial = [
            jnp.sum(term, axis=1)[None, :]
            for term in (
                own_project * project_sum,
                own_project * project_totals,
                own_expand * expand_sum,
                own_expand * expand_totals,
            )
        ]
    partial = jnp.concatenate(partial + [mine(bias_totals, block, index)[None, :]])
    partial = sum_over(partial, "tensor", across)
    partial = lax.dynamic_slice_in_dim(partial, rank * piece, piece, 1)
    return (
        output,
        inputs_gradient,
        partial[0],
        partial[1],
        partial[2],
        partial[3],
        project_gradient,
        mine(by_head(project_totals[0]), project_bias.shape[0], index),
        dense_sum,
        partial[4],
        expand_gradient,
        mine(expand_totals[0], expand_bias.shape[0], index),
        shrink_sum,
        partial[4],
    )


def solution(mesh):
    in_specs = (
        P(("fsdp", "tensor"), None),
        P("fsdp"),
        P(("fsdp", "tensor"), None),
        P(("fsdp", "tensor")),
        P(("fsdp", "tensor")),
        P(("fsdp", "tensor")),
        P(("fsdp", "tensor")),
        P("fsdp", "tensor"),
        P(("tensor", "fsdp")),
        P(("tensor", "fsdp"), None),
        P(("fsdp", "tensor")),
        P("fsdp", "tensor"),
        P(("tensor", "fsdp")),
        P(("tensor", "fsdp"), None),
        P(("fsdp", "tensor")),
    )
    out_specs = (
        P(("fsdp", "tensor"), None),
        P(("fsdp", "tensor"), None),
        P(("fsdp", "tensor")),
        P(("fsdp", "tensor")),
        P(("fsdp", "tensor")),
        P(("fsdp", "tensor")),
        P("fsdp", "tensor"),
        P(("tensor", "fsdp")),
        P(("tensor", "fsdp"), None),
        P(("fsdp", "tensor")),
        P("fsdp", "tensor"),
        P(("tensor", "fsdp")),
        P(("tensor", "fsdp"), None),
        P(("fsdp", "tensor")),
    )
    return jax.shard_map(local, mesh=mesh, in_specs=in_specs, out_specs=out_specs, check_vma=False)
```

time: 914 us -> 303 us (0.33)
  waiting for transfers between devices: 288 us -> 79.3 us
  matrix products: 186 us -> 0 us
  blocking collectives: 171 us -> 0 us
  local copies, waits for them, and re-layouts: 168 us -> 18.1 us
  Pallas kernels: 0 us -> 141 us
  other arithmetic: 68.2 us -> 17.9 us
  starting transfers between devices: 0.99 us -> 40.4 us
  between operations: 17.2 us -> 1.36 us
    reduce_scatter x7 -> x0, waiting for transfers between devices: 286 us -> none  [the longest x1 92.5 us: local(): lax.psum_scatter(expand_grad, 'fsdp', scatter_dimension=0, tiled=True)]
    dot_general x40 -> x0, matrix products: 186 us -> none  [the longest x4 44.1 us: contract_columns(): lax.dot_general(left, right, (((1,), (1,)), ((), ())), preferred_element_...]
    pallas_call x0 -> x15, Pallas kernels: none -> 141 us  [the longest x2 45.4 us: attention(): pl.pallas_call(attention_kernel, in_specs=[SMEM] + [VMEM] * 9, out_specs=...]
    unnamed x4 -> x0, blocking collectives: 121 us -> none
    dynamic_update_slice x12 -> x0, local copies, waits for them, and re-layouts: 115 us -> none  [local(): lax.map(attend_back, (shaped(query), shaped(keys), shaped(values), labels...]
    ppermute x0 -> x36, waiting for transfers between devices: none -> 79.3 us  [exchange(): return lax.ppermute(value, axis, [(i, i ^ offset) for i in range(size)])]
    all_gather x2 -> x0, blocking collectives: 49.7 us -> none  [the longest x1 33.6 us: local(): lax.all_gather(dense_weight, 'fsdp', axis=0, tiled=True)]
    ppermute x0 -> x36, starting transfers between devices: none -> 40.4 us  [exchange(): return lax.ppermute(value, axis, [(i, i ^ offset) for i in range(size)])]
  transfers between devices with their start and end apart: 13 -> 36, of which waited for: 4 -> 19; matrix products, arithmetic and copies ran while one was open for 46% -> 10% of each run, Pallas kernels for 0% -> 46%
where the time goes in v2:
time: 303 us; the launch traced here: 298 us
  Pallas kernels  141 us (47%)
  waiting for transfers between devices  79.3 us (26%)
  starting transfers between devices  40.4 us (13%)
  local copies, waits for them, and re-layouts  18.1 us (6%)
  other arithmetic  17.9 us (6%)
    ppermute x36, waiting for transfers between devices, exchange(): return lax.ppermute(value, axis, [(i, i ^ offset) for i in range(size)])  79.3 us
    pallas_call x2, Pallas kernels, attention(): pl.pallas_call(attention_kernel, in_specs=[SMEM] + [VMEM] * 9, out_specs=...  45.4 us
    ppermute x36, starting transfers between devices, exchange(): return lax.ppermute(value, axis, [(i, i ^ offset) for i in range(size)])  40.4 us
    pallas_call x2, Pallas kernels, results(): pl.pallas_call(functools.partial(results_kernel, first=first), in_specs=[...  21.8 us
    pallas_call x1, Pallas kernels, unhidden_layer(): pl.pallas_call(unhidden_kernel, in_specs=[SMEM] + [ANY] * 6, out_specs=[A...  14.7 us
    pallas_call x1, Pallas kernels, hidden_layer(): pl.pallas_call(hidden_kernel, in_specs=[ANY] * 5 + [VMEM], out_specs=[ANY...  11.9 us
    pallas_call x1, Pallas kernels, shrink_grads(): pl.pallas_call(shrink_grads_kernel, grid_spec=pltpu.PrefetchScalarGridSpe...  9.83 us
    pallas_call x1, Pallas kernels, attention_grads(): pl.pallas_call(attention_grads_kernel, in_specs=[SMEM] + [ANY] * 8, out_s...  9.35 us
  transfers between devices with their start and end apart: 36, of which 19 were waited for; matrix products, arithmetic and copies ran while one was open for 10% of the time, Pallas kernels for 46%

profile of v2, /device:TPU:0, one launch (start us, length us, event | category | flops | bytes accessed | tf_op | source)
XLA Modules:
  0.0 297.9 jit_solution(8090421548255049971)
XLA Ops:
  0.6 4.1 %collective-permute-start.3 = (bf16[128,1024]{1,0:T(8,128)(2,1)}, bf16[128,1024]{1,0:T(8,128)(2,1)S(1)}, u32[]{:S(2)}, u32[]{:S(2)}) collective-permute-start(bf16[128,1024]{1,0:T(8,128)(2,1)} %w_ref.2), channel_id=1, source_target_pairs={{0,16},{4,20},{8,24},{12,28},{16,0},{20,4},{24,8},{28,12},{1,17},{... | collective-permute-start | bytes 786440 | tf_op jit(solution)/shard_map/ppermute | solution.py:773
  19.4 3.8 %prepare.1 = (bf16[2,512,1024]{2,1,0:T(8,128)(2,1)}, f32[1,1024]{1,0:T(1,128)}) custom-call(bf16[512,1024]{1,0:T(8,128)(2,1)} %inputs_ref.2, bf16[512,1024]{1,0:T(8,128)(2,1)} %cotangent_ref.3, f32[512,1]{1,0:T(8,128)} %copy.41.keep_ref), custom_call_target="tpu_custom_call" | custom-call | bytes 6291456 | tf_op jit(solution)/shard_map/prepare/pallas_call | solution.py:198
  34.0 3.5 %collective-permute-done.9.refs_1_ = bf16[2,128,1024]{2,1,0:T(8,128)(2,1)S(1)} collective-permute-done((bf16[2,128,1024]{2,1,0:T(8,128)(2,1)S(1)}, bf16[2,128,1024]{2,1,0:T(8,128)(2,1)S(1)}, u32[]{:S(2)}, u32[]{:S(2)}) %collective-permute-start.9) | collective-permute-done | bytes 524320 | tf_op jit(solution)/shard_map/ppermute | solution.py:773
  40.7 5.9 %collective-permute-done.4.refs_3_ = bf16[128,1024]{1,0:T(8,128)(2,1)S(1)} collective-permute-done((bf16[128,1024]{1,0:T(8,128)(2,1)S(1)}, bf16[128,1024]{1,0:T(8,128)(2,1)S(1)}, u32[]{:S(2)}, u32[]{:S(2)}) %collective-permute-start.4) | collective-permute-done | bytes 262176 | tf_op jit(solution)/shard_map/ppermute | solution.py:773
  46.6 13.1 %collective-permute-done.12.refs_2_ = bf16[2,128,1024]{2,1,0:T(8,128)(2,1)S(1)} collective-permute-done((bf16[2,128,1024]{2,1,0:T(8,128)(2,1)S(1)}, bf16[2,128,1024]{2,1,0:T(8,128)(2,1)S(1)}, u32[]{:S(2)}, u32[]{:S(2)}) %collective-permute-start.12) | collective-permute-done | bytes 524320 | tf_op jit(solution)/shard_map/ppermute | solution.py:773
  64.9 11.6 %collective-permute-done.11.refs_5_ = bf16[2,128,1024]{2,1,0:T(8,128)(2,1)S(1)} collective-permute-done((bf16[2,128,1024]{2,1,0:T(8,128)(2,1)S(1)}, bf16[2,128,1024]{2,1,0:T(8,128)(2,1)S(1)}, u32[]{:S(2)}, u32[]{:S(2)}) %collective-permute-start.11) | collective-permute-done | bytes 524320 | tf_op jit(solution)/shard_map/ppermute | solution.py:773
  77.3 3.6 %join_expand.1 = (bf16[1024,1024]{1,0:T(8,128)(2,1)}, f32[1,1024]{1,0:T(1,128)}) custom-call(s32[1]{0:T(128)} %bitcast.2.place_ref, bf16[128,1024]{1,0:T(8,128)(2,1)} %w_ref.2, bf16[128,1024]{1,0:T(8,128)(2,1)} %copy-done.28, bf16[128,1024]{1,0:T(8,128)(2,1)} %copy-done.16, bf16[128,1024]{1,0:T(8,128)(2,1)} %copy-done.29, bf16[2,128,1024]{2,1,0:T(8,128)(2,1)} %copy-done.26, ...), custom_call_target="tpu_custom_call" | custom-call | flops 1000000000 | bytes 6291456 | tf_op jit(solution)/shard_map/join_expand/pallas_call | solution.py:173
  80.9 4.5 %collective-permute-done.13.refs_3_ = bf16[2,128,1024]{2,1,0:T(8,128)(2,1)S(1)} collective-permute-done((bf16[2,128,1024]{2,1,0:T(8,128)(2,1)S(1)}, bf16[2,128,1024]{2,1,0:T(8,128)(2,1)S(1)}, u32[]{:S(2)}, u32[]{:S(2)}) %collective-permute-start.13) | collective-permute-done | bytes 524320 | tf_op jit(solution)/shard_map/ppermute | solution.py:773
  90.7 11.9 %hidden.1 = (bf16[2048,1024]{1,0:T(8,128)(2,1)}, bf16[2048,1024]{1,0:T(8,128)(2,1)}) custom-call(bf16[2,512,1024]{2,1,0:T(8,128)(2,1)} %get-tuple-element.121.a_ref.first_ref, bf16[2,512,1024]{2,1,0:T(8,128)(2,1)} %collective-permute-done.15.b_ref.second_ref, bf16[2,512,1024]{2,1,0:T(8,128)(2,1)} %collective-permute-done.1.c_ref.first_ref, ...), custom_call_target="tpu_custom_call" | custom-call | flops 6000000000 | bytes 14680064 | tf_op jit(solution)/shard_map/hidden/pallas_call | solution.py:463
  102.6 9.8 %shrink_grads.1 = (bf16[4,128,1024]{2,1,0:T(8,128)(2,1)}, bf16[4,128,1024]{2,1,0:T(8,128)(2,1)}) custom-call(s32[1]{0:T(128)} %bitcast.2.place_ref, bf16[2048,1024]{1,0:T(8,128)(2,1)} %get-tuple-element.166.act_ref, bf16[2,512,1024]{2,1,0:T(8,128)(2,1)} %get-tuple-element.121.a_ref.first_ref, bf16[2,512,1024]{2,1,0:T(8,128)(2,1)} %collective-permute-done.15.b_ref.second_ref, ...), custom_call_target="tpu_custom_call" | custom-call | flops 6000000000 | bytes 10485760 | tf_op jit(solution)/shard_map/shrink_grads/pallas_call | solution.py:499
  116.4 4.9 %join_rest.1 = (bf16[1024,1024]{1,0:T(8,128)(2,1)}, bf16[1024,768]{1,0:T(8,128)(2,1)}, bf16[256,1024]{1,0:T(8,128)(2,1)}, f32[1,768]{1,0:T(1,128)}) custom-call(s32[1]{0:T(128)} %bitcast.2.place_ref, bf16[2,128,1024]{2,1,0:T(8,128)(2,1)} %get-tuple-element.128.refs_0_, bf16[2,128,1024]{2,1,0:T(8,128)(2,1)} %copy-done.12, bf16[2,128,1024]{2,1,0:T(8,128)(2,1)} %copy-done.3, ...), custom_call_target="tpu_custom_call" | custom-call | flops 1000000000 | bytes 10485760 | tf_op jit(solution)/shard_map/join_rest/pallas_call | solution.py:145
  121.3 14.7 %unhidden.1 = (bf16[2048,1024]{1,0:T(8,128)(2,1)}, bf16[4,128,1024]{2,1,0:T(8,128)(2,1)}, bf16[4,128,1024]{2,1,0:T(8,128)(2,1)}, f32[1,1024]{1,0:T(1,128)}) custom-call(s32[1]{0:T(128)} %bitcast.2.place_ref, bf16[2,512,1024]{2,1,0:T(8,128)(2,1)} %get-tuple-element.121.a_ref.first_ref, bf16[2,512,1024]{2,1,0:T(8,128)(2,1)} %collective-permute-done.15.b_ref.second_ref, ...), custom_call_target="tpu_custom_call" | custom-call | flops 12000000000 | bytes 23068672 | tf_op jit(solution)/shard_map/unhidden/pallas_call | solution.py:592
  137.7 3.5 %collective-permute-done.18 = bf16[4,128,1024]{2,1,0:T(8,128)(2,1)S(1)} collective-permute-done((bf16[4,128,1024]{2,1,0:T(8,128)(2,1)}, bf16[4,128,1024]{2,1,0:T(8,128)(2,1)S(1)}, u32[]{:S(2)}, u32[]{:S(2)}) %collective-permute-start.18) | collective-permute-done | bytes 1048608 | tf_op jit(solution)/shard_map/ppermute | solution.py:773
  144.0 22.5 %attention.2 = (bf16[2,512,256]{2,1,0:T(8,128)(2,1)}, bf16[2,512,768]{2,1,0:T(8,128)(2,1)}, f32[1,768]{1,0:T(1,128)}) custom-call(s32[1]{0:T(128)} %bitcast.core_ref, bf16[2,512,1024]{2,1,0:T(8,128)(2,1)} %collective-permute-done.1.c_ref.first_ref, bf16[2,512,1024]{2,1,0:T(8,128)(2,1)} %collective-permute-done.16.d_ref.second_ref, ...), custom_call_target="tpu_custom_call" | custom-call | flops 23000000512 | bytes 8388608 | tf_op jit(solution)/shard_map/attention/pallas_call | solution.py:361
  170.8 11.0 %results.2 = (bf16[2,512,1024]{2,1,0:T(8,128)(2,1)}, bf16[2,512,1024]{2,1,0:T(8,128)(2,1)}) custom-call(bf16[2,512,256]{2,1,0:T(8,128)(2,1)} %get-tuple-element.142.mixed_ref.mixed_two_ref, bf16[2,512,768]{2,1,0:T(8,128)(2,1)} %get-tuple-element.143.pg_ref.pg_two_ref, bf16[2048,1024]{1,0:T(8,128)(2,1)} %get-tuple-element.166.act_ref, ...), custom_call_target="tpu_custom_call" | custom-call | flops 8000000000 | bytes 16777216 | tf_op jit(solution)/shard_map/results/pallas_call | solution.py:756
  185.1 22.9 %attention.3 = (bf16[2,512,256]{2,1,0:T(8,128)(2,1)}, bf16[2,512,768]{2,1,0:T(8,128)(2,1)}, f32[1,768]{1,0:T(1,128)}) custom-call(s32[1]{0:T(128)} %bitcast.core_ref, bf16[2,512,1024]{2,1,0:T(8,128)(2,1)} %get-tuple-element.121.a_ref.first_ref, bf16[2,512,1024]{2,1,0:T(8,128)(2,1)} %collective-permute-done.15.b_ref.second_ref, ...), custom_call_target="tpu_custom_call" | custom-call | flops 23000000512 | bytes 8388608 | tf_op jit(solution)/shard_map/attention/pallas_call | solution.py:361
  213.5 9.4 %attention_grads.1 = (bf16[2,128,1024]{2,1,0:T(8,128)(2,1)}, bf16[2,128,1024]{2,1,0:T(8,128)(2,1)}, bf16[4,128,1024]{2,1,0:T(8,128)(2,1)}) custom-call(s32[1]{0:T(128)} %bitcast.2.place_ref, bf16[2,512,1024]{2,1,0:T(8,128)(2,1)} %get-tuple-element.121.a_ref.first_ref, bf16[2,512,1024]{2,1,0:T(8,128)(2,1)} %collective-permute-done.15.b_ref.second_ref, ...), custom_call_target="tpu_custom_call" | custom-call | flops 7000000000 | bytes 16777216 | tf_op jit(solution)/shard_map/attention_grads/pallas_call | solution.py:675
  229.2 10.8 %results.3 = (bf16[2,512,1024]{2,1,0:T(8,128)(2,1)}, bf16[2,512,1024]{2,1,0:T(8,128)(2,1)}) custom-call(bf16[2,512,256]{2,1,0:T(8,128)(2,1)} %get-tuple-element.161.mixed_one_ref.mixed_ref, bf16[2,512,768]{2,1,0:T(8,128)(2,1)} %get-tuple-element.164.pg_one_ref.pg_ref, bf16[2048,1024]{1,0:T(8,128)(2,1)} %get-tuple-element.166.act_ref, ...), custom_call_target="tpu_custom_call" | custom-call | flops 8000000000 | bytes 16777216 | tf_op jit(solution)/shard_map/results/pallas_call | solution.py:756
  240.1 9.5 %collective-permute-done.27.late_ref = bf16[2,128,1024]{2,1,0:T(8,128)(2,1)S(1)} collective-permute-done((bf16[2,128,1024]{2,1,0:T(8,128)(2,1)}, bf16[2,128,1024]{2,1,0:T(8,128)(2,1)S(1)}, u32[]{:S(2)}, u32[]{:S(2)}) %collective-permute-start.27) | collective-permute-done | bytes 524320 | tf_op jit(solution)/shard_map/ppermute | solution.py:773
  257.4 7.9 %collective-permute-done.31 = f32[1,2816]{1,0:T(1,128)S(1)} collective-permute-done((f32[1,2816]{1,0:T(1,128)S(1)}, f32[1,2816]{1,0:T(1,128)S(1)}, u32[]{:S(2)}, u32[]{:S(2)}) %collective-permute-start.31) | collective-permute-done | bytes 11296 | tf_op jit(solution)/shard_map/ppermute | solution.py:773
  269.6 3.4 %collective-permute-start.33 = (bf16[128,1024]{1,0:T(8,128)(2,1)S(1)}, bf16[128,1024]{1,0:T(8,128)(2,1)S(1)}, u32[]{:S(2)}, u32[]{:S(2)}) collective-permute-start(bf16[128,1024]{1,0:T(8,128)(2,1)S(1)} %fusion.2), channel_id=1, source_target_pairs={{0,16},{4,20},{8,24},{12,28},{16,0},{20,4},{24,8},{28,12},{1,17},{... | collective-permute-start | bytes 786440 | tf_op jit(solution)/shard_map/ppermute | solution.py:773
  274.9 5.9 %finish_tokens.1 = (bf16[512,1024]{1,0:T(8,128)(2,1)}, bf16[512,1024]{1,0:T(8,128)(2,1)}) custom-call(bf16[2,512,1024]{2,1,0:T(8,128)(2,1)} %get-tuple-element.179.mine_ref, bf16[2,512,1024]{2,1,0:T(8,128)(2,1)} %copy-done.4, bf16[2,512,1024]{2,1,0:T(8,128)(2,1)} %collective-permute-done.22.far_ref, bf16[512,1024]{1,0:T(8,128)(2,1)} %inputs_ref.2, ...), custom_call_target="tpu_custom_call" | custom-call | bytes 12582912 | tf_op jit(solution)/shard_map/finish_tokens/pallas_call | solution.py:958
  280.9 4.7 %collective-permute-done.33.far_ref = bf16[128,1024]{1,0:T(8,128)(2,1)S(1)} collective-permute-done((bf16[128,1024]{1,0:T(8,128)(2,1)S(1)}, bf16[128,1024]{1,0:T(8,128)(2,1)S(1)}, u32[]{:S(2)}, u32[]{:S(2)}) %collective-permute-start.33) | collective-permute-done | bytes 262176 | tf_op jit(solution)/shard_map/ppermute | solution.py:773
  286.3 4.2 %finish_project.1 = (f32[128,768]{1,0:T(8,128)}, f32[32,1024]{1,0:T(8,128)}, f32[2,128]{1,0:T(2,128)}) custom-call(bf16[4,128,1024]{2,1,0:T(8,128)(2,1)} %get-tuple-element.165.own_ref, bf16[2,128,1024]{2,1,0:T(8,128)(2,1)} %copy-done.7, bf16[2,128,1024]{2,1,0:T(8,128)(2,1)} %collective-permute-done.30.pair_ref, bf16[128,1024]{1,0:T(8,128)(2,1)} %copy-done.15, ...), custom_call_target="tpu_custom_call" | custom-call | bytes 4194304 | tf_op jit(solution)/shard_map/finish_project/pallas_call | solution.py:893
  (197 shorter events, 89.4 us)
Async XLA Ops:
  0.6 22.7 %collective-permute-start.3 = (bf16[128,1024]{1,0:T(8,128)(2,1)}, bf16[128,1024]{1,0:T(8,128)(2,1)S(1)}, u32[]{:S(2)}, u32[]{:S(2)}) collective-permute-start(bf16[128,1024]{1,0:T(8,128)(2,1)} %w_ref.2), channel_id=1, source_target_pairs={{0,16},{4,20},{8,24},{12,28},{16,0},{20,4},{24,8},{28,12},{1,17},{... | collective-permute-start | bytes 786440 | tf_op jit(solution)/shard_map/ppermute | solution.py:773
  4.7 18.6 %collective-permute-start.2 = (bf16[128,1024]{1,0:T(8,128)(2,1)}, bf16[128,1024]{1,0:T(8,128)(2,1)S(1)}, u32[]{:S(2)}, u32[]{:S(2)}) collective-permute-start(bf16[128,1024]{1,0:T(8,128)(2,1)} %w_ref.2), channel_id=1, source_target_pairs={{0,4},{4,0},{8,12},{12,8},{16,20},{20,16},{24,28},{28,24},{1,5},{5... | collective-permute-start | bytes 786440 | tf_op jit(solution)/shard_map/ppermute | solution.py:773
  23.4 14.1 %collective-permute-start.9 = (bf16[2,128,1024]{2,1,0:T(8,128)(2,1)S(1)}, bf16[2,128,1024]{2,1,0:T(8,128)(2,1)S(1)}, u32[]{:S(2)}, u32[]{:S(2)}) collective-permute-start(bf16[2,128,1024]{2,1,0:T(8,128)(2,1)S(1)} %copy-done.2), channel_id=1, source_target_pairs={{0,4},{4,0},{8,12},{12,8},{16,20},{20,16},{24,28},{28,24},{1,5},{5... | collective-permute-start | bytes 1572872 | tf_op jit(solution)/shard_map/ppermute | solution.py:773
  25.3 60.1 %collective-permute-start.1 = (bf16[2,512,1024]{2,1,0:T(8,128)(2,1)}, bf16[2,512,1024]{2,1,0:T(8,128)(2,1)}, u32[]{:S(2)}, u32[]{:S(2)}) collective-permute-start(bf16[2,512,1024]{2,1,0:T(8,128)(2,1)} %get-tuple-element.121.a_ref.first_ref), channel_id=1, source_target_pairs={{0,2},{1,3},{2,0},{3,1},{4,6},{5,7},{6,4},{7,5},{8,10},{9,11},{10,... | collective-permute-start | bytes 6291464 | tf_op jit(solution)/shard_map/ppermute | solution.py:773
  30.0 56.2 %collective-permute-start.15 = (bf16[2,512,1024]{2,1,0:T(8,128)(2,1)}, bf16[2,512,1024]{2,1,0:T(8,128)(2,1)}, u32[]{:S(2)}, u32[]{:S(2)}) collective-permute-start(bf16[2,512,1024]{2,1,0:T(8,128)(2,1)} %get-tuple-element.121.a_ref.first_ref), channel_id=1, source_target_pairs={{0,1},{1,0},{2,3},{3,2},{4,5},{5,4},{6,7},{7,6},{8,9},{9,8},{10,11... | collective-permute-start | bytes 6291464 | tf_op jit(solution)/shard_map/ppermute | solution.py:773
  33.9 25.8 %collective-permute-start.12 = (bf16[2,128,1024]{2,1,0:T(8,128)(2,1)S(1)}, bf16[2,128,1024]{2,1,0:T(8,128)(2,1)S(1)}, u32[]{:S(2)}, u32[]{:S(2)}) collective-permute-start(bf16[2,128,1024]{2,1,0:T(8,128)(2,1)S(1)} %copy-done.2), channel_id=1, source_target_pairs={{0,16},{4,20},{8,24},{12,28},{16,0},{20,4},{24,8},{28,12},{1,17},{... | collective-permute-start | bytes 1572872 | tf_op jit(solution)/shard_map/ppermute | solution.py:773
  37.5 23.8 %collective-permute-start.10 = (bf16[2,128,1024]{2,1,0:T(8,128)(2,1)S(1)}, bf16[2,128,1024]{2,1,0:T(8,128)(2,1)S(1)}, u32[]{:S(2)}, u32[]{:S(2)}) collective-permute-start(bf16[2,128,1024]{2,1,0:T(8,128)(2,1)S(1)} %pad_maximum_fusion.1), channel_id=1, source_target_pairs={{0,8},{4,12},{8,0},{12,4},{16,24},{20,28},{24,16},{28,20},{1,9},{5... | collective-permute-start | bytes 1572872 | tf_op jit(solution)/shard_map/ppermute | solution.py:773
  61.5 23.9 %collective-permute-start.14 = (bf16[2,2,128,1024]{3,2,1,0:T(8,128)(2,1)S(1)}, bf16[2,2,128,1024]{3,2,1,0:T(8,128)(2,1)S(1)}, u32[]{:S(2)}, u32[]{:S(2)}) collective-permute-start(bf16[2,2,128,1024]{3,2,1,0:T(8,128)(2,1)S(1)} %pad_maximum_fusion), channel_id=1, source_target_pairs={{0,8},{4,12},{8,0},{12,4},{16,24},{20,28},{24,16},{28,20},{1,9},{5... | collective-permute-start | bytes 3145736 | tf_op jit(solution)/shard_map/ppermute | solution.py:773
  61.6 14.9 %collective-permute-start.11 = (bf16[2,128,1024]{2,1,0:T(8,128)(2,1)S(1)}, bf16[2,128,1024]{2,1,0:T(8,128)(2,1)S(1)}, u32[]{:S(2)}, u32[]{:S(2)}) collective-permute-start(bf16[2,128,1024]{2,1,0:T(8,128)(2,1)S(1)} %collective-permute-done.10.refs_4_), channel_id=1, source_target_pairs={{0,4},{4,0},{8,12},{12,8},{16,20},{20,16},{24,28},{28,24},{1,5},{5... | collective-permute-start | bytes 1572872 | tf_op jit(solution)/shard_map/ppermute | solution.py:773
  63.8 21.6 %collective-permute-start.13 = (bf16[2,128,1024]{2,1,0:T(8,128)(2,1)S(1)}, bf16[2,128,1024]{2,1,0:T(8,128)(2,1)S(1)}, u32[]{:S(2)}, u32[]{:S(2)}) collective-permute-start(bf16[2,128,1024]{2,1,0:T(8,128)(2,1)S(1)} %collective-permute-done.12.refs_2_), channel_id=1, source_target_pairs={{0,4},{4,0},{8,12},{12,8},{16,20},{20,16},{24,28},{28,24},{1,5},{5... | collective-permute-start | bytes 1572872 | tf_op jit(solution)/shard_map/ppermute | solution.py:773
  88.4 25.5 %collective-permute-start.17 = (bf16[2,2,128,1024]{3,2,1,0:T(8,128)(2,1)S(1)}, bf16[2,2,128,1024]{3,2,1,0:T(8,128)(2,1)S(1)}, u32[]{:S(2)}, u32[]{:S(2)}) collective-permute-start(bf16[2,2,128,1024]{3,2,1,0:T(8,128)(2,1)S(1)} %collective-permute-done.14.refs_4_), channel_id=1, source_target_pairs={{0,4},{4,0},{8,12},{12,8},{16,20},{20,16},{24,28},{28,24},{1,5},{5... | collective-permute-start | bytes 3145736 | tf_op jit(solution)/shard_map/ppermute | solution.py:773
  114.9 26.3 %collective-permute-start.18 = (bf16[4,128,1024]{2,1,0:T(8,128)(2,1)}, bf16[4,128,1024]{2,1,0:T(8,128)(2,1)S(1)}, u32[]{:S(2)}, u32[]{:S(2)}) collective-permute-start(bf16[4,128,1024]{2,1,0:T(8,128)(2,1)} %get-tuple-element.135), channel_id=1, source_target_pairs={{0,4},{4,0},{8,12},{12,8},{16,20},{20,16},{24,28},{28,24},{1,5},{5... | collective-permute-start | bytes 3145736 | tf_op jit(solution)/shard_map/ppermute | solution.py:773
  136.0 30.5 %collective-permute-start.20 = (bf16[4,128,1024]{2,1,0:T(8,128)(2,1)}, bf16[4,128,1024]{2,1,0:T(8,128)(2,1)S(1)}, u32[]{:S(2)}, u32[]{:S(2)}) collective-permute-start(bf16[4,128,1024]{2,1,0:T(8,128)(2,1)} %get-tuple-element.151), channel_id=1, source_target_pairs={{0,4},{4,0},{8,12},{12,8},{16,20},{20,16},{24,28},{28,24},{1,5},{5... | collective-permute-start | bytes 3145736 | tf_op jit(solution)/shard_map/ppermute | solution.py:773
  142.3 24.9 %collective-permute-start.19 = (bf16[2,128,1024]{2,1,0:T(8,128)(2,1)}, bf16[2,128,1024]{2,1,0:T(8,128)(2,1)}, u32[]{:S(2)}, u32[]{:S(2)}) collective-permute-start(bf16[2,128,1024]{2,1,0:T(8,128)(2,1)} %add_convert_fusion.3), channel_id=1, source_target_pairs={{0,8},{4,12},{8,0},{12,4},{16,24},{20,28},{24,16},{28,20},{1,9},{5... | collective-permute-start | bytes 1572872 | tf_op jit(solution)/shard_map/ppermute | solution.py:773
  166.8 16.7 %collective-permute-start.23 = (bf16[2,128,1024]{2,1,0:T(8,128)(2,1)S(1)}, bf16[2,128,1024]{2,1,0:T(8,128)(2,1)S(1)}, u32[]{:S(2)}, u32[]{:S(2)}) collective-permute-start(bf16[2,128,1024]{2,1,0:T(8,128)(2,1)S(1)} %add_convert_fusion.2), channel_id=1, source_target_pairs={{0,8},{4,12},{8,0},{12,4},{16,24},{20,28},{24,16},{28,20},{1,9},{5... | collective-permute-start | bytes 1572872 | tf_op jit(solution)/shard_map/ppermute | solution.py:773
  168.4 16.6 %collective-permute-start.24 = (bf16[128,1024]{1,0:T(8,128)(2,1)S(1)}, bf16[128,1024]{1,0:T(8,128)(2,1)S(1)}, u32[]{:S(2)}, u32[]{:S(2)}) collective-permute-start(bf16[128,1024]{1,0:T(8,128)(2,1)S(1)} %fusion), channel_id=1, source_target_pairs={{0,16},{4,20},{8,24},{12,28},{16,0},{20,4},{24,8},{28,12},{1,17},{... | collective-permute-start | bytes 786440 | tf_op jit(solution)/shard_map/ppermute | solution.py:773
  184.8 28.7 %collective-permute-start.25 = (bf16[128,1024]{1,0:T(8,128)(2,1)S(1)}, bf16[128,1024]{1,0:T(8,128)(2,1)S(1)}, u32[]{:S(2)}, u32[]{:S(2)}) collective-permute-start(bf16[128,1024]{1,0:T(8,128)(2,1)S(1)} %fusion.1), channel_id=1, source_target_pairs={{0,16},{4,20},{8,24},{12,28},{16,0},{20,4},{24,8},{28,12},{1,17},{... | collective-permute-start | bytes 786440 | tf_op jit(solution)/shard_map/ppermute | solution.py:773
  185.0 23.6 %collective-permute-start.21 = (bf16[2,512,1024]{2,1,0:T(8,128)(2,1)}, bf16[2,512,1024]{2,1,0:T(8,128)(2,1)}, u32[]{:S(2)}, u32[]{:S(2)}) collective-permute-start(bf16[2,512,1024]{2,1,0:T(8,128)(2,1)} %get-tuple-element.155), channel_id=1, source_target_pairs={{0,1},{1,0},{2,3},{3,2},{4,5},{5,4},{6,7},{7,6},{8,9},{9,8},{10,11... | collective-permute-start | bytes 6291464 | tf_op jit(solution)/shard_map/ppermute | solution.py:773
  211.9 56.5 %collective-permute-start.22 = (bf16[2,512,1024]{2,1,0:T(8,128)(2,1)S(1)}, bf16[2,512,1024]{2,1,0:T(8,128)(2,1)}, u32[]{:S(2)}, u32[]{:S(2)}) collective-permute-start(bf16[2,512,1024]{2,1,0:T(8,128)(2,1)S(1)} %add_convert_fusion), channel_id=1, source_target_pairs={{0,2},{1,3},{2,0},{3,1},{4,6},{5,7},{6,4},{7,5},{8,10},{9,11},{10,... | collective-permute-start | bytes 6291464 | tf_op jit(solution)/shard_map/ppermute | solution.py:773
  224.4 15.7 %collective-permute-start.26 = (bf16[2,128,1024]{2,1,0:T(8,128)(2,1)}, bf16[2,128,1024]{2,1,0:T(8,128)(2,1)}, u32[]{:S(2)}, u32[]{:S(2)}) collective-permute-start(bf16[2,128,1024]{2,1,0:T(8,128)(2,1)} %get-tuple-element.169), channel_id=1, source_target_pairs={{0,4},{4,0},{8,12},{12,8},{16,20},{20,16},{24,28},{28,24},{1,5},{5... | collective-permute-start | bytes 1572872 | tf_op jit(solution)/shard_map/ppermute | solution.py:773
  224.9 24.7 %collective-permute-start.27 = (bf16[2,128,1024]{2,1,0:T(8,128)(2,1)}, bf16[2,128,1024]{2,1,0:T(8,128)(2,1)S(1)}, u32[]{:S(2)}, u32[]{:S(2)}) collective-permute-start(bf16[2,128,1024]{2,1,0:T(8,128)(2,1)} %get-tuple-element.170), channel_id=1, source_target_pairs={{0,4},{4,0},{8,12},{12,8},{16,20},{20,16},{24,28},{28,24},{1,5},{5... | collective-permute-start | bytes 1572872 | tf_op jit(solution)/shard_map/ppermute | solution.py:773
  226.6 13.5 %collective-permute-start.29 = (f32[1,2816]{1,0:T(1,128)S(1)}, f32[1,2816]{1,0:T(1,128)S(1)}, u32[]{:S(2)}, u32[]{:S(2)}) collective-permute-start(f32[1,2816]{1,0:T(1,128)S(1)} %add.119), channel_id=1, source_target_pairs={{0,8},{4,12},{8,0},{12,4},{16,24},{20,28},{24,16},{28,20},{1,9},{5... | collective-permute-start | bytes 33800 | tf_op jit(solution)/shard_map/ppermute | solution.py:773
  251.9 16.5 %collective-permute-start.30 = (bf16[2,128,1024]{2,1,0:T(8,128)(2,1)}, bf16[2,128,1024]{2,1,0:T(8,128)(2,1)}, u32[]{:S(2)}, u32[]{:S(2)}) collective-permute-start(bf16[2,128,1024]{2,1,0:T(8,128)(2,1)} %add_convert_fusion.1), channel_id=1, source_target_pairs={{0,8},{4,12},{8,0},{12,4},{16,24},{20,28},{24,16},{28,20},{1,9},{5... | collective-permute-start | bytes 1572872 | tf_op jit(solution)/shard_map/ppermute | solution.py:773
  269.6 16.0 %collective-permute-start.33 = (bf16[128,1024]{1,0:T(8,128)(2,1)S(1)}, bf16[128,1024]{1,0:T(8,128)(2,1)S(1)}, u32[]{:S(2)}, u32[]{:S(2)}) collective-permute-start(bf16[128,1024]{1,0:T(8,128)(2,1)S(1)} %fusion.2), channel_id=1, source_target_pairs={{0,16},{4,20},{8,24},{12,28},{16,0},{20,4},{24,8},{28,12},{1,17},{... | collective-permute-start | bytes 786440 | tf_op jit(solution)/shard_map/ppermute | solution.py:773
  (42 other events, 540.2 us)

commit v3 on v2

--- a/solution.py
+++ b/solution.py
@@ -53,20 +53,19 @@
     return made
 
 
-def pack_kernel(project_ref, dense_ref, shrink_ref, turns_ref, out_ref, cos_ref, up_ref, dn_ref):
+def pack_kernel(project_ref, dense_ref, turns_ref, out_ref, cos_ref, up_ref, dn_ref):
     heads = project_ref.shape[1] // (3 * HD)
     rows = dense_ref.shape[0]
     width = heads * HD
-    out_ref[0] = shrink_ref[...]
     for part in range(3):
         pieces = [
             project_ref[:, (3 * head + part) * HD : (3 * head + part + 1) * HD]
             for head in range(heads)
         ]
-        out_ref[1, :, part * width : (part + 1) * width] = jnp.concatenate(pieces, axis=1)
+        out_ref[:, part * width : (part + 1) * width] = jnp.concatenate(pieces, axis=1)
     for j in range(4):
         columns = slice(j * width, (j + 1) * width)
-        out_ref[1, j * rows : (j + 1) * rows, 3 * width :] = dense_ref[:, columns]
+        out_ref[j * rows : (j + 1) * rows, 3 * width :] = dense_ref[:, columns]
     half = ROT // 2
     length = turns_ref.shape[0]
     cosine, sine = turns_ref[:, :half], turns_ref[:, half:]
@@ -77,17 +76,17 @@
     dn_ref[...] = jnp.concatenate([-sine, none, rest] * 2, axis=1)
 
 
-def pack(project, dense, shrink, turns):
+def pack(project, dense, turns):
     table = shape_of((turns.shape[0], 2 * HD), F32)
     return pl.pallas_call(
         pack_kernel,
-        in_specs=[VMEM] * 4,
+        in_specs=[VMEM] * 3,
         out_specs=[VMEM] * 4,
-        out_shape=[shape_of((2,) + shrink.shape)] + [table] * 3,
+        out_shape=[shape_of((project.shape[0], dense.shape[1]))] + [table] * 3,
         compiler_params=PARAMS,
         cost_estimate=cost(0, 3 << 20),
         name="pack",
-    )(project, dense, shrink, turns)
+    )(project, dense, turns)
 
 
 def column(row):
@@ -116,16 +115,15 @@
     return [own, near, pair.at[0], pair_near.at[0], far, far_near, pair.at[1], pair_near.at[1]]
 
 
-def join_rest_kernel(place_ref, *refs):
-    gain_ref, shift_ref, offset_ref, shrink_ref, project_ref, dense_ref, bias_ref = refs[6:]
+def join_project_kernel(place_ref, *refs):
+    gain_ref, shift_ref, offset_ref, project_ref, dense_ref, bias_ref = refs[6:]
     total = offset_ref[...]
     wide = project_ref.shape[1]
     for k, ref in enumerate(block_list(refs[:6])):
-        block = ref[1]
+        block = ref[...]
         start, scaled, part = scaled_rows(
             place_ref[0], k, block[:, :wide], gain_ref, shift_ref
         )
-        shrink_ref[pl.ds(start, block.shape[0]), :] = ref[0]
         project_ref[pl.ds(start, block.shape[0]), :] = scaled
         total = total + part
         rows = block.shape[0] // 4
@@ -138,23 +136,22 @@
     bias_ref[...] = total
 
 
-def join_rest(place, blocks, gain, shift, offset):
-    _, rows, columns = blocks[0].shape
+def join_project(place, blocks, gain, shift, offset):
+    rows, columns = blocks[0].shape
     total = 8 * rows
     wide = offset.shape[1]
     return pl.pallas_call(
-        join_rest_kernel,
+        join_project_kernel,
         in_specs=[SMEM] + [VMEM] * 9,
-        out_specs=[VMEM] * 4,
+        out_specs=[VMEM] * 3,
         out_shape=[
-            shape_of((total, columns)),
             shape_of((total, wide)),
             shape_of((total // 4, columns)),
             shape_of((1, wide), F32),
         ],
         compiler_params=PARAMS,
         cost_estimate=cost(1e9, 10 << 20),
-        name="join_rest",
+        name="join_project",
     )(place, *blocks, gain, shift, offset)
 
 
@@ -179,6 +176,27 @@
         cost_estimate=cost(1e9, 6 << 20),
         name="join_expand",
     )(place, *blocks, gain, shift, offset)
+
+
+def join_kernel(place_ref, *refs):
+    out_ref = refs[6]
+    for k, ref in enumerate(block_list(refs[:6])):
+        rows = ref.shape[0]
+        start = pl.multiple_of(lax.bitwise_xor(place_ref[0], k) * rows, rows)
+        out_ref[pl.ds(start, rows), :] = ref[...]
+
+
+def join(place, blocks):
+    rows, columns = blocks[0].shape
+    return pl.pallas_call(
+        join_kernel,
+        in_specs=[SMEM] + [VMEM] * 6,
+        out_specs=VMEM,
+        out_shape=shape_of((8 * rows, columns)),
+        compiler_params=PARAMS,
+        cost_estimate=cost(0, 4 << 20),
+        name="join",
+    )(place, *blocks)
 
 
 def normalise(features):
@@ -419,7 +437,18 @@
     )
 
 
+def send_pairs(near_s, own_s, near_ref, own_ref, sems, first):
+    def copy(m):
+        return (
+            pltpu.make_async_copy(near_s.at[m], near_ref.at[m], sems.at[first + 2 * m]),
+            pltpu.make_async_copy(own_s.at[m], own_ref.at[m], sems.at[first + 2 * m + 1]),
+        )
+
+    return copy
+
+
 def hidden_kernel(
+    place_ref,
     a_ref,
     b_ref,
     c_ref,
@@ -428,16 +457,23 @@
     bias_ref,
     act_ref,
     slope_ref,
+    near_ref,
+    own_ref,
     tokens_s,
+    grads_s,
     w_s,
     act_s,
     slope_s,
+    near_s,
+    own_s,
     in_sems,
     out_sems,
 ):
     rows = a_ref.shape[1]
+    parts = (a_ref, b_ref, c_ref, d_ref)
     loads = copies([(w_ref, w_s)], in_sems)
-    loads += loaded((a_ref, b_ref, c_ref, d_ref), tokens_s, in_sems, 1, 0)
+    loads += loaded(parts, tokens_s, in_sems, 1, 0)
+    loads += loaded(parts, grads_s, in_sems, 5, 1)
     loads[0].wait()
     stores = []
     for p in range(4):
@@ -453,75 +489,43 @@
             out_sems,
             2 * p,
         )
+    for copy in loads[5:]:
+        copy.wait()
+    count, block, _ = near_ref.shape
+    send = send_pairs(near_s, own_s, near_ref, own_ref, out_sems, 8)
+
+    def one_pair(m, carry):
+        product = tn(act_s[:, pair_rows(place_ref, m, 2 * block)], grads_s[...])
+        put_pair(place_ref, m, product, near_s, own_s)
+        for copy in send(m):
+            copy.start()
+        return carry
+
+    lax.fori_loop(0, count, one_pair, 0)
+    for m in range(count):
+        stores += send(m)
     for copy in stores:
         copy.wait()
 
 
-def hidden_layer(parts, w, bias):
+def hidden_layer(place, parts, w, bias, pairs):
     _, rows, width = parts[0].shape
     units = w.shape[1]
+    blocks = (pairs, units // (2 * pairs), width)
     return pl.pallas_call(
         hidden_kernel,
-        in_specs=[ANY] * 5 + [VMEM],
-        out_specs=[ANY] * 2,
-        out_shape=[shape_of((4 * rows, units))] * 2,
-        scratch_shapes=[pltpu.VMEM((4 * rows, width), BF16), pltpu.VMEM(w.shape, BF16)]
+        in_specs=[SMEM] + [ANY] * 5 + [VMEM],
+        out_specs=[ANY] * 4,
+        out_shape=[shape_of((4 * rows, units))] * 2 + [shape_of(blocks)] * 2,
+        scratch_shapes=[pltpu.VMEM((4 * rows, width), BF16)] * 2
+        + [pltpu.VMEM(w.shape, BF16)]
         + [pltpu.VMEM((4 * rows, units), BF16)] * 2
-        + [pltpu.SemaphoreType.DMA((5,)), pltpu.SemaphoreType.DMA((8,))],
+        + [pltpu.VMEM(blocks, BF16)] * 2
+        + [pltpu.SemaphoreType.DMA((9,)), pltpu.SemaphoreType.DMA((8 + 2 * pairs,))],
         compiler_params=PARAMS,
-        cost_estimate=cost(6e9, 14 << 20),
+        cost_estimate=cost(1.2e10, 20 << 20),
         name="hidden",
-    )(*parts, w, bias)
-
-
-def shrink_grads_kernel(
-    place_ref, act_ref, a_ref, b_ref, c_ref, d_ref, near_ref, own_ref, grads_s, in_sems
-):
-    m = pl.program_id(0)
-
-    @pl.when(m == 0)
-    def _():
-        for copy in loaded((a_ref, b_ref, c_ref, d_ref), grads_s, in_sems, 0, 1):
-            copy.wait()
-
-    product = tn(act_ref[...], grads_s[...])
-    rows = product.shape[0] // 2
-    low, high = product[:rows], product[rows:]
-    swap = (place_ref[0] & 1) == 1
-    own_ref[...] = jnp.where(swap, high, low).astype(BF16)
-    near_ref[...] = jnp.where(swap, low, high).astype(BF16)
-
-
-def shrink_grads(place, active, parts, pairs):
-    _, rows, width = parts[0].shape
-    units = active.shape[1]
-    block = units // (2 * pairs)
-    return pl.pallas_call(
-        shrink_grads_kernel,
-        grid_spec=pltpu.PrefetchScalarGridSpec(
-            num_scalar_prefetch=1,
-            grid=(pairs,),
-            in_specs=[
-                pl.BlockSpec(
-                    (4 * rows, 2 * block),
-                    lambda m, place: (
-                        0,
-                        lax.bitwise_xor(lax.shift_right_logical(place[0], 1), turn(m)),
-                    ),
-                )
-            ]
-            + [ANY] * 4,
-            out_specs=[pl.BlockSpec((None, block, width), lambda m, place: (m, 0, 0))] * 2,
-            scratch_shapes=[
-                pltpu.VMEM((4 * rows, width), BF16),
-                pltpu.SemaphoreType.DMA((4,)),
-            ],
-        ),
-        out_shape=[shape_of((pairs, block, width))] * 2,
-        compiler_params=PARAMS,
-        cost_estimate=cost(6e9, 10 << 20),
-        name="shrink_grads",
-    )(place, active, *parts)
+    )(place, *parts, w, bias)
 
 
 def unhidden_kernel(
@@ -830,7 +834,7 @@
             self.arrived = self.near
 
     def second(self, *first):
-        near, own = after((self.near, self.own[2:]), self.late, *first)
+        near, own = after((self.near, self.own[2:]), *first)
         self.pair = hop((own.astype(F32) + near.astype(F32)).astype(BF16), self.size, 2)
         return self.arrived
 
@@ -1035,7 +1039,7 @@
     early = inputs
     if direct:
         first = Gather(expand_weight, size)
-    packed_weights, *tables = pack(project_weight, dense_weight, shrink_weight, rotary_turns())
+    packed_weights, *tables = pack(project_weight, dense_weight, rotary_turns())
     if direct:
         (early,) = after((early,), packed_weights)
     own, bias_grad = prepare(early, cotangent, keep)
@@ -1088,23 +1092,28 @@
     partner = chip_pair(own_near)
     if direct:
         first.second_near()
-        (own_block,) = after((packed_weights,), packed_near)
-        rest_near = hop(own_block, size, 1)
-        first.second(packed, rest_near)
-        (packed_weights,) = after((packed_weights,), packed)
-        rest = Gather(packed_weights, size, False)
-        first.third(first.far_near)
-        rest.near = rest_near
-        rest.second(first.pair, first.far_near)
+        (near_block,) = after((shrink_weight,), packed_near)
+        near_block = hop(near_block, size, 1)
+        first.second(packed)
+        (far_block,) = after((shrink_weight,), packed)
+        second = Gather(far_block, size, False)
+        second.near = near_block
+        second.second(first.pair, first.far_near)
+        (far_block,) = after((packed_weights,), second.far)
+        third = Gather(far_block, size, False)
+        first.third(first.far_near, near_block)
         expand, expand_row = join_expand(
             place,
-            first.blocks(rest.far),
+            first.blocks(),
             vectors[2][None, :],
             vectors[3][None, :],
             expand_offset[None, :],
         )
-        across_chip, expand = after((across_chip, expand), rest.far_near, rest.pair, partner)
-        rest.third(expand)
+        across_chip, expand = after(
+            (across_chip, expand), second.far_near, second.pair, third.far, partner
+        )
+        second.third(expand)
+        third.second(second.pair)
     else:
         expand, expand_row = folded(expand_weight, vectors[2], vectors[3], expand_offset)
         project, project_row = folded(
@@ -1114,24 +1123,25 @@
         shrink = gathered(shrink_weight)
     parts = (own, partner, across_chip, chip_pair(across_chip))
 
-    active, slope = hidden_layer(parts, expand, expand_row)
-    shrink_near, shrink_own = shrink_grads(place, active, parts, pairs)
+    active, slope, shrink_near, shrink_own = hidden_layer(place, parts, expand, expand_row, pairs)
     if direct:
         shrink_sums = Scatter(shrink_near, shrink_own, size)
-        shrink, project, dense, project_row = join_rest(
-            place,
-            rest.blocks(shrink_own),
-            vectors[0][None, :],
-            vectors[1][None, :],
-            project_offset[None, :],
-        )
+        (near_block,) = after((packed_weights,), shrink_own)
+        third.near = hop(near_block, size, 1)
+        third.third(shrink_own)
+        shrink = join(place, second.blocks(shrink_own))
     hidden_grad, expand_near, expand_own, expand_offset_grad = unhidden_layer(
         place, parts, shrink, slope, pairs
     )
     if direct:
         expand_sums = Scatter(expand_near, expand_own, size)
-        ready = shrink_sums.second(expand_own)
-        (project,) = after((project,), ready)
+        project, dense, project_row = join_project(
+            place,
+            third.blocks(expand_own),
+            vectors[0][None, :],
+            vectors[1][None, :],
+            project_offset[None, :],
+        )
     else:
         (project,) = after((project,), expand_own)
 
@@ -1143,21 +1153,22 @@
     weights = (dense, shrink, project, expand)
     act = active
     if direct:
-        ready = shrink_sums.third(two[2])
-        more = expand_sums.second(two[2])
-        (act,) = after((active,), ready, more)
+        ready = shrink_sums.second(two[2])
+        (act,) = after((active,), ready)
     far_mine, far_theirs = results(two[0], two[1], act, hidden_grad, *weights, first=2)
     far = chip_pair(far_theirs)
     far_sum = (far_mine.astype(F32) + far.astype(F32)).astype(BF16)
     far = other_chip(far_sum)
     if direct:
-        ready = expand_sums.third(far_mine)
-        (project,) = after((project,), ready, shrink_sums.far)
+        ready = shrink_sums.third(far_mine)
+        more = expand_sums.second(far_mine)
+        (project,) = after((project,), ready, more)
     else:
         (project,) = after((project,), far_mine)
     one = attend(0)
     if direct:
-        (pair_grads,) = after((one[1],), expand_sums.far, far_sum)
+        ready = expand_sums.third(one[2])
+        (pair_grads,) = after((one[1],), ready, shrink_sums.far, far_sum)
         one = (one[0], pair_grads, one[2])
     both_near, both_late, both_own = attention_grads(place, parts, one[:2], two[:2], pairs)
     project_offset_grad = one[2] + two[2]
@@ -1179,7 +1190,7 @@
     act = active
     if direct:
         both_sums = Scatter(both_near, both_own, size, both_late)
-        (act,) = after((active,), both_own)
+        (act,) = after((active,), both_own, expand_sums.far)
     near_mine, near_theirs = results(one[0], one[1], act, hidden_grad, *weights, first=0)
     def mine(vector, count, start):
         return lax.dynamic_slice_in_dim(vector, start * count, count, 0)
@@ -1188,16 +1199,17 @@
     if direct:
         both_sums.second(near_mine, totals_pair)
         shrink_sum = shrink_sums.total()
+        ready = both_sums.third(shrink_sum)
+        (expand_totals,) = after((expand_totals,), ready)
         expand_gradient, expand_parts = finish_expand(
             expand_sums.terms(), expand_weight, expand_totals, own_rows
         )
-        ready = both_sums.third(expand_gradient, shrink_sum)
         far, near_mine, near_theirs = after((far, near_mine, near_theirs), ready)
         near = chip_pair(near_theirs)
         output, inputs_gradient = finish_tokens(
             near_mine, near, far, inputs, cotangent, keep, vectors[4][None, :]
         )
-        (project_totals,) = after((project_totals,), output)
+        (project_totals,) = after((project_totals,), output, expand_parts)
         project_gradient, dense_sum, project_parts = finish_project(
             both_sums.terms(), project_weight, project_totals, own_rows, few
         )

time: 303 us -> 280 us (0.924)
  waiting for transfers between devices: 79.3 us -> 57.7 us
  starting transfers between devices: 40.4 us -> 45.2 us
  Pallas kernels: 141 us -> 137 us
    ppermute x36 -> x41, waiting for transfers between devices: 79.3 us -> 57.7 us  [exchange(): return lax.ppermute(value, axis, [(i, i ^ offset) for i in range(size)])]
    ppermute x36 -> x41, starting transfers between devices: 40.4 us -> 45.2 us  [exchange(): return lax.ppermute(value, axis, [(i, i ^ offset) for i in range(size)])]
    pallas_call x4, Pallas kernels: 29.7 us -> 26.2 us  [the longest x1 16.7 us: hidden_layer(): pl.pallas_call(hidden_kernel, in_specs=[SMEM] + [ANY] * 5 + [VMEM], out_s...]
  transfers between devices with their start and end apart: 36 -> 41, of which waited for: 19 -> 19; matrix products, arithmetic and copies ran while one was open for 10% -> 10% of each run, Pallas kernels for 46% -> 48%
where the time goes in v3:
time: 280 us; the launch traced here: 276 us
  Pallas kernels  137 us (49%)
  waiting for transfers between devices  57.7 us (21%)
  starting transfers between devices  45.2 us (16%)
  other arithmetic  17.6 us (6%)
  local copies, waits for them, and re-layouts  16.3 us (6%)
    ppermute x41, waiting for transfers between devices, exchange(): return lax.ppermute(value, axis, [(i, i ^ offset) for i in range(size)])  57.7 us
    pallas_call x2, Pallas kernels, attention(): pl.pallas_call(attention_kernel, in_specs=[SMEM] + [VMEM] * 9, out_specs=...  45.4 us
    ppermute x41, starting transfers between devices, exchange(): return lax.ppermute(value, axis, [(i, i ^ offset) for i in range(size)])  45.2 us
    pallas_call x2, Pallas kernels, results(): pl.pallas_call(functools.partial(results_kernel, first=first), in_specs=[...  21.9 us
    pallas_call x1, Pallas kernels, hidden_layer(): pl.pallas_call(hidden_kernel, in_specs=[SMEM] + [ANY] * 5 + [VMEM], out_s...  16.7 us
    pallas_call x1, Pallas kernels, unhidden_layer(): pl.pallas_call(unhidden_kernel, in_specs=[SMEM] + [ANY] * 6, out_specs=[A...  14.7 us
    pallas_call x1, Pallas kernels, attention_grads(): pl.pallas_call(attention_grads_kernel, in_specs=[SMEM] + [ANY] * 8, out_s...  9.34 us
    pallas_call x1, Pallas kernels, finish_tokens(): pl.pallas_call(finish_tokens_kernel, grid=(4,), in_specs=[both] * 3 + [bl...  5.94 us
  transfers between devices with their start and end apart: 41, of which 19 were waited for; matrix products, arithmetic and copies ran while one was open for 10% of the time, Pallas kernels for 48%

profile of v3, /device:TPU:0, one launch (start us, length us, event | category | flops | bytes accessed | tf_op | source)
XLA Modules:
  0.0 275.6 jit_solution(2574667187646260176)
XLA Ops:
  0.6 4.1 %collective-permute-start.3 = (bf16[128,1024]{1,0:T(8,128)(2,1)}, bf16[128,1024]{1,0:T(8,128)(2,1)S(1)}, u32[]{:S(2)}, u32[]{:S(2)}) collective-permute-start(bf16[128,1024]{1,0:T(8,128)(2,1)} %w_ref.2), channel_id=1, source_target_pairs={{0,16},{4,20},{8,24},{12,28},{16,0},{20,4},{24,8},{28,12},{1,17},{... | collective-permute-start | bytes 786440 | tf_op jit(solution)/shard_map/ppermute | solution.py:777
  16.3 3.0 %pack.1 = (bf16[128,1024]{1,0:T(8,128)(2,1)}, f32[1024,128]{1,0:T(8,128)}, f32[1024,128]{1,0:T(8,128)}, f32[1024,128]{1,0:T(8,128)}) custom-call(bf16[128,768]{1,0:T(8,128)(2,1)} %w_ref.3, bf16[32,1024]{1,0:T(8,128)(2,1)} %dense_ref.1, f32[1024,16]{1,0:T(8,128)} %copy.40.turns_ref), custom_call_target="tpu_custom_call" | custom-call | bytes 3145728 | tf_op jit(solution)/shard_map/pack/pallas_call | solution.py:81
  19.3 3.8 %prepare.1 = (bf16[2,512,1024]{2,1,0:T(8,128)(2,1)}, f32[1,1024]{1,0:T(1,128)}) custom-call(bf16[512,1024]{1,0:T(8,128)(2,1)} %inputs_ref.2, bf16[512,1024]{1,0:T(8,128)(2,1)} %cotangent_ref.3, f32[512,1]{1,0:T(8,128)} %copy.41.keep_ref), custom_call_target="tpu_custom_call" | custom-call | bytes 6291456 | tf_op jit(solution)/shard_map/prepare/pallas_call | solution.py:216
  25.1 2.9 %collective-permute-done.7 = f32[8,864]{1,0:T(8,128)S(1)} collective-permute-done((f32[8,864]{1,0:T(8,128)S(1)}, f32[8,864]{1,0:T(8,128)S(1)}, u32[]{:S(2)}, u32[]{:S(2)}) %collective-permute-start.7) | collective-permute-done | bytes 27680 | tf_op jit(solution)/shard_map/ppermute | solution.py:777
  35.8 7.3 %collective-permute-done.4.refs_3_ = bf16[128,1024]{1,0:T(8,128)(2,1)} collective-permute-done((bf16[128,1024]{1,0:T(8,128)(2,1)S(1)}, bf16[128,1024]{1,0:T(8,128)(2,1)}, u32[]{:S(2)}, u32[]{:S(2)}) %collective-permute-start.4) | collective-permute-done | bytes 262176 | tf_op jit(solution)/shard_map/ppermute | solution.py:777
  43.4 3.5 %collective-permute-done.10.refs_1_ = bf16[128,1024]{1,0:T(8,128)(2,1)S(1)} collective-permute-done((bf16[128,1024]{1,0:T(8,128)(2,1)S(1)}, bf16[128,1024]{1,0:T(8,128)(2,1)S(1)}, u32[]{:S(2)}, u32[]{:S(2)}) %collective-permute-start.10) | collective-permute-done | bytes 262176 | tf_op jit(solution)/shard_map/ppermute | solution.py:777
  50.0 4.7 %collective-permute-done.12.refs_2_ = bf16[128,1024]{1,0:T(8,128)(2,1)S(1)} collective-permute-done((bf16[128,1024]{1,0:T(8,128)(2,1)S(1)}, bf16[128,1024]{1,0:T(8,128)(2,1)S(1)}, u32[]{:S(2)}, u32[]{:S(2)}) %collective-permute-start.12) | collective-permute-done | bytes 262176 | tf_op jit(solution)/shard_map/ppermute | solution.py:777
  56.7 3.3 %collective-permute-done.11.refs_5_ = bf16[2,128,1024]{2,1,0:T(8,128)(2,1)S(1)} collective-permute-done((bf16[2,128,1024]{2,1,0:T(8,128)(2,1)S(1)}, bf16[2,128,1024]{2,1,0:T(8,128)(2,1)S(1)}, u32[]{:S(2)}, u32[]{:S(2)}) %collective-permute-start.11) | collective-permute-done | bytes 524320 | tf_op jit(solution)/shard_map/ppermute | solution.py:777
  62.2 3.6 %join_expand.1 = (bf16[1024,1024]{1,0:T(8,128)(2,1)}, f32[1,1024]{1,0:T(1,128)}) custom-call(s32[1]{0:T(128)} %bitcast.2.place_ref, bf16[128,1024]{1,0:T(8,128)(2,1)} %w_ref.2, bf16[128,1024]{1,0:T(8,128)(2,1)} %copy-done.30, bf16[128,1024]{1,0:T(8,128)(2,1)} %copy-done.16, bf16[128,1024]{1,0:T(8,128)(2,1)} %collective-permute-done.4.refs_3_, ...), custom_call_target="tpu_custom_call" | custom-call | flops 1000000000 | bytes 6291456 | tf_op jit(solution)/shard_map/join_expand/pallas_call | solution.py:170
  65.8 4.4 %collective-permute-done.15.refs_2_ = bf16[128,1024]{1,0:T(8,128)(2,1)S(1)} collective-permute-done((bf16[128,1024]{1,0:T(8,128)(2,1)}, bf16[128,1024]{1,0:T(8,128)(2,1)S(1)}, u32[]{:S(2)}, u32[]{:S(2)}) %collective-permute-start.15) | collective-permute-done | bytes 262176 | tf_op jit(solution)/shard_map/ppermute | solution.py:777
  78.3 16.7 %hidden.1 = (bf16[2048,1024]{1,0:T(8,128)(2,1)}, bf16[2048,1024]{1,0:T(8,128)(2,1)}, bf16[4,128,1024]{2,1,0:T(8,128)(2,1)}, bf16[4,128,1024]{2,1,0:T(8,128)(2,1)}) custom-call(s32[1]{0:T(128)} %bitcast.2.place_ref, bf16[2,512,1024]{2,1,0:T(8,128)(2,1)} %get-tuple-element.120.a_ref.first_ref, bf16[2,512,1024]{2,1,0:T(8,128)(2,1)} %collective-permute-done.16.b_ref.second_ref, ...), custom_call_target="tpu_custom_call" | custom-call | flops 12000000000 | bytes 20971520 | tf_op jit(solution)/shard_map/hidden/pallas_call | solution.py:515
  99.8 3.1 %join.1.w_ref.shrink_ref = bf16[1024,1024]{1,0:T(8,128)(2,1)} custom-call(s32[1]{0:T(128)} %bitcast.2.place_ref, bf16[128,1024]{1,0:T(8,128)(2,1)} %refs_0_.2, bf16[128,1024]{1,0:T(8,128)(2,1)} %copy-done.12, bf16[128,1024]{1,0:T(8,128)(2,1)} %copy-done.9, bf16[128,1024]{1,0:T(8,128)(2,1)} %copy-done.14, bf16[2,128,1024]{2,1,0:T(8,128)(2,1)} %copy-done.10, ...), custom_call_target="tpu_custom_call" | custom-call | bytes 4194304 | tf_op jit(solution)/shard_map/join/pallas_call | solution.py:191
  102.8 14.7 %unhidden.1 = (bf16[2048,1024]{1,0:T(8,128)(2,1)}, bf16[4,128,1024]{2,1,0:T(8,128)(2,1)}, bf16[4,128,1024]{2,1,0:T(8,128)(2,1)}, f32[1,1024]{1,0:T(1,128)}) custom-call(s32[1]{0:T(128)} %bitcast.2.place_ref, bf16[2,512,1024]{2,1,0:T(8,128)(2,1)} %get-tuple-element.120.a_ref.first_ref, bf16[2,512,1024]{2,1,0:T(8,128)(2,1)} %collective-permute-done.16.b_ref.second_ref, ...), custom_call_target="tpu_custom_call" | custom-call | flops 12000000000 | bytes 23068672 | tf_op jit(solution)/shard_map/unhidden/pallas_call | solution.py:596
  120.0 3.4 %join_project.1 = (bf16[1024,768]{1,0:T(8,128)(2,1)}, bf16[256,1024]{1,0:T(8,128)(2,1)}, f32[1,768]{1,0:T(1,128)}) custom-call(s32[1]{0:T(128)} %bitcast.2.place_ref, bf16[128,1024]{1,0:T(8,128)(2,1)} %get-tuple-element.138.refs_0_, bf16[128,1024]{1,0:T(8,128)(2,1)} %collective-permute-done.18.refs_1_, bf16[128,1024]{1,0:T(8,128)(2,1)} %copy-done.17, ...), custom_call_target="tpu_custom_call" | custom-call | flops 1000000000 | bytes 10485760 | tf_op jit(solution)/shard_map/join_project/pallas_call | solution.py:143
  123.4 22.6 %attention.2 = (bf16[2,512,256]{2,1,0:T(8,128)(2,1)}, bf16[2,512,768]{2,1,0:T(8,128)(2,1)}, f32[1,768]{1,0:T(1,128)}) custom-call(s32[1]{0:T(128)} %bitcast.core_ref, bf16[2,512,1024]{2,1,0:T(8,128)(2,1)} %collective-permute-done.1.c_ref.first_ref, bf16[2,512,1024]{2,1,0:T(8,128)(2,1)} %collective-permute-done.17.d_ref.second_ref, ...), custom_call_target="tpu_custom_call" | custom-call | flops 23000000512 | bytes 8388608 | tf_op jit(solution)/shard_map/attention/pallas_call | solution.py:379
  148.7 11.1 %results.2 = (bf16[2,512,1024]{2,1,0:T(8,128)(2,1)}, bf16[2,512,1024]{2,1,0:T(8,128)(2,1)}) custom-call(bf16[2,512,256]{2,1,0:T(8,128)(2,1)} %get-tuple-element.150.mixed_ref.mixed_two_ref, bf16[2,512,768]{2,1,0:T(8,128)(2,1)} %get-tuple-element.151.pg_ref.pg_two_ref, bf16[2048,1024]{1,0:T(8,128)(2,1)} %get-tuple-element.174.act_ref, ...), custom_call_target="tpu_custom_call" | custom-call | flops 8000000000 | bytes 16777216 | tf_op jit(solution)/shard_map/results/pallas_call | solution.py:760
  165.1 22.8 %attention.3 = (bf16[2,512,256]{2,1,0:T(8,128)(2,1)}, bf16[2,512,768]{2,1,0:T(8,128)(2,1)}, f32[1,768]{1,0:T(1,128)}) custom-call(s32[1]{0:T(128)} %bitcast.core_ref, bf16[2,512,1024]{2,1,0:T(8,128)(2,1)} %get-tuple-element.120.a_ref.first_ref, bf16[2,512,1024]{2,1,0:T(8,128)(2,1)} %collective-permute-done.16.b_ref.second_ref, ...), custom_call_target="tpu_custom_call" | custom-call | flops 23000000512 | bytes 8388608 | tf_op jit(solution)/shard_map/attention/pallas_call | solution.py:379
  191.9 3.2 %add_convert_fusion = bf16[2,512,1024]{2,1,0:T(8,128)(2,1)S(1)} fusion(bf16[2,512,1024]{2,1,0:T(8,128)(2,1)} %collective-permute-done.24, bf16[2,512,1024]{2,1,0:T(8,128)(2,1)} %get-tuple-element.156), kind=kLoop, calls=%fused_computation | loop fusion | flops 4194304 | bytes 6291456 | tf_op jit(solution)/shard_map/convert_element_type | solution.py:1160
  196.5 9.3 %attention_grads.1 = (bf16[2,128,1024]{2,1,0:T(8,128)(2,1)}, bf16[2,128,1024]{2,1,0:T(8,128)(2,1)}, bf16[4,128,1024]{2,1,0:T(8,128)(2,1)}) custom-call(s32[1]{0:T(128)} %bitcast.2.place_ref, bf16[2,512,1024]{2,1,0:T(8,128)(2,1)} %get-tuple-element.120.a_ref.first_ref, bf16[2,512,1024]{2,1,0:T(8,128)(2,1)} %collective-permute-done.16.b_ref.second_ref, ...), custom_call_target="tpu_custom_call" | custom-call | flops 7000000000 | bytes 16777216 | tf_op jit(solution)/shard_map/attention_grads/pallas_call | solution.py:679
  210.5 10.8 %results.3 = (bf16[2,512,1024]{2,1,0:T(8,128)(2,1)}, bf16[2,512,1024]{2,1,0:T(8,128)(2,1)}) custom-call(bf16[2,512,256]{2,1,0:T(8,128)(2,1)} %get-tuple-element.164.mixed_one_ref.mixed_ref, bf16[2,512,768]{2,1,0:T(8,128)(2,1)} %get-tuple-element.171.pg_one_ref.pg_ref, bf16[2048,1024]{1,0:T(8,128)(2,1)} %get-tuple-element.174.act_ref, ...), custom_call_target="tpu_custom_call" | custom-call | flops 8000000000 | bytes 16777216 | tf_op jit(solution)/shard_map/results/pallas_call | solution.py:760
  226.6 7.5 %collective-permute-done.35.late_ref = bf16[2,128,1024]{2,1,0:T(8,128)(2,1)S(1)} collective-permute-done((bf16[2,128,1024]{2,1,0:T(8,128)(2,1)}, bf16[2,128,1024]{2,1,0:T(8,128)(2,1)S(1)}, u32[]{:S(2)}, u32[]{:S(2)}) %collective-permute-start.35) | collective-permute-done | bytes 524320 | tf_op jit(solution)/shard_map/ppermute | solution.py:777
  235.5 7.3 %collective-permute-done.25.far_ref = bf16[2,512,1024]{2,1,0:T(8,128)(2,1)} collective-permute-done((bf16[2,512,1024]{2,1,0:T(8,128)(2,1)S(1)}, bf16[2,512,1024]{2,1,0:T(8,128)(2,1)}, u32[]{:S(2)}, u32[]{:S(2)}) %collective-permute-start.25) | collective-permute-done | bytes 2097184 | tf_op jit(solution)/shard_map/ppermute | solution.py:777
  255.2 5.9 %finish_tokens.1 = (bf16[512,1024]{1,0:T(8,128)(2,1)}, bf16[512,1024]{1,0:T(8,128)(2,1)}) custom-call(bf16[2,512,1024]{2,1,0:T(8,128)(2,1)} %get-tuple-element.185.mine_ref, bf16[2,512,1024]{2,1,0:T(8,128)(2,1)} %copy-done.2, bf16[2,512,1024]{2,1,0:T(8,128)(2,1)} %collective-permute-done.25.far_ref, bf16[512,1024]{1,0:T(8,128)(2,1)} %inputs_ref.2, ...), custom_call_target="tpu_custom_call" | custom-call | bytes 12582912 | tf_op jit(solution)/shard_map/finish_tokens/pallas_call | solution.py:962
  264.0 4.2 %finish_project.1 = (f32[128,768]{1,0:T(8,128)}, f32[32,1024]{1,0:T(8,128)}, f32[2,128]{1,0:T(2,128)}) custom-call(bf16[4,128,1024]{2,1,0:T(8,128)(2,1)} %get-tuple-element.172.own_ref, bf16[2,128,1024]{2,1,0:T(8,128)(2,1)} %copy-done.5, bf16[2,128,1024]{2,1,0:T(8,128)(2,1)} %copy-done.6, bf16[128,1024]{1,0:T(8,128)(2,1)} %copy-done.15, ...), custom_call_target="tpu_custom_call" | custom-call | bytes 4194304 | tf_op jit(solution)/shard_map/finish_project/pallas_call | solution.py:897
  (210 shorter events, 91.0 us)
Async XLA Ops:
  0.6 22.5 %collective-permute-start.3 = (bf16[128,1024]{1,0:T(8,128)(2,1)}, bf16[128,1024]{1,0:T(8,128)(2,1)S(1)}, u32[]{:S(2)}, u32[]{:S(2)}) collective-permute-start(bf16[128,1024]{1,0:T(8,128)(2,1)} %w_ref.2), channel_id=1, source_target_pairs={{0,16},{4,20},{8,24},{12,28},{16,0},{20,4},{24,8},{28,12},{1,17},{... | collective-permute-start | bytes 786440 | tf_op jit(solution)/shard_map/ppermute | solution.py:777
  4.7 18.5 %collective-permute-start.2 = (bf16[128,1024]{1,0:T(8,128)(2,1)}, bf16[128,1024]{1,0:T(8,128)(2,1)S(1)}, u32[]{:S(2)}, u32[]{:S(2)}) collective-permute-start(bf16[128,1024]{1,0:T(8,128)(2,1)} %w_ref.2), channel_id=1, source_target_pairs={{0,4},{4,0},{8,12},{12,8},{16,20},{20,16},{24,28},{28,24},{1,5},{5... | collective-permute-start | bytes 786440 | tf_op jit(solution)/shard_map/ppermute | solution.py:777
  23.4 49.0 %collective-permute-start.1 = (bf16[2,512,1024]{2,1,0:T(8,128)(2,1)}, bf16[2,512,1024]{2,1,0:T(8,128)(2,1)}, u32[]{:S(2)}, u32[]{:S(2)}) collective-permute-start(bf16[2,512,1024]{2,1,0:T(8,128)(2,1)} %get-tuple-element.120.a_ref.first_ref), channel_id=1, source_target_pairs={{0,2},{1,3},{2,0},{3,1},{4,6},{5,7},{6,4},{7,5},{8,10},{9,11},{10,... | collective-permute-start | bytes 6291464 | tf_op jit(solution)/shard_map/ppermute | solution.py:777
  28.1 44.3 %collective-permute-start.16 = (bf16[2,512,1024]{2,1,0:T(8,128)(2,1)}, bf16[2,512,1024]{2,1,0:T(8,128)(2,1)}, u32[]{:S(2)}, u32[]{:S(2)}) collective-permute-start(bf16[2,512,1024]{2,1,0:T(8,128)(2,1)} %get-tuple-element.120.a_ref.first_ref), channel_id=1, source_target_pairs={{0,1},{1,0},{2,3},{3,2},{4,5},{5,4},{6,7},{7,6},{8,9},{9,8},{10,11... | collective-permute-start | bytes 6291464 | tf_op jit(solution)/shard_map/ppermute | solution.py:777
  32.1 15.5 %collective-permute-start.9 = (bf16[2,128,1024]{2,1,0:T(8,128)(2,1)S(1)}, bf16[2,128,1024]{2,1,0:T(8,128)(2,1)S(1)}, u32[]{:S(2)}, u32[]{:S(2)}) collective-permute-start(bf16[2,128,1024]{2,1,0:T(8,128)(2,1)S(1)} %pad_maximum_fusion), channel_id=1, source_target_pairs={{0,8},{4,12},{8,0},{12,4},{16,24},{20,28},{24,16},{28,20},{1,9},{5... | collective-permute-start | bytes 1572872 | tf_op jit(solution)/shard_map/ppermute | solution.py:777
  54.7 17.6 %collective-permute-start.14 = (bf16[2,128,1024]{2,1,0:T(8,128)(2,1)S(1)}, bf16[2,128,1024]{2,1,0:T(8,128)(2,1)S(1)}, u32[]{:S(2)}, u32[]{:S(2)}) collective-permute-start(bf16[2,128,1024]{2,1,0:T(8,128)(2,1)S(1)} %pad_maximum_fusion.1), channel_id=1, source_target_pairs={{0,8},{4,12},{8,0},{12,4},{16,24},{20,28},{24,16},{28,20},{1,9},{5... | collective-permute-start | bytes 1572872 | tf_op jit(solution)/shard_map/ppermute | solution.py:777
  54.8 15.4 %collective-permute-start.15 = (bf16[128,1024]{1,0:T(8,128)(2,1)}, bf16[128,1024]{1,0:T(8,128)(2,1)S(1)}, u32[]{:S(2)}, u32[]{:S(2)}) collective-permute-start(bf16[128,1024]{1,0:T(8,128)(2,1)} %get-tuple-element.138.refs_0_), channel_id=1, source_target_pairs={{0,16},{4,20},{8,24},{12,28},{16,0},{20,4},{24,8},{28,12},{1,17},{... | collective-permute-start | bytes 786440 | tf_op jit(solution)/shard_map/ppermute | solution.py:777
  74.6 44.6 %collective-permute-start.19 = (bf16[128,1024]{1,0:T(8,128)(2,1)S(1)}, bf16[128,1024]{1,0:T(8,128)(2,1)}, u32[]{:S(2)}, u32[]{:S(2)}) collective-permute-start(bf16[128,1024]{1,0:T(8,128)(2,1)S(1)} %collective-permute-done.15.refs_2_), channel_id=1, source_target_pairs={{0,4},{4,0},{8,12},{12,8},{16,20},{20,16},{24,28},{28,24},{1,5},{5... | collective-permute-start | bytes 786440 | tf_op jit(solution)/shard_map/ppermute | solution.py:777
  76.9 19.2 %collective-permute-start.20 = (bf16[2,128,1024]{2,1,0:T(8,128)(2,1)S(1)}, bf16[2,128,1024]{2,1,0:T(8,128)(2,1)}, u32[]{:S(2)}, u32[]{:S(2)}) collective-permute-start(bf16[2,128,1024]{2,1,0:T(8,128)(2,1)S(1)} %pad_maximum_fusion.2), channel_id=1, source_target_pairs={{0,8},{4,12},{8,0},{12,4},{16,24},{20,28},{24,16},{28,20},{1,9},{5... | collective-permute-start | bytes 1572872 | tf_op jit(solution)/shard_map/ppermute | solution.py:777
  77.8 18.3 %collective-permute-start.22 = (bf16[2,128,1024]{2,1,0:T(8,128)(2,1)S(1)}, bf16[2,128,1024]{2,1,0:T(8,128)(2,1)S(1)}, u32[]{:S(2)}, u32[]{:S(2)}) collective-permute-start(bf16[2,128,1024]{2,1,0:T(8,128)(2,1)S(1)} %collective-permute-done.14.refs_4_), channel_id=1, source_target_pairs={{0,4},{4,0},{8,12},{12,8},{16,20},{20,16},{24,28},{28,24},{1,5},{5... | collective-permute-start | bytes 1572872 | tf_op jit(solution)/shard_map/ppermute | solution.py:777
  96.2 23.1 %collective-permute-start.18 = (bf16[128,1024]{1,0:T(8,128)(2,1)}, bf16[128,1024]{1,0:T(8,128)(2,1)}, u32[]{:S(2)}, u32[]{:S(2)}) collective-permute-start(bf16[128,1024]{1,0:T(8,128)(2,1)} %get-tuple-element.138.refs_0_), channel_id=1, source_target_pairs={{0,4},{4,0},{8,12},{12,8},{16,20},{20,16},{24,28},{28,24},{1,5},{5... | collective-permute-start | bytes 786440 | tf_op jit(solution)/shard_map/ppermute | solution.py:777
  97.7 21.5 %collective-permute-start.21 = (bf16[2,128,1024]{2,1,0:T(8,128)(2,1)}, bf16[2,128,1024]{2,1,0:T(8,128)(2,1)S(1)}, u32[]{:S(2)}, u32[]{:S(2)}) collective-permute-start(bf16[2,128,1024]{2,1,0:T(8,128)(2,1)} %collective-permute-done.20.refs_4_), channel_id=1, source_target_pairs={{0,4},{4,0},{8,12},{12,8},{16,20},{20,16},{24,28},{28,24},{1,5},{5... | collective-permute-start | bytes 1572872 | tf_op jit(solution)/shard_map/ppermute | solution.py:777
  98.2 47.8 %collective-permute-start.23 = (bf16[4,128,1024]{2,1,0:T(8,128)(2,1)}, bf16[4,128,1024]{2,1,0:T(8,128)(2,1)S(1)}, u32[]{:S(2)}, u32[]{:S(2)}) collective-permute-start(bf16[4,128,1024]{2,1,0:T(8,128)(2,1)} %get-tuple-element.153), channel_id=1, source_target_pairs={{0,4},{4,0},{8,12},{12,8},{16,20},{20,16},{24,28},{28,24},{1,5},{5... | collective-permute-start | bytes 3145736 | tf_op jit(solution)/shard_map/ppermute | solution.py:777
  118.6 41.9 %collective-permute-start.27 = (bf16[4,128,1024]{2,1,0:T(8,128)(2,1)}, bf16[4,128,1024]{2,1,0:T(8,128)(2,1)S(1)}, u32[]{:S(2)}, u32[]{:S(2)}) collective-permute-start(bf16[4,128,1024]{2,1,0:T(8,128)(2,1)} %get-tuple-element.162), channel_id=1, source_target_pairs={{0,4},{4,0},{8,12},{12,8},{16,20},{20,16},{24,28},{28,24},{1,5},{5... | collective-permute-start | bytes 3145736 | tf_op jit(solution)/shard_map/ppermute | solution.py:777
  147.2 15.1 %collective-permute-start.26 = (bf16[2,128,1024]{2,1,0:T(8,128)(2,1)}, bf16[2,128,1024]{2,1,0:T(8,128)(2,1)}, u32[]{:S(2)}, u32[]{:S(2)}) collective-permute-start(bf16[2,128,1024]{2,1,0:T(8,128)(2,1)} %add_convert_fusion.3), channel_id=1, source_target_pairs={{0,8},{4,12},{8,0},{12,4},{16,24},{20,28},{24,16},{28,20},{1,9},{5... | collective-permute-start | bytes 1572872 | tf_op jit(solution)/shard_map/ppermute | solution.py:777
  160.8 27.8 %collective-permute-start.28 = (bf16[2,128,1024]{2,1,0:T(8,128)(2,1)S(1)}, bf16[2,128,1024]{2,1,0:T(8,128)(2,1)S(1)}, u32[]{:S(2)}, u32[]{:S(2)}) collective-permute-start(bf16[2,128,1024]{2,1,0:T(8,128)(2,1)S(1)} %add_convert_fusion.2), channel_id=1, source_target_pairs={{0,8},{4,12},{8,0},{12,4},{16,24},{20,28},{24,16},{28,20},{1,9},{5... | collective-permute-start | bytes 1572872 | tf_op jit(solution)/shard_map/ppermute | solution.py:777
  162.2 29.7 %collective-permute-start.24 = (bf16[2,512,1024]{2,1,0:T(8,128)(2,1)}, bf16[2,512,1024]{2,1,0:T(8,128)(2,1)}, u32[]{:S(2)}, u32[]{:S(2)}) collective-permute-start(bf16[2,512,1024]{2,1,0:T(8,128)(2,1)} %get-tuple-element.157), channel_id=1, source_target_pairs={{0,1},{1,0},{2,3},{3,2},{4,5},{5,4},{6,7},{7,6},{8,9},{9,8},{10,11... | collective-permute-start | bytes 6291464 | tf_op jit(solution)/shard_map/ppermute | solution.py:777
  163.4 33.1 %collective-permute-start.29 = (bf16[128,1024]{1,0:T(8,128)(2,1)S(1)}, bf16[128,1024]{1,0:T(8,128)(2,1)S(1)}, u32[]{:S(2)}, u32[]{:S(2)}) collective-permute-start(bf16[128,1024]{1,0:T(8,128)(2,1)S(1)} %fusion), channel_id=1, source_target_pairs={{0,16},{4,20},{8,24},{12,28},{16,0},{20,4},{24,8},{28,12},{1,17},{... | collective-permute-start | bytes 786440 | tf_op jit(solution)/shard_map/ppermute | solution.py:777
  190.6 16.9 %collective-permute-start.30 = (bf16[128,1024]{1,0:T(8,128)(2,1)}, bf16[128,1024]{1,0:T(8,128)(2,1)S(1)}, u32[]{:S(2)}, u32[]{:S(2)}) collective-permute-start(bf16[128,1024]{1,0:T(8,128)(2,1)} %fusion.1), channel_id=1, source_target_pairs={{0,16},{4,20},{8,24},{12,28},{16,0},{20,4},{24,8},{28,12},{1,17},{... | collective-permute-start | bytes 786440 | tf_op jit(solution)/shard_map/ppermute | solution.py:777
  195.1 47.6 %collective-permute-start.25 = (bf16[2,512,1024]{2,1,0:T(8,128)(2,1)S(1)}, bf16[2,512,1024]{2,1,0:T(8,128)(2,1)}, u32[]{:S(2)}, u32[]{:S(2)}) collective-permute-start(bf16[2,512,1024]{2,1,0:T(8,128)(2,1)S(1)} %add_convert_fusion), channel_id=1, source_target_pairs={{0,2},{1,3},{2,0},{3,1},{4,6},{5,7},{6,4},{7,5},{8,10},{9,11},{10,... | collective-permute-start | bytes 6291464 | tf_op jit(solution)/shard_map/ppermute | solution.py:777
  207.4 15.6 %collective-permute-start.31 = (bf16[2,128,1024]{2,1,0:T(8,128)(2,1)}, bf16[2,128,1024]{2,1,0:T(8,128)(2,1)S(1)}, u32[]{:S(2)}, u32[]{:S(2)}) collective-permute-start(bf16[2,128,1024]{2,1,0:T(8,128)(2,1)} %get-tuple-element.177), channel_id=1, source_target_pairs={{0,4},{4,0},{8,12},{12,8},{16,20},{20,16},{24,28},{28,24},{1,5},{5... | collective-permute-start | bytes 1572872 | tf_op jit(solution)/shard_map/ppermute | solution.py:777
  209.7 13.4 %collective-permute-start.33 = (f32[1,2816]{1,0:T(1,128)S(1)}, f32[1,2816]{1,0:T(1,128)S(1)}, u32[]{:S(2)}, u32[]{:S(2)}) collective-permute-start(f32[1,2816]{1,0:T(1,128)S(1)} %add.119), channel_id=1, source_target_pairs={{0,8},{4,12},{8,0},{12,4},{16,24},{20,28},{24,16},{28,20},{1,9},{5... | collective-permute-start | bytes 33800 | tf_op jit(solution)/shard_map/ppermute | solution.py:777
  221.4 12.8 %collective-permute-start.35 = (bf16[2,128,1024]{2,1,0:T(8,128)(2,1)}, bf16[2,128,1024]{2,1,0:T(8,128)(2,1)S(1)}, u32[]{:S(2)}, u32[]{:S(2)}) collective-permute-start(bf16[2,128,1024]{2,1,0:T(8,128)(2,1)} %get-tuple-element.183), channel_id=1, source_target_pairs={{0,4},{4,0},{8,12},{12,8},{16,20},{20,16},{24,28},{28,24},{1,5},{5... | collective-permute-start | bytes 1572872 | tf_op jit(solution)/shard_map/ppermute | solution.py:777
  249.3 14.0 %collective-permute-start.37 = (bf16[128,1024]{1,0:T(8,128)(2,1)S(1)}, bf16[128,1024]{1,0:T(8,128)(2,1)S(1)}, u32[]{:S(2)}, u32[]{:S(2)}) collective-permute-start(bf16[128,1024]{1,0:T(8,128)(2,1)S(1)} %fusion.2), channel_id=1, source_target_pairs={{0,16},{4,20},{8,24},{12,28},{16,0},{20,4},{24,8},{28,12},{1,17},{... | collective-permute-start | bytes 786440 | tf_op jit(solution)/shard_map/ppermute | solution.py:777
  (48 other events, 547.2 us)

commit v4 on v3

--- a/solution.py
+++ b/solution.py
@@ -804,10 +804,10 @@
         self.near = hop(block, size, 1) if near else None
         self.far_near = None
 
-    def second(self, *first):
+    def second(self, *first, near=True):
         own, far = after((self.own, self.far), *first) if first else (self.own, self.far)
         self.pair = hop(jnp.stack([own, far]), self.size, 2)
-        if self.far_near is None:
+        if near and self.far_near is None:
             self.far_near = hop(far, self.size, 1)
 
     def second_near(self):
@@ -825,18 +825,15 @@
 class Scatter:
     def __init__(self, near, own, size, late=None):
         self.own, self.size = own, size
-        if late is None:
-            near = hop(near, size, 1)
-            self.near, self.late = near[2:], near[:2]
-            self.arrived = near
-        else:
-            self.near, self.late = hop(near, size, 1), hop(late, size, 1)
-            self.arrived = self.near
+        self.near = hop(near, size, 1)
+        self.late = self.near if late is None else hop(late, size, 1)
+        self.start = 2 if late is None else 0
 
     def second(self, *first):
-        near, own = after((self.near, self.own[2:]), *first)
+        near, own = after((self.near, self.own), *first)
+        near, own = near[self.start : self.start + 2], own[2:]
         self.pair = hop((own.astype(F32) + near.astype(F32)).astype(BF16), self.size, 2)
-        return self.arrived
+        return self.near
 
     def third(self, *first):
         pair, near = after((self.pair, self.late), *first) if first else (self.pair, self.late)
@@ -1036,12 +1033,9 @@
 
     own_labels = lax.dynamic_slice_in_dim(segments, rank * rows, rows, 0)
     keep = (own_labels != 0).astype(F32)[:, None]
-    early = inputs
     if direct:
         first = Gather(expand_weight, size)
-    packed_weights, *tables = pack(project_weight, dense_weight, rotary_turns())
-    if direct:
-        (early,) = after((early,), packed_weights)
+    early = after((inputs,), first.near)[0] if direct else inputs
     own, bias_grad = prepare(early, cotangent, keep)
 
     small = jnp.concatenate(
@@ -1056,6 +1050,7 @@
     piece = small.shape[0] // 5
     small = slots(small, rank, across)
     small_far = small + exchange(small, "tensor", across, 2)
+    (small_far,) = after((small_far,), own)
     small = small_far + exchange(small_far, "tensor", across, 1)
     own_vectors = jnp.swapaxes(small.reshape(across, 5, piece), 0, 1).reshape(5, block)
     counts = (5 * block, project_bias.shape[0], expand_bias.shape[0])
@@ -1092,16 +1087,18 @@
     partner = chip_pair(own_near)
     if direct:
         first.second_near()
+        (pack_weight,) = after((project_weight,), first.far_near)
+        packed_weights, *tables = pack(pack_weight, dense_weight, rotary_turns())
         (near_block,) = after((shrink_weight,), packed_near)
         near_block = hop(near_block, size, 1)
         first.second(packed)
         (far_block,) = after((shrink_weight,), packed)
         second = Gather(far_block, size, False)
         second.near = near_block
-        second.second(first.pair, first.far_near)
+        second.second(first.pair, first.far_near, packed_weights, near_block)
         (far_block,) = after((packed_weights,), second.far)
         third = Gather(far_block, size, False)
-        first.third(first.far_near, near_block)
+        first.third(first.far_near, packed_weights)
         expand, expand_row = join_expand(
             place,
             first.blocks(),
@@ -1109,12 +1106,12 @@
             vectors[3][None, :],
             expand_offset[None, :],
         )
-        across_chip, expand = after(
-            (across_chip, expand), second.far_near, second.pair, third.far, partner
-        )
+        (across_chip,) = after((across_chip,), second.pair, third.far, expand_row)
+        (expand,) = after((expand,), second.pair, second.far_near, third.far, partner)
         second.third(expand)
-        third.second(second.pair)
+        third.second(second.pair, near=False)
     else:
+        _, *tables = pack(project_weight, dense_weight, rotary_turns())
         expand, expand_row = folded(expand_weight, vectors[2], vectors[3], expand_offset)
         project, project_row = folded(
             by_part(project_weight), vectors[0], vectors[1], project_offset
@@ -1126,8 +1123,9 @@
     active, slope, shrink_near, shrink_own = hidden_layer(place, parts, expand, expand_row, pairs)
     if direct:
         shrink_sums = Scatter(shrink_near, shrink_own, size)
-        (near_block,) = after((packed_weights,), shrink_own)
+        near_block, far_block = after((packed_weights, third.far), shrink_own)
         third.near = hop(near_block, size, 1)
+        third.far_near = hop(far_block, size, 1)
         third.third(shrink_own)
         shrink = join(place, second.blocks(shrink_own))
     hidden_grad, expand_near, expand_own, expand_offset_grad = unhidden_layer(
@@ -1167,7 +1165,7 @@
         (project,) = after((project,), far_mine)
     one = attend(0)
     if direct:
-        ready = expand_sums.third(one[2])
+        ready = expand_sums.third(one[2], far_sum)
         (pair_grads,) = after((one[1],), ready, shrink_sums.far, far_sum)
         one = (one[0], pair_grads, one[2])
     both_near, both_late, both_own = attention_grads(place, parts, one[:2], two[:2], pairs)
@@ -1197,7 +1195,7 @@
 
     own_rows = own_vectors[:4]
     if direct:
-        both_sums.second(near_mine, totals_pair)
+        both_sums.second(near_mine, totals)
         shrink_sum = shrink_sums.total()
         ready = both_sums.third(shrink_sum)
         (expand_totals,) = after((expand_totals,), ready)

time: 280 us -> 279 us (level)
  transfers between devices with their start and end apart: 41 -> 41, of which waited for: 19 -> 23; matrix products, arithmetic and copies ran while one was open for 10% -> 9% of each run, Pallas kernels for 48% -> 48%
where the time goes in v4:
time: 279 us; the launch traced here: 275 us
  Pallas kernels  137 us (49%)
  waiting for transfers between devices  56.3 us (20%)
  starting transfers between devices  47.7 us (17%)
  other arithmetic  17.1 us (6%)
  local copies, waits for them, and re-layouts  15.1 us (5%)
    ppermute x41, waiting for transfers between devices, exchange(): return lax.ppermute(value, axis, [(i, i ^ offset) for i in range(size)])  56.3 us
    ppermute x41, starting transfers between devices, exchange(): return lax.ppermute(value, axis, [(i, i ^ offset) for i in range(size)])  47.7 us
    pallas_call x2, Pallas kernels, attention(): pl.pallas_call(attention_kernel, in_specs=[SMEM] + [VMEM] * 9, out_specs=...  45.4 us
    pallas_call x2, Pallas kernels, results(): pl.pallas_call(functools.partial(results_kernel, first=first), in_specs=[...  21.8 us
    pallas_call x1, Pallas kernels, hidden_layer(): pl.pallas_call(hidden_kernel, in_specs=[SMEM] + [ANY] * 5 + [VMEM], out_s...  16.7 us
    pallas_call x1, Pallas kernels, unhidden_layer(): pl.pallas_call(unhidden_kernel, in_specs=[SMEM] + [ANY] * 6, out_specs=[A...  14.7 us
    pallas_call x1, Pallas kernels, attention_grads(): pl.pallas_call(attention_grads_kernel, in_specs=[SMEM] + [ANY] * 8, out_s...  9.24 us
    pallas_call x1, Pallas kernels, finish_tokens(): pl.pallas_call(finish_tokens_kernel, grid=(4,), in_specs=[both] * 3 + [bl...  5.94 us
  transfers between devices with their start and end apart: 41, of which 23 were waited for; matrix products, arithmetic and copies ran while one was open for 9% of the time, Pallas kernels for 48%

profile of v4, /device:TPU:0, one launch (start us, length us, event | category | flops | bytes accessed | tf_op | source)
XLA Modules:
  0.0 274.8 jit_solution(625303951409445220)
XLA Ops:
  0.7 4.1 %collective-permute-start.5 = (bf16[128,1024]{1,0:T(8,128)(2,1)}, bf16[128,1024]{1,0:T(8,128)(2,1)S(1)}, u32[]{:S(2)}, u32[]{:S(2)}) collective-permute-start(bf16[128,1024]{1,0:T(8,128)(2,1)} %w_ref.2), channel_id=1, source_target_pairs={{0,16},{4,20},{8,24},{12,28},{16,0},{20,4},{24,8},{28,12},{1,17},{... | collective-permute-start | bytes 786440 | tf_op jit(solution)/shard_map/ppermute | solution.py:777
  12.8 3.9 %prepare.1 = (bf16[2,512,1024]{2,1,0:T(8,128)(2,1)}, f32[1,1024]{1,0:T(1,128)}) custom-call(bf16[512,1024]{1,0:T(8,128)(2,1)} %inputs_ref.2, bf16[512,1024]{1,0:T(8,128)(2,1)} %cotangent_ref.3, f32[512,1]{1,0:T(8,128)} %copy.40.keep_ref), custom_call_target="tpu_custom_call" | custom-call | bytes 6291456 | tf_op jit(solution)/shard_map/prepare/pallas_call | solution.py:216
  22.9 4.4 %collective-permute-done.6 = f32[8,864]{1,0:T(8,128)S(1)} collective-permute-done((f32[8,864]{1,0:T(8,128)S(1)}, f32[8,864]{1,0:T(8,128)S(1)}, u32[]{:S(2)}, u32[]{:S(2)}) %collective-permute-start.6) | collective-permute-done | bytes 27680 | tf_op jit(solution)/shard_map/ppermute | solution.py:777
  37.4 3.9 %collective-permute-done.10.refs_3_ = bf16[128,1024]{1,0:T(8,128)(2,1)S(1)} collective-permute-done((bf16[128,1024]{1,0:T(8,128)(2,1)S(1)}, bf16[128,1024]{1,0:T(8,128)(2,1)S(1)}, u32[]{:S(2)}, u32[]{:S(2)}) %collective-permute-start.10) | collective-permute-done | bytes 262176 | tf_op jit(solution)/shard_map/ppermute | solution.py:777
  44.3 4.1 %collective-permute-done.9.refs_4_ = bf16[2,128,1024]{2,1,0:T(8,128)(2,1)S(1)} collective-permute-done((bf16[2,128,1024]{2,1,0:T(8,128)(2,1)S(1)}, bf16[2,128,1024]{2,1,0:T(8,128)(2,1)S(1)}, u32[]{:S(2)}, u32[]{:S(2)}) %collective-permute-start.9) | collective-permute-done | bytes 524320 | tf_op jit(solution)/shard_map/ppermute | solution.py:777
  50.7 3.1 %collective-permute-start.13 = (bf16[128,1024]{1,0:T(8,128)(2,1)}, bf16[128,1024]{1,0:T(8,128)(2,1)S(1)}, u32[]{:S(2)}, u32[]{:S(2)}) collective-permute-start(bf16[128,1024]{1,0:T(8,128)(2,1)} %get-tuple-element.144.refs_0_), channel_id=1, source_target_pairs={{0,16},{4,20},{8,24},{12,28},{16,0},{20,4},{24,8},{28,12},{1,17},{... | collective-permute-start | bytes 786440 | tf_op jit(solution)/shard_map/ppermute | solution.py:777
  54.4 4.2 %collective-permute-done.14.refs_5_ = bf16[2,128,1024]{2,1,0:T(8,128)(2,1)S(1)} collective-permute-done((bf16[2,128,1024]{2,1,0:T(8,128)(2,1)S(1)}, bf16[2,128,1024]{2,1,0:T(8,128)(2,1)S(1)}, u32[]{:S(2)}, u32[]{:S(2)}) %collective-permute-start.14) | collective-permute-done | bytes 524320 | tf_op jit(solution)/shard_map/ppermute | solution.py:777
  59.4 3.6 %join_expand.1 = (bf16[1024,1024]{1,0:T(8,128)(2,1)}, f32[1,1024]{1,0:T(1,128)}) custom-call(s32[1]{0:T(128)} %bitcast.7.place_ref, bf16[128,1024]{1,0:T(8,128)(2,1)} %w_ref.2, bf16[128,1024]{1,0:T(8,128)(2,1)} %copy-done.30, bf16[128,1024]{1,0:T(8,128)(2,1)} %copy-done.18, bf16[128,1024]{1,0:T(8,128)(2,1)} %copy-done.31, bf16[2,128,1024]{2,1,0:T(8,128)(2,1)} %copy-done.27, ...), custom_call_target="tpu_custom_call" | custom-call | flops 1000000000 | bytes 6291456 | tf_op jit(solution)/shard_map/join_expand/pallas_call | solution.py:170
  70.8 4.5 %collective-permute-done.17.refs_3_ = bf16[128,1024]{1,0:T(8,128)(2,1)S(1)} collective-permute-done((bf16[128,1024]{1,0:T(8,128)(2,1)S(1)}, bf16[128,1024]{1,0:T(8,128)(2,1)S(1)}, u32[]{:S(2)}, u32[]{:S(2)}) %collective-permute-start.17) | collective-permute-done | bytes 262176 | tf_op jit(solution)/shard_map/ppermute | solution.py:777
  76.4 16.7 %hidden.1 = (bf16[2048,1024]{1,0:T(8,128)(2,1)}, bf16[2048,1024]{1,0:T(8,128)(2,1)}, bf16[4,128,1024]{2,1,0:T(8,128)(2,1)}, bf16[4,128,1024]{2,1,0:T(8,128)(2,1)}) custom-call(s32[1]{0:T(128)} %bitcast.7.place_ref, bf16[2,512,1024]{2,1,0:T(8,128)(2,1)} %get-tuple-element.126.a_ref.first_ref, bf16[2,512,1024]{2,1,0:T(8,128)(2,1)} %collective-permute-done.16.b_ref.second_ref, ...), custom_call_target="tpu_custom_call" | custom-call | flops 12000000000 | bytes 20971520 | tf_op jit(solution)/shard_map/hidden/pallas_call | solution.py:515
  100.3 14.7 %unhidden.1 = (bf16[2048,1024]{1,0:T(8,128)(2,1)}, bf16[4,128,1024]{2,1,0:T(8,128)(2,1)}, bf16[4,128,1024]{2,1,0:T(8,128)(2,1)}, f32[1,1024]{1,0:T(1,128)}) custom-call(s32[1]{0:T(128)} %bitcast.7.place_ref, bf16[2,512,1024]{2,1,0:T(8,128)(2,1)} %get-tuple-element.126.a_ref.first_ref, bf16[2,512,1024]{2,1,0:T(8,128)(2,1)} %collective-permute-done.16.b_ref.second_ref, ...), custom_call_target="tpu_custom_call" | custom-call | flops 12000000000 | bytes 23068672 | tf_op jit(solution)/shard_map/unhidden/pallas_call | solution.py:596
  116.0 3.2 %collective-permute-done.21.refs_5_ = bf16[2,128,1024]{2,1,0:T(8,128)(2,1)S(1)} collective-permute-done((bf16[2,128,1024]{2,1,0:T(8,128)(2,1)}, bf16[2,128,1024]{2,1,0:T(8,128)(2,1)S(1)}, u32[]{:S(2)}, u32[]{:S(2)}) %collective-permute-start.21) | collective-permute-done | bytes 524320 | tf_op jit(solution)/shard_map/ppermute | solution.py:777
  120.1 3.4 %join_project.1 = (bf16[1024,768]{1,0:T(8,128)(2,1)}, bf16[256,1024]{1,0:T(8,128)(2,1)}, f32[1,768]{1,0:T(1,128)}) custom-call(s32[1]{0:T(128)} %bitcast.7.place_ref, bf16[128,1024]{1,0:T(8,128)(2,1)} %get-tuple-element.144.refs_0_, bf16[128,1024]{1,0:T(8,128)(2,1)} %copy-done.32, bf16[128,1024]{1,0:T(8,128)(2,1)} %copy-done.19, ...), custom_call_target="tpu_custom_call" | custom-call | flops 1000000000 | bytes 10485760 | tf_op jit(solution)/shard_map/join_project/pallas_call | solution.py:143
  123.4 22.6 %attention.2 = (bf16[2,512,256]{2,1,0:T(8,128)(2,1)}, bf16[2,512,768]{2,1,0:T(8,128)(2,1)}, f32[1,768]{1,0:T(1,128)}) custom-call(s32[1]{0:T(128)} %bitcast.core_ref, bf16[2,512,1024]{2,1,0:T(8,128)(2,1)} %collective-permute-done.2.c_ref.first_ref, bf16[2,512,1024]{2,1,0:T(8,128)(2,1)} %collective-permute-done.15.d_ref.second_ref, ...), custom_call_target="tpu_custom_call" | custom-call | flops 23000000512 | bytes 8388608 | tf_op jit(solution)/shard_map/attention/pallas_call | solution.py:379
  148.8 10.9 %results.2 = (bf16[2,512,1024]{2,1,0:T(8,128)(2,1)}, bf16[2,512,1024]{2,1,0:T(8,128)(2,1)}) custom-call(bf16[2,512,256]{2,1,0:T(8,128)(2,1)} %get-tuple-element.156.mixed_ref.mixed_two_ref, bf16[2,512,768]{2,1,0:T(8,128)(2,1)} %get-tuple-element.157.pg_ref.pg_two_ref, bf16[2048,1024]{1,0:T(8,128)(2,1)} %get-tuple-element.180.act_ref, ...), custom_call_target="tpu_custom_call" | custom-call | flops 8000000000 | bytes 16777216 | tf_op jit(solution)/shard_map/results/pallas_call | solution.py:760
  168.3 22.8 %attention.3 = (bf16[2,512,256]{2,1,0:T(8,128)(2,1)}, bf16[2,512,768]{2,1,0:T(8,128)(2,1)}, f32[1,768]{1,0:T(1,128)}) custom-call(s32[1]{0:T(128)} %bitcast.core_ref, bf16[2,512,1024]{2,1,0:T(8,128)(2,1)} %get-tuple-element.126.a_ref.first_ref, bf16[2,512,1024]{2,1,0:T(8,128)(2,1)} %collective-permute-done.16.b_ref.second_ref, ...), custom_call_target="tpu_custom_call" | custom-call | flops 23000000512 | bytes 8388608 | tf_op jit(solution)/shard_map/attention/pallas_call | solution.py:379
  191.8 4.6 %add_convert_fusion = bf16[2,512,1024]{2,1,0:T(8,128)(2,1)} fusion(bf16[2,512,1024]{2,1,0:T(8,128)(2,1)} %collective-permute-done.24, bf16[2,512,1024]{2,1,0:T(8,128)(2,1)} %get-tuple-element.162), kind=kLoop, calls=%fused_computation | loop fusion | flops 4194304 | bytes 6291456 | tf_op jit(solution)/shard_map/convert_element_type | solution.py:1158
  200.5 9.2 %attention_grads.1 = (bf16[2,128,1024]{2,1,0:T(8,128)(2,1)}, bf16[2,128,1024]{2,1,0:T(8,128)(2,1)}, bf16[4,128,1024]{2,1,0:T(8,128)(2,1)}) custom-call(s32[1]{0:T(128)} %bitcast.7.place_ref, bf16[2,512,1024]{2,1,0:T(8,128)(2,1)} %get-tuple-element.126.a_ref.first_ref, bf16[2,512,1024]{2,1,0:T(8,128)(2,1)} %collective-permute-done.16.b_ref.second_ref, ...), custom_call_target="tpu_custom_call" | custom-call | flops 7000000000 | bytes 16777216 | tf_op jit(solution)/shard_map/attention_grads/pallas_call | solution.py:679
  214.0 3.2 %collective-permute-done.33 = f32[1,2816]{1,0:T(1,128)S(1)} collective-permute-done((f32[1,2816]{1,0:T(1,128)S(1)}, f32[1,2816]{1,0:T(1,128)S(1)}, u32[]{:S(2)}, u32[]{:S(2)}) %collective-permute-start.33) | collective-permute-done | bytes 11296 | tf_op jit(solution)/shard_map/ppermute | solution.py:777
  222.0 10.9 %results.3 = (bf16[2,512,1024]{2,1,0:T(8,128)(2,1)}, bf16[2,512,1024]{2,1,0:T(8,128)(2,1)}) custom-call(bf16[2,512,256]{2,1,0:T(8,128)(2,1)} %get-tuple-element.170.mixed_one_ref.mixed_ref, bf16[2,512,768]{2,1,0:T(8,128)(2,1)} %get-tuple-element.177.pg_one_ref.pg_ref, bf16[2048,1024]{1,0:T(8,128)(2,1)} %get-tuple-element.180.act_ref, ...), custom_call_target="tpu_custom_call" | custom-call | flops 8000000000 | bytes 16777216 | tf_op jit(solution)/shard_map/results/pallas_call | solution.py:760
  237.5 4.1 %collective-permute-done.36.late_ref = bf16[2,128,1024]{2,1,0:T(8,128)(2,1)S(1)} collective-permute-done((bf16[2,128,1024]{2,1,0:T(8,128)(2,1)}, bf16[2,128,1024]{2,1,0:T(8,128)(2,1)S(1)}, u32[]{:S(2)}, u32[]{:S(2)}) %collective-permute-start.36) | collective-permute-done | bytes 524320 | tf_op jit(solution)/shard_map/ppermute | solution.py:777
  253.2 5.9 %finish_tokens.1 = (bf16[512,1024]{1,0:T(8,128)(2,1)}, bf16[512,1024]{1,0:T(8,128)(2,1)}) custom-call(bf16[2,512,1024]{2,1,0:T(8,128)(2,1)} %get-tuple-element.191.mine_ref, bf16[2,512,1024]{2,1,0:T(8,128)(2,1)} %copy-done.3, bf16[2,512,1024]{2,1,0:T(8,128)(2,1)} %collective-permute-done.25.far_ref, bf16[512,1024]{1,0:T(8,128)(2,1)} %inputs_ref.2, ...), custom_call_target="tpu_custom_call" | custom-call | bytes 12582912 | tf_op jit(solution)/shard_map/finish_tokens/pallas_call | solution.py:959
  259.2 3.4 %collective-permute-done.38.far_ref = bf16[128,1024]{1,0:T(8,128)(2,1)S(1)} collective-permute-done((bf16[128,1024]{1,0:T(8,128)(2,1)S(1)}, bf16[128,1024]{1,0:T(8,128)(2,1)S(1)}, u32[]{:S(2)}, u32[]{:S(2)}) %collective-permute-start.38) | collective-permute-done | bytes 262176 | tf_op jit(solution)/shard_map/ppermute | solution.py:777
  263.3 4.2 %finish_project.1 = (f32[128,768]{1,0:T(8,128)}, f32[32,1024]{1,0:T(8,128)}, f32[2,128]{1,0:T(2,128)}) custom-call(bf16[4,128,1024]{2,1,0:T(8,128)(2,1)} %get-tuple-element.187.own_ref, bf16[2,128,1024]{2,1,0:T(8,128)(2,1)} %copy-done.5, bf16[2,128,1024]{2,1,0:T(8,128)(2,1)} %copy-done.6, bf16[128,1024]{1,0:T(8,128)(2,1)} %copy-done.16, ...), custom_call_target="tpu_custom_call" | custom-call | bytes 4194304 | tf_op jit(solution)/shard_map/finish_project/pallas_call | solution.py:894
  (215 shorter events, 97.8 us)
Async XLA Ops:
  0.7 21.8 %collective-permute-start.5 = (bf16[128,1024]{1,0:T(8,128)(2,1)}, bf16[128,1024]{1,0:T(8,128)(2,1)S(1)}, u32[]{:S(2)}, u32[]{:S(2)}) collective-permute-start(bf16[128,1024]{1,0:T(8,128)(2,1)} %w_ref.2), channel_id=1, source_target_pairs={{0,16},{4,20},{8,24},{12,28},{16,0},{20,4},{24,8},{28,12},{1,17},{... | collective-permute-start | bytes 786440 | tf_op jit(solution)/shard_map/ppermute | solution.py:777
  16.6 49.0 %collective-permute-start.2 = (bf16[2,512,1024]{2,1,0:T(8,128)(2,1)}, bf16[2,512,1024]{2,1,0:T(8,128)(2,1)}, u32[]{:S(2)}, u32[]{:S(2)}) collective-permute-start(bf16[2,512,1024]{2,1,0:T(8,128)(2,1)} %get-tuple-element.126.a_ref.first_ref), channel_id=1, source_target_pairs={{0,2},{1,3},{2,0},{3,1},{4,6},{5,7},{6,4},{7,5},{8,10},{9,11},{10,... | collective-permute-start | bytes 6291464 | tf_op jit(solution)/shard_map/ppermute | solution.py:777
  31.3 17.1 %collective-permute-start.9 = (bf16[2,128,1024]{2,1,0:T(8,128)(2,1)S(1)}, bf16[2,128,1024]{2,1,0:T(8,128)(2,1)S(1)}, u32[]{:S(2)}, u32[]{:S(2)}) collective-permute-start(bf16[2,128,1024]{2,1,0:T(8,128)(2,1)S(1)} %pad_maximum_fusion), channel_id=1, source_target_pairs={{0,8},{4,12},{8,0},{12,4},{16,24},{20,28},{24,16},{28,20},{1,9},{5... | collective-permute-start | bytes 1572872 | tf_op jit(solution)/shard_map/ppermute | solution.py:777
  34.7 13.7 %collective-permute-start.11 = (bf16[128,1024]{1,0:T(8,128)(2,1)S(1)}, bf16[128,1024]{1,0:T(8,128)(2,1)S(1)}, u32[]{:S(2)}, u32[]{:S(2)}) collective-permute-start(bf16[128,1024]{1,0:T(8,128)(2,1)S(1)} %copy-done.9), channel_id=1, source_target_pairs={{0,4},{4,0},{8,12},{12,8},{16,20},{20,16},{24,28},{28,24},{1,5},{5... | collective-permute-start | bytes 786440 | tf_op jit(solution)/shard_map/ppermute | solution.py:777
  35.2 13.2 %collective-permute-start.8 = (bf16[128,1024]{1,0:T(8,128)(2,1)S(1)}, bf16[128,1024]{1,0:T(8,128)(2,1)S(1)}, u32[]{:S(2)}, u32[]{:S(2)}) collective-permute-start(bf16[128,1024]{1,0:T(8,128)(2,1)S(1)} %copy-done.9), channel_id=1, source_target_pairs={{0,16},{4,20},{8,24},{12,28},{16,0},{20,4},{24,8},{28,12},{1,17},{... | collective-permute-start | bytes 786440 | tf_op jit(solution)/shard_map/ppermute | solution.py:777
  41.3 34.0 %collective-permute-start.16 = (bf16[2,512,1024]{2,1,0:T(8,128)(2,1)}, bf16[2,512,1024]{2,1,0:T(8,128)(2,1)}, u32[]{:S(2)}, u32[]{:S(2)}) collective-permute-start(bf16[2,512,1024]{2,1,0:T(8,128)(2,1)} %get-tuple-element.126.a_ref.first_ref), channel_id=1, source_target_pairs={{0,1},{1,0},{2,3},{3,2},{4,5},{5,4},{6,7},{7,6},{8,9},{9,8},{10,11... | collective-permute-start | bytes 6291464 | tf_op jit(solution)/shard_map/ppermute | solution.py:777
  50.5 15.1 %collective-permute-start.12 = (bf16[2,128,1024]{2,1,0:T(8,128)(2,1)S(1)}, bf16[2,128,1024]{2,1,0:T(8,128)(2,1)S(1)}, u32[]{:S(2)}, u32[]{:S(2)}) collective-permute-start(bf16[2,128,1024]{2,1,0:T(8,128)(2,1)S(1)} %pad_maximum_fusion.1), channel_id=1, source_target_pairs={{0,8},{4,12},{8,0},{12,4},{16,24},{20,28},{24,16},{28,20},{1,9},{5... | collective-permute-start | bytes 1572872 | tf_op jit(solution)/shard_map/ppermute | solution.py:777
  50.7 13.8 %collective-permute-start.13 = (bf16[128,1024]{1,0:T(8,128)(2,1)}, bf16[128,1024]{1,0:T(8,128)(2,1)S(1)}, u32[]{:S(2)}, u32[]{:S(2)}) collective-permute-start(bf16[128,1024]{1,0:T(8,128)(2,1)} %get-tuple-element.144.refs_0_), channel_id=1, source_target_pairs={{0,16},{4,20},{8,24},{12,28},{16,0},{20,4},{24,8},{28,12},{1,17},{... | collective-permute-start | bytes 786440 | tf_op jit(solution)/shard_map/ppermute | solution.py:777
  69.1 24.0 %collective-permute-start.20 = (bf16[2,128,1024]{2,1,0:T(8,128)(2,1)S(1)}, bf16[2,128,1024]{2,1,0:T(8,128)(2,1)}, u32[]{:S(2)}, u32[]{:S(2)}) collective-permute-start(bf16[2,128,1024]{2,1,0:T(8,128)(2,1)S(1)} %pad_maximum_fusion.2), channel_id=1, source_target_pairs={{0,8},{4,12},{8,0},{12,4},{16,24},{20,28},{24,16},{28,20},{1,9},{5... | collective-permute-start | bytes 1572872 | tf_op jit(solution)/shard_map/ppermute | solution.py:777
  75.3 17.8 %collective-permute-start.22 = (bf16[2,128,1024]{2,1,0:T(8,128)(2,1)S(1)}, bf16[2,128,1024]{2,1,0:T(8,128)(2,1)S(1)}, u32[]{:S(2)}, u32[]{:S(2)}) collective-permute-start(bf16[2,128,1024]{2,1,0:T(8,128)(2,1)S(1)} %collective-permute-done.12.refs_4_), channel_id=1, source_target_pairs={{0,4},{4,0},{8,12},{12,8},{16,20},{20,16},{24,28},{28,24},{1,5},{5... | collective-permute-start | bytes 1572872 | tf_op jit(solution)/shard_map/ppermute | solution.py:777
  93.1 22.9 %collective-permute-start.18 = (bf16[128,1024]{1,0:T(8,128)(2,1)S(1)}, bf16[128,1024]{1,0:T(8,128)(2,1)S(1)}, u32[]{:S(2)}, u32[]{:S(2)}) collective-permute-start(bf16[128,1024]{1,0:T(8,128)(2,1)S(1)} %copy-done.17), channel_id=1, source_target_pairs={{0,4},{4,0},{8,12},{12,8},{16,20},{20,16},{24,28},{28,24},{1,5},{5... | collective-permute-start | bytes 786440 | tf_op jit(solution)/shard_map/ppermute | solution.py:777
  94.1 21.9 %collective-permute-start.19 = (bf16[128,1024]{1,0:T(8,128)(2,1)S(1)}, bf16[128,1024]{1,0:T(8,128)(2,1)S(1)}, u32[]{:S(2)}, u32[]{:S(2)}) collective-permute-start(bf16[128,1024]{1,0:T(8,128)(2,1)S(1)} %collective-permute-done.13.refs_2_), channel_id=1, source_target_pairs={{0,4},{4,0},{8,12},{12,8},{16,20},{20,16},{24,28},{28,24},{1,5},{5... | collective-permute-start | bytes 786440 | tf_op jit(solution)/shard_map/ppermute | solution.py:777
  95.2 24.1 %collective-permute-start.21 = (bf16[2,128,1024]{2,1,0:T(8,128)(2,1)}, bf16[2,128,1024]{2,1,0:T(8,128)(2,1)S(1)}, u32[]{:S(2)}, u32[]{:S(2)}) collective-permute-start(bf16[2,128,1024]{2,1,0:T(8,128)(2,1)} %collective-permute-done.20.refs_4_), channel_id=1, source_target_pairs={{0,4},{4,0},{8,12},{12,8},{16,20},{20,16},{24,28},{28,24},{1,5},{5... | collective-permute-start | bytes 1572872 | tf_op jit(solution)/shard_map/ppermute | solution.py:777
  96.1 49.9 %collective-permute-start.23 = (bf16[4,128,1024]{2,1,0:T(8,128)(2,1)}, bf16[4,128,1024]{2,1,0:T(8,128)(2,1)S(1)}, u32[]{:S(2)}, u32[]{:S(2)}) collective-permute-start(bf16[4,128,1024]{2,1,0:T(8,128)(2,1)} %get-tuple-element.159), channel_id=1, source_target_pairs={{0,4},{4,0},{8,12},{12,8},{16,20},{20,16},{24,28},{28,24},{1,5},{5... | collective-permute-start | bytes 3145736 | tf_op jit(solution)/shard_map/ppermute | solution.py:777
  115.0 47.7 %collective-permute-start.27 = (bf16[4,128,1024]{2,1,0:T(8,128)(2,1)}, bf16[4,128,1024]{2,1,0:T(8,128)(2,1)S(1)}, u32[]{:S(2)}, u32[]{:S(2)}) collective-permute-start(bf16[4,128,1024]{2,1,0:T(8,128)(2,1)} %get-tuple-element.168), channel_id=1, source_target_pairs={{0,4},{4,0},{8,12},{12,8},{16,20},{20,16},{24,28},{28,24},{1,5},{5... | collective-permute-start | bytes 3145736 | tf_op jit(solution)/shard_map/ppermute | solution.py:777
  147.2 18.2 %collective-permute-start.26 = (bf16[2,128,1024]{2,1,0:T(8,128)(2,1)}, bf16[2,128,1024]{2,1,0:T(8,128)(2,1)}, u32[]{:S(2)}, u32[]{:S(2)}) collective-permute-start(bf16[2,128,1024]{2,1,0:T(8,128)(2,1)} %add_convert_fusion.3), channel_id=1, source_target_pairs={{0,8},{4,12},{8,0},{12,4},{16,24},{20,28},{24,16},{28,20},{1,9},{5... | collective-permute-start | bytes 1572872 | tf_op jit(solution)/shard_map/ppermute | solution.py:777
  163.9 33.6 %collective-permute-start.28 = (bf16[2,128,1024]{2,1,0:T(8,128)(2,1)}, bf16[2,128,1024]{2,1,0:T(8,128)(2,1)S(1)}, u32[]{:S(2)}, u32[]{:S(2)}) collective-permute-start(bf16[2,128,1024]{2,1,0:T(8,128)(2,1)} %add_convert_fusion.2), channel_id=1, source_target_pairs={{0,8},{4,12},{8,0},{12,4},{16,24},{20,28},{24,16},{28,20},{1,9},{5... | collective-permute-start | bytes 1572872 | tf_op jit(solution)/shard_map/ppermute | solution.py:777
  165.5 26.4 %collective-permute-start.24 = (bf16[2,512,1024]{2,1,0:T(8,128)(2,1)}, bf16[2,512,1024]{2,1,0:T(8,128)(2,1)}, u32[]{:S(2)}, u32[]{:S(2)}) collective-permute-start(bf16[2,512,1024]{2,1,0:T(8,128)(2,1)} %get-tuple-element.163), channel_id=1, source_target_pairs={{0,1},{1,0},{2,3},{3,2},{4,5},{5,4},{6,7},{7,6},{8,9},{9,8},{10,11... | collective-permute-start | bytes 6291464 | tf_op jit(solution)/shard_map/ppermute | solution.py:777
  167.3 30.2 %collective-permute-start.29 = (bf16[128,1024]{1,0:T(8,128)(2,1)}, bf16[128,1024]{1,0:T(8,128)(2,1)S(1)}, u32[]{:S(2)}, u32[]{:S(2)}) collective-permute-start(bf16[128,1024]{1,0:T(8,128)(2,1)} %fusion), channel_id=1, source_target_pairs={{0,16},{4,20},{8,24},{12,28},{16,0},{20,4},{24,8},{28,12},{1,17},{... | collective-permute-start | bytes 786440 | tf_op jit(solution)/shard_map/ppermute | solution.py:777
  196.4 48.1 %collective-permute-start.25 = (bf16[2,512,1024]{2,1,0:T(8,128)(2,1)}, bf16[2,512,1024]{2,1,0:T(8,128)(2,1)}, u32[]{:S(2)}, u32[]{:S(2)}) collective-permute-start(bf16[2,512,1024]{2,1,0:T(8,128)(2,1)} %add_convert_fusion), channel_id=1, source_target_pairs={{0,2},{1,3},{2,0},{3,1},{4,6},{5,7},{6,4},{7,5},{8,10},{9,11},{10,... | collective-permute-start | bytes 6291464 | tf_op jit(solution)/shard_map/ppermute | solution.py:777
  198.3 23.6 %collective-permute-start.30 = (bf16[128,1024]{1,0:T(8,128)(2,1)}, bf16[128,1024]{1,0:T(8,128)(2,1)}, u32[]{:S(2)}, u32[]{:S(2)}) collective-permute-start(bf16[128,1024]{1,0:T(8,128)(2,1)} %fusion.1), channel_id=1, source_target_pairs={{0,16},{4,20},{8,24},{12,28},{16,0},{20,4},{24,8},{28,12},{1,17},{... | collective-permute-start | bytes 786440 | tf_op jit(solution)/shard_map/ppermute | solution.py:777
  218.1 15.1 %collective-permute-start.31 = (bf16[2,128,1024]{2,1,0:T(8,128)(2,1)}, bf16[2,128,1024]{2,1,0:T(8,128)(2,1)S(1)}, u32[]{:S(2)}, u32[]{:S(2)}) collective-permute-start(bf16[2,128,1024]{2,1,0:T(8,128)(2,1)} %get-tuple-element.183), channel_id=1, source_target_pairs={{0,4},{4,0},{8,12},{12,8},{16,20},{20,16},{24,28},{28,24},{1,5},{5... | collective-permute-start | bytes 1572872 | tf_op jit(solution)/shard_map/ppermute | solution.py:777
  219.6 22.0 %collective-permute-start.36 = (bf16[2,128,1024]{2,1,0:T(8,128)(2,1)}, bf16[2,128,1024]{2,1,0:T(8,128)(2,1)S(1)}, u32[]{:S(2)}, u32[]{:S(2)}) collective-permute-start(bf16[2,128,1024]{2,1,0:T(8,128)(2,1)} %get-tuple-element.189), channel_id=1, source_target_pairs={{0,4},{4,0},{8,12},{12,8},{16,20},{20,16},{24,28},{28,24},{1,5},{5... | collective-permute-start | bytes 1572872 | tf_op jit(solution)/shard_map/ppermute | solution.py:777
  247.3 15.3 %collective-permute-start.38 = (bf16[128,1024]{1,0:T(8,128)(2,1)S(1)}, bf16[128,1024]{1,0:T(8,128)(2,1)S(1)}, u32[]{:S(2)}, u32[]{:S(2)}) collective-permute-start(bf16[128,1024]{1,0:T(8,128)(2,1)S(1)} %fusion.2), channel_id=1, source_target_pairs={{0,16},{4,20},{8,24},{12,28},{16,0},{20,4},{24,8},{28,12},{1,17},{... | collective-permute-start | bytes 786440 | tf_op jit(solution)/shard_map/ppermute | solution.py:777
  (53 other events, 607.4 us)

commit v5 on v4

--- a/solution.py
+++ b/solution.py
@@ -369,7 +369,7 @@
             mixed_ref[piece, :, sl] = out_s[pl.ds(starts(piece), half_rows), :]
         return carry
 
-    lax.fori_loop(0, width // 128, pair, 0)
+    lax.fori_loop(0, width // 128, pair, 0, unroll=True)
 
 
 def attention(core, parts, w, b, dense, marks, tables):

time: 279 us -> 278 us (level)
  no operation moved by 1% of the time
where the time goes in v5:
time: 278 us; the launch traced here: 274 us
  Pallas kernels  137 us (49%)
  waiting for transfers between devices  56.4 us (20%)
  starting transfers between devices  47.7 us (17%)
  other arithmetic  17.1 us (6%)
  local copies, waits for them, and re-layouts  14.7 us (5%)
    ppermute x41, waiting for transfers between devices, exchange(): return lax.ppermute(value, axis, [(i, i ^ offset) for i in range(size)])  56.4 us
    ppermute x41, starting transfers between devices, exchange(): return lax.ppermute(value, axis, [(i, i ^ offset) for i in range(size)])  47.7 us
    pallas_call x2, Pallas kernels, attention(): pl.pallas_call(attention_kernel, in_specs=[SMEM] + [VMEM] * 9, out_specs=...  44.7 us
    pallas_call x2, Pallas kernels, results(): pl.pallas_call(functools.partial(results_kernel, first=first), in_specs=[...  21.8 us
    pallas_call x1, Pallas kernels, hidden_layer(): pl.pallas_call(hidden_kernel, in_specs=[SMEM] + [ANY] * 5 + [VMEM], out_s...  16.7 us
    pallas_call x1, Pallas kernels, unhidden_layer(): pl.pallas_call(unhidden_kernel, in_specs=[SMEM] + [ANY] * 6, out_specs=[A...  14.7 us
    pallas_call x1, Pallas kernels, attention_grads(): pl.pallas_call(attention_grads_kernel, in_specs=[SMEM] + [ANY] * 8, out_s...  9.25 us
    pallas_call x1, Pallas kernels, finish_tokens(): pl.pallas_call(finish_tokens_kernel, grid=(4,), in_specs=[both] * 3 + [bl...  5.94 us
  transfers between devices with their start and end apart: 41, of which 23 were waited for; matrix products, arithmetic and copies ran while one was open for 9% of the time, Pallas kernels for 48%

profile of v5, /device:TPU:0, one launch (start us, length us, event | category | flops | bytes accessed | tf_op | source)
XLA Modules:
  0.0 273.8 jit_solution(9320656758254953770)
XLA Ops:
  0.7 4.1 %collective-permute-start.5 = (bf16[128,1024]{1,0:T(8,128)(2,1)}, bf16[128,1024]{1,0:T(8,128)(2,1)S(1)}, u32[]{:S(2)}, u32[]{:S(2)}) collective-permute-start(bf16[128,1024]{1,0:T(8,128)(2,1)} %w_ref.2), channel_id=1, source_target_pairs={{0,16},{4,20},{8,24},{12,28},{16,0},{20,4},{24,8},{28,12},{1,17},{... | collective-permute-start | bytes 786440 | tf_op jit(solution)/shard_map/ppermute | solution.py:777
  12.8 3.9 %prepare.1 = (bf16[2,512,1024]{2,1,0:T(8,128)(2,1)}, f32[1,1024]{1,0:T(1,128)}) custom-call(bf16[512,1024]{1,0:T(8,128)(2,1)} %inputs_ref.2, bf16[512,1024]{1,0:T(8,128)(2,1)} %cotangent_ref.3, f32[512,1]{1,0:T(8,128)} %copy.40.keep_ref), custom_call_target="tpu_custom_call" | custom-call | bytes 6291456 | tf_op jit(solution)/shard_map/prepare/pallas_call | solution.py:216
  22.9 4.4 %collective-permute-done.6 = f32[8,864]{1,0:T(8,128)S(1)} collective-permute-done((f32[8,864]{1,0:T(8,128)S(1)}, f32[8,864]{1,0:T(8,128)S(1)}, u32[]{:S(2)}, u32[]{:S(2)}) %collective-permute-start.6) | collective-permute-done | bytes 27680 | tf_op jit(solution)/shard_map/ppermute | solution.py:777
  37.4 3.9 %collective-permute-done.10.refs_3_ = bf16[128,1024]{1,0:T(8,128)(2,1)S(1)} collective-permute-done((bf16[128,1024]{1,0:T(8,128)(2,1)S(1)}, bf16[128,1024]{1,0:T(8,128)(2,1)S(1)}, u32[]{:S(2)}, u32[]{:S(2)}) %collective-permute-start.10) | collective-permute-done | bytes 262176 | tf_op jit(solution)/shard_map/ppermute | solution.py:777
  44.3 4.1 %collective-permute-done.9.refs_4_ = bf16[2,128,1024]{2,1,0:T(8,128)(2,1)S(1)} collective-permute-done((bf16[2,128,1024]{2,1,0:T(8,128)(2,1)S(1)}, bf16[2,128,1024]{2,1,0:T(8,128)(2,1)S(1)}, u32[]{:S(2)}, u32[]{:S(2)}) %collective-permute-start.9) | collective-permute-done | bytes 524320 | tf_op jit(solution)/shard_map/ppermute | solution.py:777
  50.7 3.1 %collective-permute-start.13 = (bf16[128,1024]{1,0:T(8,128)(2,1)}, bf16[128,1024]{1,0:T(8,128)(2,1)S(1)}, u32[]{:S(2)}, u32[]{:S(2)}) collective-permute-start(bf16[128,1024]{1,0:T(8,128)(2,1)} %get-tuple-element.144.refs_0_), channel_id=1, source_target_pairs={{0,16},{4,20},{8,24},{12,28},{16,0},{20,4},{24,8},{28,12},{1,17},{... | collective-permute-start | bytes 786440 | tf_op jit(solution)/shard_map/ppermute | solution.py:777
  54.4 4.2 %collective-permute-done.14.refs_5_ = bf16[2,128,1024]{2,1,0:T(8,128)(2,1)S(1)} collective-permute-done((bf16[2,128,1024]{2,1,0:T(8,128)(2,1)S(1)}, bf16[2,128,1024]{2,1,0:T(8,128)(2,1)S(1)}, u32[]{:S(2)}, u32[]{:S(2)}) %collective-permute-start.14) | collective-permute-done | bytes 524320 | tf_op jit(solution)/shard_map/ppermute | solution.py:777
  59.4 3.6 %join_expand.1 = (bf16[1024,1024]{1,0:T(8,128)(2,1)}, f32[1,1024]{1,0:T(1,128)}) custom-call(s32[1]{0:T(128)} %bitcast.7.place_ref, bf16[128,1024]{1,0:T(8,128)(2,1)} %w_ref.2, bf16[128,1024]{1,0:T(8,128)(2,1)} %copy-done.30, bf16[128,1024]{1,0:T(8,128)(2,1)} %copy-done.18, bf16[128,1024]{1,0:T(8,128)(2,1)} %copy-done.31, bf16[2,128,1024]{2,1,0:T(8,128)(2,1)} %copy-done.27, ...), custom_call_target="tpu_custom_call" | custom-call | flops 1000000000 | bytes 6291456 | tf_op jit(solution)/shard_map/join_expand/pallas_call | solution.py:170
  70.4 4.5 %collective-permute-done.17.refs_3_ = bf16[128,1024]{1,0:T(8,128)(2,1)S(1)} collective-permute-done((bf16[128,1024]{1,0:T(8,128)(2,1)S(1)}, bf16[128,1024]{1,0:T(8,128)(2,1)S(1)}, u32[]{:S(2)}, u32[]{:S(2)}) %collective-permute-start.17) | collective-permute-done | bytes 262176 | tf_op jit(solution)/shard_map/ppermute | solution.py:777
  76.0 16.7 %hidden.1 = (bf16[2048,1024]{1,0:T(8,128)(2,1)}, bf16[2048,1024]{1,0:T(8,128)(2,1)}, bf16[4,128,1024]{2,1,0:T(8,128)(2,1)}, bf16[4,128,1024]{2,1,0:T(8,128)(2,1)}) custom-call(s32[1]{0:T(128)} %bitcast.7.place_ref, bf16[2,512,1024]{2,1,0:T(8,128)(2,1)} %get-tuple-element.126.a_ref.first_ref, bf16[2,512,1024]{2,1,0:T(8,128)(2,1)} %collective-permute-done.16.b_ref.second_ref, ...), custom_call_target="tpu_custom_call" | custom-call | flops 12000000000 | bytes 20971520 | tf_op jit(solution)/shard_map/hidden/pallas_call | solution.py:515
  99.9 14.7 %unhidden.1 = (bf16[2048,1024]{1,0:T(8,128)(2,1)}, bf16[4,128,1024]{2,1,0:T(8,128)(2,1)}, bf16[4,128,1024]{2,1,0:T(8,128)(2,1)}, f32[1,1024]{1,0:T(1,128)}) custom-call(s32[1]{0:T(128)} %bitcast.7.place_ref, bf16[2,512,1024]{2,1,0:T(8,128)(2,1)} %get-tuple-element.126.a_ref.first_ref, bf16[2,512,1024]{2,1,0:T(8,128)(2,1)} %collective-permute-done.16.b_ref.second_ref, ...), custom_call_target="tpu_custom_call" | custom-call | flops 12000000000 | bytes 23068672 | tf_op jit(solution)/shard_map/unhidden/pallas_call | solution.py:596
  115.7 3.2 %collective-permute-done.21.refs_5_ = bf16[2,128,1024]{2,1,0:T(8,128)(2,1)S(1)} collective-permute-done((bf16[2,128,1024]{2,1,0:T(8,128)(2,1)}, bf16[2,128,1024]{2,1,0:T(8,128)(2,1)S(1)}, u32[]{:S(2)}, u32[]{:S(2)}) %collective-permute-start.21) | collective-permute-done | bytes 524320 | tf_op jit(solution)/shard_map/ppermute | solution.py:777
  119.7 3.4 %join_project.1 = (bf16[1024,768]{1,0:T(8,128)(2,1)}, bf16[256,1024]{1,0:T(8,128)(2,1)}, f32[1,768]{1,0:T(1,128)}) custom-call(s32[1]{0:T(128)} %bitcast.7.place_ref, bf16[128,1024]{1,0:T(8,128)(2,1)} %get-tuple-element.144.refs_0_, bf16[128,1024]{1,0:T(8,128)(2,1)} %copy-done.32, bf16[128,1024]{1,0:T(8,128)(2,1)} %copy-done.19, ...), custom_call_target="tpu_custom_call" | custom-call | flops 1000000000 | bytes 10485760 | tf_op jit(solution)/shard_map/join_project/pallas_call | solution.py:143
  123.1 22.6 %attention.2 = (bf16[2,512,256]{2,1,0:T(8,128)(2,1)}, bf16[2,512,768]{2,1,0:T(8,128)(2,1)}, f32[1,768]{1,0:T(1,128)}) custom-call(s32[1]{0:T(128)} %bitcast.core_ref, bf16[2,512,1024]{2,1,0:T(8,128)(2,1)} %collective-permute-done.2.c_ref.first_ref, bf16[2,512,1024]{2,1,0:T(8,128)(2,1)} %collective-permute-done.15.d_ref.second_ref, ...), custom_call_target="tpu_custom_call" | custom-call | flops 23000000512 | bytes 8388608 | tf_op jit(solution)/shard_map/attention/pallas_call | solution.py:379
  148.5 10.9 %results.2 = (bf16[2,512,1024]{2,1,0:T(8,128)(2,1)}, bf16[2,512,1024]{2,1,0:T(8,128)(2,1)}) custom-call(bf16[2,512,256]{2,1,0:T(8,128)(2,1)} %get-tuple-element.156.mixed_ref.mixed_two_ref, bf16[2,512,768]{2,1,0:T(8,128)(2,1)} %get-tuple-element.157.pg_ref.pg_two_ref, bf16[2048,1024]{1,0:T(8,128)(2,1)} %get-tuple-element.180.act_ref, ...), custom_call_target="tpu_custom_call" | custom-call | flops 8000000000 | bytes 16777216 | tf_op jit(solution)/shard_map/results/pallas_call | solution.py:760
  168.0 22.1 %attention.3 = (bf16[2,512,256]{2,1,0:T(8,128)(2,1)}, bf16[2,512,768]{2,1,0:T(8,128)(2,1)}, f32[1,768]{1,0:T(1,128)}) custom-call(s32[1]{0:T(128)} %bitcast.core_ref, bf16[2,512,1024]{2,1,0:T(8,128)(2,1)} %get-tuple-element.126.a_ref.first_ref, bf16[2,512,1024]{2,1,0:T(8,128)(2,1)} %collective-permute-done.16.b_ref.second_ref, ...), custom_call_target="tpu_custom_call" | custom-call | flops 23000000512 | bytes 8388608 | tf_op jit(solution)/shard_map/attention/pallas_call | solution.py:379
  190.8 4.6 %add_convert_fusion = bf16[2,512,1024]{2,1,0:T(8,128)(2,1)} fusion(bf16[2,512,1024]{2,1,0:T(8,128)(2,1)} %collective-permute-done.24, bf16[2,512,1024]{2,1,0:T(8,128)(2,1)} %get-tuple-element.162), kind=kLoop, calls=%fused_computation | loop fusion | flops 4194304 | bytes 6291456 | tf_op jit(solution)/shard_map/convert_element_type | solution.py:1158
  199.5 9.2 %attention_grads.1 = (bf16[2,128,1024]{2,1,0:T(8,128)(2,1)}, bf16[2,128,1024]{2,1,0:T(8,128)(2,1)}, bf16[4,128,1024]{2,1,0:T(8,128)(2,1)}) custom-call(s32[1]{0:T(128)} %bitcast.7.place_ref, bf16[2,512,1024]{2,1,0:T(8,128)(2,1)} %get-tuple-element.126.a_ref.first_ref, bf16[2,512,1024]{2,1,0:T(8,128)(2,1)} %collective-permute-done.16.b_ref.second_ref, ...), custom_call_target="tpu_custom_call" | custom-call | flops 7000000000 | bytes 16777216 | tf_op jit(solution)/shard_map/attention_grads/pallas_call | solution.py:679
  213.0 3.2 %collective-permute-done.33 = f32[1,2816]{1,0:T(1,128)S(1)} collective-permute-done((f32[1,2816]{1,0:T(1,128)S(1)}, f32[1,2816]{1,0:T(1,128)S(1)}, u32[]{:S(2)}, u32[]{:S(2)}) %collective-permute-start.33) | collective-permute-done | bytes 11296 | tf_op jit(solution)/shard_map/ppermute | solution.py:777
  221.0 10.9 %results.3 = (bf16[2,512,1024]{2,1,0:T(8,128)(2,1)}, bf16[2,512,1024]{2,1,0:T(8,128)(2,1)}) custom-call(bf16[2,512,256]{2,1,0:T(8,128)(2,1)} %get-tuple-element.170.mixed_one_ref.mixed_ref, bf16[2,512,768]{2,1,0:T(8,128)(2,1)} %get-tuple-element.177.pg_one_ref.pg_ref, bf16[2048,1024]{1,0:T(8,128)(2,1)} %get-tuple-element.180.act_ref, ...), custom_call_target="tpu_custom_call" | custom-call | flops 8000000000 | bytes 16777216 | tf_op jit(solution)/shard_map/results/pallas_call | solution.py:760
  236.4 4.1 %collective-permute-done.36.late_ref = bf16[2,128,1024]{2,1,0:T(8,128)(2,1)S(1)} collective-permute-done((bf16[2,128,1024]{2,1,0:T(8,128)(2,1)}, bf16[2,128,1024]{2,1,0:T(8,128)(2,1)S(1)}, u32[]{:S(2)}, u32[]{:S(2)}) %collective-permute-start.36) | collective-permute-done | bytes 524320 | tf_op jit(solution)/shard_map/ppermute | solution.py:777
  252.2 5.9 %finish_tokens.1 = (bf16[512,1024]{1,0:T(8,128)(2,1)}, bf16[512,1024]{1,0:T(8,128)(2,1)}) custom-call(bf16[2,512,1024]{2,1,0:T(8,128)(2,1)} %get-tuple-element.191.mine_ref, bf16[2,512,1024]{2,1,0:T(8,128)(2,1)} %copy-done.3, bf16[2,512,1024]{2,1,0:T(8,128)(2,1)} %collective-permute-done.25.far_ref, bf16[512,1024]{1,0:T(8,128)(2,1)} %inputs_ref.2, ...), custom_call_target="tpu_custom_call" | custom-call | bytes 12582912 | tf_op jit(solution)/shard_map/finish_tokens/pallas_call | solution.py:959
  258.2 3.4 %collective-permute-done.38.far_ref = bf16[128,1024]{1,0:T(8,128)(2,1)S(1)} collective-permute-done((bf16[128,1024]{1,0:T(8,128)(2,1)S(1)}, bf16[128,1024]{1,0:T(8,128)(2,1)S(1)}, u32[]{:S(2)}, u32[]{:S(2)}) %collective-permute-start.38) | collective-permute-done | bytes 262176 | tf_op jit(solution)/shard_map/ppermute | solution.py:777
  262.3 4.2 %finish_project.1 = (f32[128,768]{1,0:T(8,128)}, f32[32,1024]{1,0:T(8,128)}, f32[2,128]{1,0:T(2,128)}) custom-call(bf16[4,128,1024]{2,1,0:T(8,128)(2,1)} %get-tuple-element.187.own_ref, bf16[2,128,1024]{2,1,0:T(8,128)(2,1)} %copy-done.5, bf16[2,128,1024]{2,1,0:T(8,128)(2,1)} %copy-done.6, bf16[128,1024]{1,0:T(8,128)(2,1)} %copy-done.16, ...), custom_call_target="tpu_custom_call" | custom-call | bytes 4194304 | tf_op jit(solution)/shard_map/finish_project/pallas_call | solution.py:894
  (215 shorter events, 97.5 us)
Async XLA Ops:
  0.7 21.8 %collective-permute-start.5 = (bf16[128,1024]{1,0:T(8,128)(2,1)}, bf16[128,1024]{1,0:T(8,128)(2,1)S(1)}, u32[]{:S(2)}, u32[]{:S(2)}) collective-permute-start(bf16[128,1024]{1,0:T(8,128)(2,1)} %w_ref.2), channel_id=1, source_target_pairs={{0,16},{4,20},{8,24},{12,28},{16,0},{20,4},{24,8},{28,12},{1,17},{... | collective-permute-start | bytes 786440 | tf_op jit(solution)/shard_map/ppermute | solution.py:777
  16.6 49.0 %collective-permute-start.2 = (bf16[2,512,1024]{2,1,0:T(8,128)(2,1)}, bf16[2,512,1024]{2,1,0:T(8,128)(2,1)}, u32[]{:S(2)}, u32[]{:S(2)}) collective-permute-start(bf16[2,512,1024]{2,1,0:T(8,128)(2,1)} %get-tuple-element.126.a_ref.first_ref), channel_id=1, source_target_pairs={{0,2},{1,3},{2,0},{3,1},{4,6},{5,7},{6,4},{7,5},{8,10},{9,11},{10,... | collective-permute-start | bytes 6291464 | tf_op jit(solution)/shard_map/ppermute | solution.py:777
  31.3 17.1 %collective-permute-start.9 = (bf16[2,128,1024]{2,1,0:T(8,128)(2,1)S(1)}, bf16[2,128,1024]{2,1,0:T(8,128)(2,1)S(1)}, u32[]{:S(2)}, u32[]{:S(2)}) collective-permute-start(bf16[2,128,1024]{2,1,0:T(8,128)(2,1)S(1)} %pad_maximum_fusion), channel_id=1, source_target_pairs={{0,8},{4,12},{8,0},{12,4},{16,24},{20,28},{24,16},{28,20},{1,9},{5... | collective-permute-start | bytes 1572872 | tf_op jit(solution)/shard_map/ppermute | solution.py:777
  34.7 13.7 %collective-permute-start.11 = (bf16[128,1024]{1,0:T(8,128)(2,1)S(1)}, bf16[128,1024]{1,0:T(8,128)(2,1)S(1)}, u32[]{:S(2)}, u32[]{:S(2)}) collective-permute-start(bf16[128,1024]{1,0:T(8,128)(2,1)S(1)} %copy-done.9), channel_id=1, source_target_pairs={{0,4},{4,0},{8,12},{12,8},{16,20},{20,16},{24,28},{28,24},{1,5},{5... | collective-permute-start | bytes 786440 | tf_op jit(solution)/shard_map/ppermute | solution.py:777
  35.2 13.2 %collective-permute-start.8 = (bf16[128,1024]{1,0:T(8,128)(2,1)S(1)}, bf16[128,1024]{1,0:T(8,128)(2,1)S(1)}, u32[]{:S(2)}, u32[]{:S(2)}) collective-permute-start(bf16[128,1024]{1,0:T(8,128)(2,1)S(1)} %copy-done.9), channel_id=1, source_target_pairs={{0,16},{4,20},{8,24},{12,28},{16,0},{20,4},{24,8},{28,12},{1,17},{... | collective-permute-start | bytes 786440 | tf_op jit(solution)/shard_map/ppermute | solution.py:777
  41.3 33.6 %collective-permute-start.16 = (bf16[2,512,1024]{2,1,0:T(8,128)(2,1)}, bf16[2,512,1024]{2,1,0:T(8,128)(2,1)}, u32[]{:S(2)}, u32[]{:S(2)}) collective-permute-start(bf16[2,512,1024]{2,1,0:T(8,128)(2,1)} %get-tuple-element.126.a_ref.first_ref), channel_id=1, source_target_pairs={{0,1},{1,0},{2,3},{3,2},{4,5},{5,4},{6,7},{7,6},{8,9},{9,8},{10,11... | collective-permute-start | bytes 6291464 | tf_op jit(solution)/shard_map/ppermute | solution.py:777
  50.5 15.1 %collective-permute-start.12 = (bf16[2,128,1024]{2,1,0:T(8,128)(2,1)S(1)}, bf16[2,128,1024]{2,1,0:T(8,128)(2,1)S(1)}, u32[]{:S(2)}, u32[]{:S(2)}) collective-permute-start(bf16[2,128,1024]{2,1,0:T(8,128)(2,1)S(1)} %pad_maximum_fusion.1), channel_id=1, source_target_pairs={{0,8},{4,12},{8,0},{12,4},{16,24},{20,28},{24,16},{28,20},{1,9},{5... | collective-permute-start | bytes 1572872 | tf_op jit(solution)/shard_map/ppermute | solution.py:777
  50.7 13.8 %collective-permute-start.13 = (bf16[128,1024]{1,0:T(8,128)(2,1)}, bf16[128,1024]{1,0:T(8,128)(2,1)S(1)}, u32[]{:S(2)}, u32[]{:S(2)}) collective-permute-start(bf16[128,1024]{1,0:T(8,128)(2,1)} %get-tuple-element.144.refs_0_), channel_id=1, source_target_pairs={{0,16},{4,20},{8,24},{12,28},{16,0},{20,4},{24,8},{28,12},{1,17},{... | collective-permute-start | bytes 786440 | tf_op jit(solution)/shard_map/ppermute | solution.py:777
  68.7 24.0 %collective-permute-start.20 = (bf16[2,128,1024]{2,1,0:T(8,128)(2,1)S(1)}, bf16[2,128,1024]{2,1,0:T(8,128)(2,1)}, u32[]{:S(2)}, u32[]{:S(2)}) collective-permute-start(bf16[2,128,1024]{2,1,0:T(8,128)(2,1)S(1)} %pad_maximum_fusion.2), channel_id=1, source_target_pairs={{0,8},{4,12},{8,0},{12,4},{16,24},{20,28},{24,16},{28,20},{1,9},{5... | collective-permute-start | bytes 1572872 | tf_op jit(solution)/shard_map/ppermute | solution.py:777
  74.9 17.8 %collective-permute-start.22 = (bf16[2,128,1024]{2,1,0:T(8,128)(2,1)S(1)}, bf16[2,128,1024]{2,1,0:T(8,128)(2,1)S(1)}, u32[]{:S(2)}, u32[]{:S(2)}) collective-permute-start(bf16[2,128,1024]{2,1,0:T(8,128)(2,1)S(1)} %collective-permute-done.12.refs_4_), channel_id=1, source_target_pairs={{0,4},{4,0},{8,12},{12,8},{16,20},{20,16},{24,28},{28,24},{1,5},{5... | collective-permute-start | bytes 1572872 | tf_op jit(solution)/shard_map/ppermute | solution.py:777
  92.8 22.9 %collective-permute-start.18 = (bf16[128,1024]{1,0:T(8,128)(2,1)S(1)}, bf16[128,1024]{1,0:T(8,128)(2,1)S(1)}, u32[]{:S(2)}, u32[]{:S(2)}) collective-permute-start(bf16[128,1024]{1,0:T(8,128)(2,1)S(1)} %copy-done.17), channel_id=1, source_target_pairs={{0,4},{4,0},{8,12},{12,8},{16,20},{20,16},{24,28},{28,24},{1,5},{5... | collective-permute-start | bytes 786440 | tf_op jit(solution)/shard_map/ppermute | solution.py:777
  93.8 21.9 %collective-permute-start.19 = (bf16[128,1024]{1,0:T(8,128)(2,1)S(1)}, bf16[128,1024]{1,0:T(8,128)(2,1)S(1)}, u32[]{:S(2)}, u32[]{:S(2)}) collective-permute-start(bf16[128,1024]{1,0:T(8,128)(2,1)S(1)} %collective-permute-done.13.refs_2_), channel_id=1, source_target_pairs={{0,4},{4,0},{8,12},{12,8},{16,20},{20,16},{24,28},{28,24},{1,5},{5... | collective-permute-start | bytes 786440 | tf_op jit(solution)/shard_map/ppermute | solution.py:777
  94.9 24.1 %collective-permute-start.21 = (bf16[2,128,1024]{2,1,0:T(8,128)(2,1)}, bf16[2,128,1024]{2,1,0:T(8,128)(2,1)S(1)}, u32[]{:S(2)}, u32[]{:S(2)}) collective-permute-start(bf16[2,128,1024]{2,1,0:T(8,128)(2,1)} %collective-permute-done.20.refs_4_), channel_id=1, source_target_pairs={{0,4},{4,0},{8,12},{12,8},{16,20},{20,16},{24,28},{28,24},{1,5},{5... | collective-permute-start | bytes 1572872 | tf_op jit(solution)/shard_map/ppermute | solution.py:777
  95.8 49.9 %collective-permute-start.23 = (bf16[4,128,1024]{2,1,0:T(8,128)(2,1)}, bf16[4,128,1024]{2,1,0:T(8,128)(2,1)S(1)}, u32[]{:S(2)}, u32[]{:S(2)}) collective-permute-start(bf16[4,128,1024]{2,1,0:T(8,128)(2,1)} %get-tuple-element.159), channel_id=1, source_target_pairs={{0,4},{4,0},{8,12},{12,8},{16,20},{20,16},{24,28},{28,24},{1,5},{5... | collective-permute-start | bytes 3145736 | tf_op jit(solution)/shard_map/ppermute | solution.py:777
  114.7 47.7 %collective-permute-start.27 = (bf16[4,128,1024]{2,1,0:T(8,128)(2,1)}, bf16[4,128,1024]{2,1,0:T(8,128)(2,1)S(1)}, u32[]{:S(2)}, u32[]{:S(2)}) collective-permute-start(bf16[4,128,1024]{2,1,0:T(8,128)(2,1)} %get-tuple-element.168), channel_id=1, source_target_pairs={{0,4},{4,0},{8,12},{12,8},{16,20},{20,16},{24,28},{28,24},{1,5},{5... | collective-permute-start | bytes 3145736 | tf_op jit(solution)/shard_map/ppermute | solution.py:777
  146.8 18.3 %collective-permute-start.26 = (bf16[2,128,1024]{2,1,0:T(8,128)(2,1)}, bf16[2,128,1024]{2,1,0:T(8,128)(2,1)}, u32[]{:S(2)}, u32[]{:S(2)}) collective-permute-start(bf16[2,128,1024]{2,1,0:T(8,128)(2,1)} %add_convert_fusion.3), channel_id=1, source_target_pairs={{0,8},{4,12},{8,0},{12,4},{16,24},{20,28},{24,16},{28,20},{1,9},{5... | collective-permute-start | bytes 1572872 | tf_op jit(solution)/shard_map/ppermute | solution.py:777
  163.5 32.9 %collective-permute-start.28 = (bf16[2,128,1024]{2,1,0:T(8,128)(2,1)}, bf16[2,128,1024]{2,1,0:T(8,128)(2,1)S(1)}, u32[]{:S(2)}, u32[]{:S(2)}) collective-permute-start(bf16[2,128,1024]{2,1,0:T(8,128)(2,1)} %add_convert_fusion.2), channel_id=1, source_target_pairs={{0,8},{4,12},{8,0},{12,4},{16,24},{20,28},{24,16},{28,20},{1,9},{5... | collective-permute-start | bytes 1572872 | tf_op jit(solution)/shard_map/ppermute | solution.py:777
  165.1 25.7 %collective-permute-start.24 = (bf16[2,512,1024]{2,1,0:T(8,128)(2,1)}, bf16[2,512,1024]{2,1,0:T(8,128)(2,1)}, u32[]{:S(2)}, u32[]{:S(2)}) collective-permute-start(bf16[2,512,1024]{2,1,0:T(8,128)(2,1)} %get-tuple-element.163), channel_id=1, source_target_pairs={{0,1},{1,0},{2,3},{3,2},{4,5},{5,4},{6,7},{7,6},{8,9},{9,8},{10,11... | collective-permute-start | bytes 6291464 | tf_op jit(solution)/shard_map/ppermute | solution.py:777
  167.0 29.5 %collective-permute-start.29 = (bf16[128,1024]{1,0:T(8,128)(2,1)}, bf16[128,1024]{1,0:T(8,128)(2,1)S(1)}, u32[]{:S(2)}, u32[]{:S(2)}) collective-permute-start(bf16[128,1024]{1,0:T(8,128)(2,1)} %fusion), channel_id=1, source_target_pairs={{0,16},{4,20},{8,24},{12,28},{16,0},{20,4},{24,8},{28,12},{1,17},{... | collective-permute-start | bytes 786440 | tf_op jit(solution)/shard_map/ppermute | solution.py:777
  195.4 48.1 %collective-permute-start.25 = (bf16[2,512,1024]{2,1,0:T(8,128)(2,1)}, bf16[2,512,1024]{2,1,0:T(8,128)(2,1)}, u32[]{:S(2)}, u32[]{:S(2)}) collective-permute-start(bf16[2,512,1024]{2,1,0:T(8,128)(2,1)} %add_convert_fusion), channel_id=1, source_target_pairs={{0,2},{1,3},{2,0},{3,1},{4,6},{5,7},{6,4},{7,5},{8,10},{9,11},{10,... | collective-permute-start | bytes 6291464 | tf_op jit(solution)/shard_map/ppermute | solution.py:777
  197.3 23.7 %collective-permute-start.30 = (bf16[128,1024]{1,0:T(8,128)(2,1)}, bf16[128,1024]{1,0:T(8,128)(2,1)}, u32[]{:S(2)}, u32[]{:S(2)}) collective-permute-start(bf16[128,1024]{1,0:T(8,128)(2,1)} %fusion.1), channel_id=1, source_target_pairs={{0,16},{4,20},{8,24},{12,28},{16,0},{20,4},{24,8},{28,12},{1,17},{... | collective-permute-start | bytes 786440 | tf_op jit(solution)/shard_map/ppermute | solution.py:777
  217.1 15.1 %collective-permute-start.31 = (bf16[2,128,1024]{2,1,0:T(8,128)(2,1)}, bf16[2,128,1024]{2,1,0:T(8,128)(2,1)S(1)}, u32[]{:S(2)}, u32[]{:S(2)}) collective-permute-start(bf16[2,128,1024]{2,1,0:T(8,128)(2,1)} %get-tuple-element.183), channel_id=1, source_target_pairs={{0,4},{4,0},{8,12},{12,8},{16,20},{20,16},{24,28},{28,24},{1,5},{5... | collective-permute-start | bytes 1572872 | tf_op jit(solution)/shard_map/ppermute | solution.py:777
  218.6 21.9 %collective-permute-start.36 = (bf16[2,128,1024]{2,1,0:T(8,128)(2,1)}, bf16[2,128,1024]{2,1,0:T(8,128)(2,1)S(1)}, u32[]{:S(2)}, u32[]{:S(2)}) collective-permute-start(bf16[2,128,1024]{2,1,0:T(8,128)(2,1)} %get-tuple-element.189), channel_id=1, source_target_pairs={{0,4},{4,0},{8,12},{12,8},{16,20},{20,16},{24,28},{28,24},{1,5},{5... | collective-permute-start | bytes 1572872 | tf_op jit(solution)/shard_map/ppermute | solution.py:777
  246.3 15.3 %collective-permute-start.38 = (bf16[128,1024]{1,0:T(8,128)(2,1)S(1)}, bf16[128,1024]{1,0:T(8,128)(2,1)S(1)}, u32[]{:S(2)}, u32[]{:S(2)}) collective-permute-start(bf16[128,1024]{1,0:T(8,128)(2,1)S(1)} %fusion.2), channel_id=1, source_target_pairs={{0,16},{4,20},{8,24},{12,28},{16,0},{20,4},{24,8},{28,12},{1,17},{... | collective-permute-start | bytes 786440 | tf_op jit(solution)/shard_map/ppermute | solution.py:777
  (53 other events, 602.9 us)
